TPU v7x, 256 devices: a whole 4x4x8 slice. The times are simulated.
256 devices in a mesh: space: 128 (over z, y, x), rep: 2 (over core).
Axes of the slice: x: 4, y: 4, z: 8, core: 2. Of those that a mesh axis runs over, the one named last changes fastest.
Arguments:
- features: bfloat16 [2, 512, 64, 512], P('rep', 'space'), may hold values from -6 to 6
- neighbours: int32 [2, 512, 26], P('rep', 'space'), may hold values from -1 to 35, as said below
- send_list: int32 [2, 128, 2, 16], P('rep', 'space'), may hold values from -1 to 3, as said below
- w_fine: bfloat16 [64, 1728], replicated, may hold values from -0.15625 to 0.15625
- w_down: bfloat16 [64, 512], replicated, may hold values from -0.25 to 0.25
- w_coarse: bfloat16 [64, 1728], replicated, may hold values from -0.15625 to 0.15625
- w_up: bfloat16 [64, 512], replicated, may hold values from -0.75 to 0.75
- cotangent: bfloat16 [2, 512, 64, 512], P('rep', 'space'), may hold values from -6 to 6
Outputs:
- decoded: bfloat16 [2, 512, 64, 512], P('rep', 'space')
- grad_fine: float32 [64, 1728], replicated
- grad_down: float32 [64, 512], replicated
- grad_coarse: float32 [64, 1728], replicated
- grad_up: float32 [64, 512], replicated
Inputs may be any that keep to these rules, and one draw needn't show every extreme that they name: `neighbours`: A scene is a corridor 4 block positions across in the second and third dimensions; device d holds the occupied positions whose first coordinate lies in 4 d .. 4 d + 3, in Morton order. Entries follow true adjacency: below 4 a block of the same device, 4 + s (s < 4**2) the block of device d - 1 in slot s of its side 0, 4 + 4**2 + s the block of device d + 1 in slot s of its side 1, -1 an empty or outside position. In every slab the positions (0, 3, 3) and (3, 3, 3) are occupied and (3, 0, 0) is empty. send_list[d, 0, y * 4 + z] is device d's block at the last first-coordinate plane of its slab and position (y, z), send_list[d, 1, y * 4 + z] the one at the first plane; -1 where that position is empty.
All inputs are finite; a program needn't handle non-finite values.
Results may differ from a plain program's by a relative error of at most 0.007.
Values may be sent and summed in bfloat16 or wider, within the bound.
No kernel may reach another device: no remote copies, remote signals or barrier semaphores. Data moves between devices by JAX's collectives and lax.ppermute only.
A program may use at most 128 MiB of HBM per device.

v0:
```python
import math

import jax
import jax.numpy as jnp
from jax import lax
from jax.sharding import PartitionSpec as P

EDGE = 8


DIRECTIONS = [
    (a, c, e) for a in (-1, 0, 1) for c in (-1, 0, 1) for e in (-1, 0, 1) if (a, c, e) != (0, 0, 0)
]


def passed_along(block, axis, distance):
    devices = range(lax.axis_size(axis))
    route = [(i - distance, i) for i in devices if i - distance in devices]
    return lax.ppermute(block, axis, route)


def silu_slope(values):
    sig = jax.nn.sigmoid(values)
    return sig * (1.0 + values * (1.0 - sig))


def source_range(step, side):
    if step < 0:
        return slice(side - 1, side)
    if step == 0:
        return slice(0, side)
    return slice(0, 1)


def target_range(step, side):
    if step < 0:
        return slice(0, 1)
    if step == 0:
        return slice(1, side + 1)
    return slice(side + 1, side + 2)


def assemble(own_blocks, combined, sources, side):
    count, channels = (own_blocks.shape[0], own_blocks.shape[1])
    cubes = combined.reshape(combined.shape[0], channels, side, side, side)
    padded = jnp.zeros((count, channels, side + 2, side + 2, side + 2), own_blocks.dtype)
    padded = padded.at[:, :, 1 : side + 1, 1 : side + 1, 1 : side + 1].set(
        own_blocks.reshape(count, channels, side, side, side)
    )
    for k, (a, c, e) in enumerate(DIRECTIONS):
        part_cells = cubes[
            :, :, source_range(a, side), source_range(c, side), source_range(e, side)
        ]
        source_ids = sources[:, k]
        gathered = jnp.take(part_cells, jnp.maximum(source_ids, 0), axis=0)
        gathered = jnp.where(
            (source_ids >= 0)[:, None, None, None, None], gathered, jnp.zeros_like(gathered)
        )
        padded = padded.at[
            :, :, target_range(a, side), target_range(c, side), target_range(e, side)
        ].set(gathered)
    return padded


def lattice_columns(padded, side):
    count, channels = (padded.shape[0], padded.shape[1])
    parts_list = [
        padded[:, :, a : a + side, c : c + side, e : e + side].reshape(count, channels, side**3)
        for a in range(3)
        for c in range(3)
        for e in range(3)
    ]
    return jnp.concatenate(parts_list, axis=1)


def spread_back(back_cols, side):
    count = back_cols.shape[0]
    channels = back_cols.shape[1] // 27
    result = jnp.zeros((count, channels, side + 2, side + 2, side + 2), jnp.float32)
    for a in range(3):
        for c in range(3):
            for e in range(3):
                offset = 9 * a + 3 * c + e
                piece = back_cols[:, offset * channels : (offset + 1) * channels].reshape(
                    count, channels, side, side, side
                )
                result = result.at[:, :, a : a + side, c : c + side, e : e + side].add(piece)
    return result


def to_patches(field, side):
    count, channels = (field.shape[0], field.shape[1])
    half = side // 2
    shaped = field.reshape(count, channels, half, 2, half, 2, half, 2).transpose(
        0, 3, 5, 7, 1, 2, 4, 6
    )
    return shaped.reshape(count, 8 * channels, half**3)


def from_patches(values, half):
    count = values.shape[0]
    channels = values.shape[1] // 8
    shaped = values.reshape(count, 2, 2, 2, channels, half, half, half).transpose(
        0, 4, 5, 1, 6, 2, 7, 3
    )
    return shaped.reshape(count, channels, 8 * half**3)


def shards(features, neighbours, send_list, w_fine, w_down, w_coarse, w_up, cotangent):
    f32 = jnp.float32
    fine_in = features[0]
    sources = neighbours[0]
    sends = send_list[0, 0]
    block_count, channels = (fine_in.shape[0], fine_in.shape[1])
    slot_count = sends.shape[1]
    peer_count = lax.axis_size("space")
    coarse_side = EDGE // 2
    upper_ids = jnp.maximum(sends[0], 0)
    lower_ids = jnp.maximum(sends[1], 0)
    to_upper = jnp.take(fine_in, upper_ids, axis=0)
    to_lower = jnp.take(fine_in, lower_ids, axis=0)
    arrived = []
    for offset, payload in ((1, to_upper), (-1, to_lower)):
        arrived.append(passed_along(payload, "space", offset))
    halo0 = assemble(fine_in, jnp.concatenate([fine_in] + arrived, axis=0), sources, EDGE)
    pad_groups = halo0.reshape((block_count // 4, 4) + halo0.shape[1:])

    def fine_forward(pad_group):
        return jnp.einsum(
            "ok,gkv->gov", w_fine, lattice_columns(pad_group, EDGE), preferred_element_type=f32
        )

    fine_pre = lax.map(fine_forward, pad_groups).reshape(block_count, channels, EDGE**3)
    hidden0 = jax.nn.silu(fine_pre).astype(jnp.bfloat16)
    patches0 = to_patches(hidden0, EDGE)
    coarse_pre = jnp.einsum("ok,bkv->bov", w_down, patches0, preferred_element_type=f32)
    hidden1 = jax.nn.silu(coarse_pre).astype(jnp.bfloat16)
    coarse_upper = jnp.take(hidden1, upper_ids, axis=0)
    coarse_lower = jnp.take(hidden1, lower_ids, axis=0)
    arrived1 = []
    for offset, payload in ((1, coarse_upper), (-1, coarse_lower)):
        arrived1.append(passed_along(payload, "space", offset))
    halo1 = assemble(hidden1, jnp.concatenate([hidden1] + arrived1, axis=0), sources, coarse_side)
    columns1 = lattice_columns(halo1, coarse_side)
    coarse_conv = jnp.einsum("ok,bkv->bov", w_coarse, columns1, preferred_element_type=f32)
    gated = jax.nn.silu(coarse_conv).astype(jnp.bfloat16)
    up_terms = from_patches(
        jnp.einsum("ik,biv->bkv", w_up, gated, preferred_element_type=f32), coarse_side
    )
    decoded = (hidden0.astype(f32) + up_terms).astype(jnp.bfloat16)
    cot_patch = to_patches(cotangent[0], EDGE)
    grad_up = jnp.einsum("biv,bkv->ik", gated, cot_patch, preferred_element_type=f32)
    up_back = jnp.einsum("ik,bkv->biv", w_up, cot_patch, preferred_element_type=f32)
    delta_up = (up_back * silu_slope(coarse_conv)).astype(jnp.bfloat16)
    grad_coarse = jnp.einsum("bov,bkv->ok", delta_up, columns1, preferred_element_type=f32)
    back_cols = jnp.einsum("ok,bov->bkv", w_coarse, delta_up, preferred_element_type=f32)
    back_pad = spread_back(back_cols, coarse_side)
    slot_total = block_count + 2 * slot_count
    slot_ids = jnp.arange(slot_total, dtype=jnp.int32)
    accumulated = jnp.zeros((slot_total, channels, coarse_side, coarse_side, coarse_side), f32)
    for k, (a, c, e) in enumerate(DIRECTIONS):
        piece = back_pad[
            :,
            :,
            target_range(a, coarse_side),
            target_range(c, coarse_side),
            target_range(e, coarse_side),
        ]
        selector = (sources[:, k][:, None] == slot_ids[None, :]).astype(f32)
        moved = jnp.einsum("bm,bcxyz->mcxyz", selector, piece, precision=lax.Precision.HIGHEST)
        accumulated = accumulated.at[
            :,
            :,
            source_range(a, coarse_side),
            source_range(c, coarse_side),
            source_range(e, coarse_side),
        ].add(moved)
    lower_owned = accumulated[block_count : block_count + slot_count][
        :, :, coarse_side - 1
    ].reshape(slot_count, channels * coarse_side**2)
    upper_owned = accumulated[block_count + slot_count :][:, :, 0].reshape(
        slot_count, channels * coarse_side**2
    )
    returned = []
    for offset, payload in ((-1, lower_owned), (1, upper_owned)):
        returned.append(
            passed_along(payload.astype(jnp.bfloat16), "space", offset).astype(payload.dtype)
        )
    block_ids = jnp.arange(block_count, dtype=jnp.int32)
    chooser_upper = (sends[0][:, None] == block_ids[None, :]).astype(f32)
    chooser_lower = (sends[1][:, None] == block_ids[None, :]).astype(f32)
    face_high = jnp.einsum("sb,sf->bf", chooser_upper, returned[0], precision=lax.Precision.HIGHEST)
    face_low = jnp.einsum("sb,sf->bf", chooser_lower, returned[1], precision=lax.Precision.HIGHEST)
    centre = back_pad[:, :, 1 : coarse_side + 1, 1 : coarse_side + 1, 1 : coarse_side + 1]
    grad_cube = centre + accumulated[:block_count]
    grad_cube = grad_cube.at[:, :, coarse_side - 1].add(
        face_high.reshape(block_count, channels, coarse_side, coarse_side)
    )
    grad_cube = grad_cube.at[:, :, 0].add(
        face_low.reshape(block_count, channels, coarse_side, coarse_side)
    )
    grad_hidden1 = grad_cube.reshape(block_count, channels, coarse_side**3)
    delta_down = (grad_hidden1 * silu_slope(coarse_pre)).astype(jnp.bfloat16)
    grad_down = jnp.einsum("bov,bkv->ok", delta_down, patches0, preferred_element_type=f32)
    down_back = jnp.einsum("ok,bov->bkv", w_down, delta_down, preferred_element_type=f32)
    grad_hidden0 = cotangent[0].astype(f32) + from_patches(down_back, coarse_side)
    delta_fine = (grad_hidden0 * silu_slope(fine_pre)).astype(jnp.bfloat16)
    delta_groups = delta_fine.reshape((block_count // 4, 4) + delta_fine.shape[1:])

    def fine_weights(total, pair):
        pad_group, delta_group = pair
        cols = lattice_columns(pad_group, EDGE)
        return (
            total + jnp.einsum("gov,gkv->ok", delta_group, cols, preferred_element_type=f32),
            None,
        )

    grad_fine, _ = lax.scan(fine_weights, jnp.zeros(w_fine.shape, f32), (pad_groups, delta_groups))
    grad_fine, grad_down, grad_coarse, grad_up = lax.psum(
        (grad_fine, grad_down, grad_coarse, grad_up), ("space", "rep")
    )
    factor = 1.0 / math.sqrt(lax.axis_size("rep") * peer_count * block_count * EDGE**3)
    return (
        decoded[None],
        grad_fine * factor,
        grad_down * factor,
        grad_coarse * factor,
        grad_up * factor,
    )


def solution(mesh):
    in_specs = (
        P("rep", "space", None, None),
        P("rep", "space", None),
        P("rep", "space", None, None),
        P(),
        P(),
        P(),
        P(),
        P("rep", "space", None, None),
    )
    out_specs = (P("rep", "space", None, None), P(), P(), P(), P())
    return jax.shard_map(shards, mesh=mesh, in_specs=in_specs, out_specs=out_specs, check_vma=False)
```

profile of v0, /device:TPU:2, one launch (start us, length us, event | category | flops | bytes accessed | tf_op | source)
XLA Modules:
  0.0 604.1 jit_solution(300199098272582646)
XLA Ops:
  10.6 3.4 collective-permute-start
  15.8 3.4 collective-permute-start.1
  48.4 3.0 copy.303
  51.4 3.8 copy.304
  58.0 2.5 pad_maximum_fusion
  105.1 3.2 fusion.228
  108.3 5.6 fusion.227
  113.9 2.1 copy.375
  116.0 2.0 copy.374
  118.0 2.0 copy.373
  120.0 2.0 copy.372
  123.0 2.1 copy.370
  133.4 2.1 copy.391
  135.5 2.0 copy.390
  141.5 2.0 copy.387
  144.6 2.1 copy.385
  148.6 2.0 copy.383
  150.6 2.0 copy.382
  152.7 2.0 copy.381
  180.5 4.4 multiply_convert_fusion
  189.4 2.4 collective-permute-start.2
  191.9 4.1 collective-permute-start.3
  199.2 2.1 collective-permute-done.3
  261.2 3.1 concatenate.384
  280.3 2.3 fusion.22
  283.7 2.3 fusion.27
  286.3 2.2 fusion.30
  290.6 5.0 collective-permute-start.5
  296.7 2.2 collective-permute-start.4
  300.9 6.0 collective-permute-done.4
  311.8 6.0 convolution_bitcast_fusion.2
  320.4 269.7 %all-reduce.7.cloned.1.call-done = (f32[64,1728]{1,0:T(8,128)}, f32[64,512]{1,0:T(8,128)}, f32[64,1728]{1,0:T(8,128)}, f32[64,512]{1,0:T(8,128)}) async-done(((f32[64,1728]{1,0:T(8,128)}, f32[64,512]{1,0:T(8,128)}, f32[64,1728]{1,0:T(8,128)}, f32[64,512]{1,0:T(8,128)}), (f32[64,1728]{1,0:T(8,128)}, f32[64,512]{1,0:T(8,128)}, f32[64,1728]{1,0:T(8,128)}, f32[64,512]{1,0:T(8,128)})) %all-reduce.7.cloned.1.call-update) | async-done | bytes 1146896 | tf_op jit(solution)/shard_map/psum | solution.py:219
  (747 shorter events, 225.8 us)
Async XLA Ops:
  7.2 257.1 %copy-start = (bf16[64,1728]{1,0:T(8,128)(2,1)S(1)}, bf16[64,1728]{1,0:T(8,128)(2,1)}, u32[]{:S(2)}) copy-start(bf16[64,1728]{1,0:T(8,128)(2,1)} %param.261) | copy-start | bytes 663556
  7.2 582.9 %all-reduce.7.cloned.1.call-start = ((), (), s32[]{:S(2)}) async-start(), calls=%async_computation | async-start | bytes 2359296 | tf_op jit(solution)/shard_map/psum | solution.py:219
  10.6 37.8 %collective-permute-start = (bf16[16,64,512]{2,1,0:T(8,128)(2,1)S(1)}, bf16[16,64,512]{2,1,0:T(8,128)(2,1)}, u32[]{:S(2)}, u32[]{:S(2)}) collective-permute-start(bf16[16,64,512]{2,1,0:T(8,128)(2,1)S(1)} %broadcast_select_fusion.1), channel_id=1, source_target_pairs={{0,2},{2,4},{4,6},{6,8},{8,10},{10,12},{12,14},{14,16},{16,18},{18... | collective-permute-start | bytes 3145736 | tf_op jit(solution)/shard_map/ppermute | solution.py:19
  15.8 35.5 %collective-permute-start.1 = (bf16[16,64,512]{2,1,0:T(8,128)(2,1)}, bf16[16,64,512]{2,1,0:T(8,128)(2,1)}, u32[]{:S(2)}, u32[]{:S(2)}) collective-permute-start(bf16[16,64,512]{2,1,0:T(8,128)(2,1)} %broadcast_select_fusion), channel_id=1, source_target_pairs={{2,0},{4,2},{6,4},{8,6},{10,8},{12,10},{14,12},{16,14},{18,16},{20... | collective-permute-start | bytes 3145736 | tf_op jit(solution)/shard_map/ppermute | solution.py:19
  19.3 22.6 %copy-start.150 = (s32[2]{0:T(128)}, s32[2]{0:T(128)S(1)}, u32[]{:S(2)}) copy-start(s32[2]{0:T(128)S(1)} %iota_multiply_fusion) | copy-start | bytes 28
  20.2 21.6 %copy-start.73 = (s32[4]{0:T(128)}, s32[4]{0:T(128)S(1)}, u32[]{:S(2)}) copy-start(s32[4]{0:T(128)S(1)} %get-tuple-element.1376) | copy-start | bytes 52
  23.2 18.7 %copy-start.43 = (s32[4]{0:T(128)}, s32[4]{0:T(128)S(1)}, u32[]{:S(2)}) copy-start(s32[4]{0:T(128)S(1)} %get-tuple-element.1356) | copy-start | bytes 52
  23.2 18.7 %copy-start.45 = (s32[4]{0:T(128)}, s32[4]{0:T(128)S(1)}, u32[]{:S(2)}) copy-start(s32[4]{0:T(128)S(1)} %get-tuple-element.1357) | copy-start | bytes 52
  23.2 18.7 %copy-start.47 = (s32[4]{0:T(128)}, s32[4]{0:T(128)S(1)}, u32[]{:S(2)}) copy-start(s32[4]{0:T(128)S(1)} %get-tuple-element.1359) | copy-start | bytes 52
  23.2 18.7 %copy-start.49 = (s32[4]{0:T(128)}, s32[4]{0:T(128)S(1)}, u32[]{:S(2)}) copy-start(s32[4]{0:T(128)S(1)} %get-tuple-element.1361) | copy-start | bytes 52
  23.2 18.7 %copy-start.107 = (s32[4]{0:T(128)}, s32[4]{0:T(128)S(1)}, u32[]{:S(2)}) copy-start(s32[4]{0:T(128)S(1)} %get-tuple-element.1352) | copy-start | bytes 52
  23.2 18.7 %copy-start.109 = (s32[4]{0:T(128)}, s32[4]{0:T(128)S(1)}, u32[]{:S(2)}) copy-start(s32[4]{0:T(128)S(1)} %get-tuple-element.1354) | copy-start | bytes 52
  23.3 18.7 %copy-start.111 = (s32[4]{0:T(128)}, s32[4]{0:T(128)S(1)}, u32[]{:S(2)}) copy-start(s32[4]{0:T(128)S(1)} %get-tuple-element.1358) | copy-start | bytes 52
  23.3 18.7 %copy-start.113 = (s32[4]{0:T(128)}, s32[4]{0:T(128)S(1)}, u32[]{:S(2)}) copy-start(s32[4]{0:T(128)S(1)} %get-tuple-element.1360) | copy-start | bytes 52
  23.3 25.0 %copy-start.51 = (s32[4]{0:T(128)}, s32[4]{0:T(128)S(1)}, u32[]{:S(2)}) copy-start(s32[4]{0:T(128)S(1)} %get-tuple-element.1362) | copy-start | bytes 52
  23.3 25.0 %copy-start.53 = (s32[4]{0:T(128)}, s32[4]{0:T(128)S(1)}, u32[]{:S(2)}) copy-start(s32[4]{0:T(128)S(1)} %get-tuple-element.1363) | copy-start | bytes 52
  23.3 25.0 %copy-start.55 = (s32[4]{0:T(128)}, s32[4]{0:T(128)S(1)}, u32[]{:S(2)}) copy-start(s32[4]{0:T(128)S(1)} %get-tuple-element.1364) | copy-start | bytes 52
  23.3 25.0 %copy-start.57 = (s32[4]{0:T(128)}, s32[4]{0:T(128)S(1)}, u32[]{:S(2)}) copy-start(s32[4]{0:T(128)S(1)} %get-tuple-element.1365) | copy-start | bytes 52
  23.3 25.0 %copy-start.59 = (s32[4]{0:T(128)}, s32[4]{0:T(128)S(1)}, u32[]{:S(2)}) copy-start(s32[4]{0:T(128)S(1)} %get-tuple-element.1366) | copy-start | bytes 52
  23.3 25.0 %copy-start.61 = (s32[4]{0:T(128)}, s32[4]{0:T(128)S(1)}, u32[]{:S(2)}) copy-start(s32[4]{0:T(128)S(1)} %get-tuple-element.1367) | copy-start | bytes 52
  23.3 25.0 %copy-start.63 = (s32[4]{0:T(128)}, s32[4]{0:T(128)S(1)}, u32[]{:S(2)}) copy-start(s32[4]{0:T(128)S(1)} %get-tuple-element.1368) | copy-start | bytes 52
  23.3 25.0 %copy-start.115 = (s32[4]{0:T(128)}, s32[4]{0:T(128)S(1)}, u32[]{:S(2)}) copy-start(s32[4]{0:T(128)S(1)} %get-tuple-element.1369) | copy-start | bytes 52
  189.4 9.8 %collective-permute-start.2 = (bf16[16,64,64]{1,2,0:T(8,128)(2,1)S(1)}, bf16[16,64,64]{1,2,0:T(8,128)(2,1)}, u32[]{:S(2)}, u32[]{:S(2)}) collective-permute-start(bf16[16,64,64]{1,2,0:T(8,128)(2,1)S(1)} %broadcast_select_fusion.3), channel_id=1, source_target_pairs={{0,2},{2,4},{4,6},{6,8},{8,10},{10,12},{12,14},{14,16},{16,18},{18... | collective-permute-start | bytes 393224 | tf_op jit(solution)/shard_map/ppermute | solution.py:19
  191.9 9.4 %collective-permute-start.3 = (bf16[16,64,64]{1,2,0:T(8,128)(2,1)}, bf16[16,64,64]{1,2,0:T(8,128)(2,1)}, u32[]{:S(2)}, u32[]{:S(2)}) collective-permute-start(bf16[16,64,64]{1,2,0:T(8,128)(2,1)} %broadcast_select_fusion.2), channel_id=1, source_target_pairs={{2,0},{4,2},{6,4},{8,6},{10,8},{12,10},{14,12},{16,14},{18,16},{20... | collective-permute-start | bytes 393224 | tf_op jit(solution)/shard_map/ppermute | solution.py:19
  203.2 17.0 %copy-start.153 = (pred[4]{0:T(512)(128)(4,1)S(1)}, pred[4]{0:T(512)(128)(4,1)}, u32[]{:S(2)}) copy-start(pred[4]{0:T(512)(128)(4,1)} %get-tuple-element.1629) | copy-start | bytes 16
  204.7 36.3 %copy-start.122 = (pred[4]{0:T(512)(128)(4,1)S(1)}, pred[4]{0:T(512)(128)(4,1)}, u32[]{:S(2)}) copy-start(pred[4]{0:T(512)(128)(4,1)} %get-tuple-element.1572) | copy-start | bytes 16
  204.9 37.5 %copy-start.118 = (pred[4]{0:T(512)(128)(4,1)S(1)}, pred[4]{0:T(512)(128)(4,1)}, u32[]{:S(2)}) copy-start(pred[4]{0:T(512)(128)(4,1)} %get-tuple-element.1576) | copy-start | bytes 16
  205.0 37.5 %copy-start.120 = (pred[4]{0:T(512)(128)(4,1)S(1)}, pred[4]{0:T(512)(128)(4,1)}, u32[]{:S(2)}) copy-start(pred[4]{0:T(512)(128)(4,1)} %get-tuple-element.1577) | copy-start | bytes 16
  290.2 16.6 %copy-start.154 = (s32[16]{0:T(128)S(1)}, s32[16]{0:T(128)}, u32[]{:S(2)}) copy-start(s32[16]{0:T(128)} %get-tuple-element.1522) | copy-start | bytes 196
  290.6 9.0 %collective-permute-start.5 = (bf16[16,1024]{0,1:T(8,128)(2,1)S(1)}, bf16[16,1024]{0,1:T(8,128)(2,1)S(1)}, u32[]{:S(2)}, u32[]{:S(2)}) collective-permute-start(bf16[16,1024]{0,1:T(8,128)(2,1)S(1)} %bitcast.1005), channel_id=1, source_target_pairs={{0,2},{2,4},{4,6},{6,8},{8,10},{10,12},{12,14},{14,16},{16,18},{18... | collective-permute-start | bytes 98312 | tf_op jit(solution)/shard_map/ppermute | solution.py:19
  296.5 13.5 %copy-start.36 = (bf16[64,512]{1,0:T(8,128)(2,1)S(1)}, bf16[64,512]{1,0:T(8,128)(2,1)}, u32[]{:S(2)}) copy-start(bf16[64,512]{1,0:T(8,128)(2,1)} %param.260) | copy-start | bytes 196612
  296.7 10.1 %collective-permute-start.4 = (bf16[16,1024]{0,1:T(8,128)(2,1)S(1)}, bf16[16,1024]{0,1:T(8,128)(2,1)S(1)}, u32[]{:S(2)}, u32[]{:S(2)}) collective-permute-start(bf16[16,1024]{0,1:T(8,128)(2,1)S(1)} %bitcast.1004), channel_id=1, source_target_pairs={{2,0},{4,2},{6,4},{8,6},{10,8},{12,10},{14,12},{16,14},{18,16},{20... | collective-permute-start | bytes 98312 | tf_op jit(solution)/shard_map/ppermute | solution.py:19
  (135 other events, 850.1 us)
Sparse Core Ops, SparseCore 0:
  317.9 272.0 all-reduce.6
where the time goes:
time: 616 us; the launch traced here: 604 us
  waiting for transfers between devices  278 us (45%)
  local copies, waits for them, and re-layouts  182 us (30%)
  other arithmetic  74.3 us (12%)
  matrix products  31.2 us (5%)
  starting transfers between devices  20.5 us (3%)
  between operations  17.5 us (3%)
    psum x1, waiting for transfers between devices, shards(): lax.psum((grad_fine, grad_down, grad_coarse, grad_up), ('space', 'rep'))  270 us
    gather x52, local copies, waits for them, and re-layouts, assemble(): gathered = jnp.take(part_cells, jnp.maximum(source_ids, 0), axis=0)  51 us
    reshape x27, local copies, waits for them, and re-layouts, lattice_columns(): padded[:, :, a:a + side, c:c + side, e:e + side]  43.6 us
    unnamed x366, local copies, waits for them, and re-layouts  29.9 us
    ppermute x6, starting transfers between devices, passed_along(): return lax.ppermute(block, axis, route)  20.5 us
    select_n x26, other arithmetic, assemble(): jnp.where((source_ids >= 0)[:, None, None, None, None], gathered, jnp.zer...  16.6 us
    gather x27, other arithmetic  15.4 us
    dot_general x26, matrix products, shards(): jnp.einsum('bm,bcxyz->mcxyz', selector, piece, precision=lax.Precision.HI...  14.4 us
  transfers between devices with their start and end apart: 7, of which 4 were waited for; matrix products, arithmetic and copies ran while one was open for 7% of the time, Pallas kernels for 0%

commit v1 on v0

v1 whole, which is shorter than its diff:
```python
import math

import jax
import jax.numpy as jnp
import numpy as np
from jax import lax
from jax.experimental import pallas as pl
from jax.experimental.pallas import tpu as pltpu
from jax.sharding import PartitionSpec as P

F32 = jnp.float32
BF16 = jnp.bfloat16
I32 = jnp.int32
AXES = ("space", "rep")
FINE_SHIFTS = [10 * (c - 1) + (e - 1) for c in range(3) for e in range(3)]
COARSE_SHIFTS = [6 * (c - 1) + (e - 1) for c in range(3) for e in range(3)]


def lane_tables():
    table = np.full((16, 2048), -1, np.int32)
    t = np.arange(128)
    y, z, inside = t // 10 - 1, t % 10 - 1, t < 100
    c, e = np.where(y < 0, 0, np.where(y >= 8, 2, 1)), np.where(z < 0, 0, np.where(z >= 8, 2, 1))
    table[0, :128] = np.where(inside, 3 * c + e, -1)
    table[1, :128] = np.where(inside, (y - 8 * (c - 1)) * 8 + (z - 8 * (e - 1)), 0)
    own = inside & (c == 1) & (e == 1)
    for b in range(4):
        table[4, 128 * b : 128 * b + 128] = np.where(own, 64 * b + y * 8 + z, -1)
    u = np.arange(64)
    cy, cz, cin = u // 6 - 1, u % 6 - 1, u < 36
    cc, ce = np.where(cy < 0, 0, np.where(cy >= 4, 2, 1)), np.where(cz < 0, 0, np.where(cz >= 4, 2, 1))
    for b in range(2):
        at = slice(64 * b, 64 * b + 64)
        table[2, at] = np.where(cin, 3 * cc + ce, -1)
        table[3, at] = np.where(cin, 6 * (cy - 4 * (cc - 1) + 1) + cz - 4 * (ce - 1) + 1, 0)
    cown = cin & (cc == 1) & (ce == 1)
    w = np.arange(64)
    for j in range(2):
        for l in range(2):
            for b in range(2):
                at = (2 * j + l) * 128 + 64 * b
                rows = 128 * b + 10 * (2 * cy + j + 1) + 2 * cz + l + 1
                table[5, at : at + 64] = np.where(cown, rows, -1)
            for b in range(4):
                ny, nz = w // 8, w % 8
                hit = (ny % 2 == j) & (nz % 2 == l)
                at = (2 * j + l) * 256 + 64 * b
                table[7, at : at + 64] = np.where(hit, 64 * b + 6 * (ny // 2 + 1) + nz // 2 + 1, -1)
                hit = own & (y % 2 == j) & (z % 2 == l)
                at = (2 * j + l) * 512 + 128 * b
                table[8, at : at + 128] = np.where(hit, 64 * b + 6 * (y // 2 + 1) + z // 2 + 1, -1)
    for b in range(2):
        table[6, 64 * b : 64 * b + 64] = 128 * b + 10 * (w // 8 + 1) + w % 8 + 1
    return table


TABLE = lane_tables()


def mm(a, b):
    return jnp.dot(a, b, preferred_element_type=F32)


def nt(a, b):
    return lax.dot_general(a, b, (((1,), (1,)), ((), ())), preferred_element_type=F32)


def roll(v, shift):
    return pltpu.roll(v, shift % 128, 1)


def onehot(code, rows):
    hit = lax.broadcasted_iota(I32, (rows, code.shape[1]), 0) == code
    return jnp.where(hit, 1.0, 0.0).astype(BF16)


def low_half(shape):
    return lax.broadcasted_iota(I32, shape, 1) < 64


def merge(low, first, second):
    return jnp.where(low, first, roll(second, 64))


def merge_high(low, first, second):
    return jnp.where(low, roll(first, 64), second)


def sigmoid(v):
    return 1.0 / (1.0 + jnp.exp(-v))


def silu(v):
    return v / (1.0 + jnp.exp(-v))


def slope(v):
    s = sigmoid(v)
    return s * (1.0 + v * (1.0 - s))


def raw_slots(neighbours, a, block, direction):
    found = jnp.full(direction.shape, -1, I32)
    for j in range(9):
        k = 9 * a + j
        entry = block if k == 13 else neighbours[block, k - (k > 13)]
        found = jnp.where(direction == j, entry, found)
    return found


def local_code(slots, cells):
    return jnp.where(slots >= 0, slots * 64 + cells, -1)


def edge_code(slots, cells, base, remote_slots):
    code = jnp.where((slots >= 0) & (slots < 4), slots * 64 + cells, -1)
    reach = (slots >= base) & (slots < base + 16)
    for j in range(4):
        hit = reach & (slots - base == remote_slots[j : j + 1])
        code = jnp.where(hit, 256 + j * 64 + cells, code)
    return code


def fine_slots(neighbours, table, a):
    direction = table[0:1, :128]
    return [raw_slots(neighbours, a, b, direction) for b in range(4)]


def coarse_slots(neighbours, table, a):
    direction = table[2:3, :128]
    low = low_half((1, 128))
    per_block = [raw_slots(neighbours, a, b, direction) for b in range(4)]
    return [jnp.where(low, per_block[0], per_block[1]), jnp.where(low, per_block[2], per_block[3])]


def arrived_slots(payload):
    return payload[128:144, :].astype(F32).astype(I32)


def tap_rows(w_ref):
    return jnp.concatenate([w_ref[:, 576 * a : 576 * a + 576] for a in range(3)], axis=0)


def put_taps(dst, at, plane, shifts):
    for s in range(plane.shape[1] // 128):
        piece = plane[:, 128 * s : 128 * s + 128]
        for j, shift in enumerate(shifts):
            moved = piece if shift == 0 else roll(piece, -shift)
            dst[64 * j : 64 * j + 64, at + 128 * s : at + 128 * s + 128] = moved


def natural_planes(ref):
    low = low_half((64, 128))
    planes = []
    for t in range(4):
        tiles = [ref[b, :, 128 * t : 128 * t + 128] for b in range(4)]
        planes.append(jnp.concatenate([merge(low, tiles[2 * p], tiles[2 * p + 1]) for p in range(2)], axis=1))
        planes.append(jnp.concatenate([merge_high(low, tiles[2 * p], tiles[2 * p + 1]) for p in range(2)], axis=1))
    return planes


def transposed_blocks(w, order):
    wt = w.astype(F32).T
    return jnp.concatenate([wt[64 * k : 64 * k + 64, :] for k in order], axis=1).astype(BF16)


def pack_faces(sends, low_tile, high_tile, to_upper, to_lower):
    low = low_half((64, 128))
    for p in range(2):
        to_upper[64 * p : 64 * p + 64, :] = merge_high(low, high_tile[2 * p], high_tile[2 * p + 1])
        to_lower[64 * p : 64 * p + 64, :] = merge(low, low_tile[2 * p], low_tile[2 * p + 1])
    rows = lax.broadcasted_iota(I32, (16, 128), 0)
    for side, out in ((0, to_upper), (1, to_lower)):
        slots = jnp.full((16, 128), -1, I32)
        for j in range(4):
            slot = jnp.int32(-1)
            for s in range(16):
                slot = jnp.where(sends[side, s] == j, s, slot)
            slots = jnp.where(rows == j, slot, slots)
        out[128:144, :] = slots.astype(F32).astype(BF16)


def fine_inner(neighbours, table, feat, cot, w_fine, w_up, w_down, w_coarse,
               pre, ext, edges, cot_plane, cot_patch, up_back, w_adj, w_ups, w_dns, taps):
    planes = natural_planes(feat)
    edges[0], edges[1] = planes[0], planes[7]
    cells = table[1:2, :128]
    code = jnp.concatenate([local_code(v, cells) for v in fine_slots(neighbours, table, 1)], axis=1)
    whole = mm(jnp.concatenate(planes, axis=0), onehot(code, 256)).astype(BF16)
    weight = tap_rows(w_fine)
    for x in range(8):
        plane = whole[64 * x : 64 * x + 64]
        ext[x] = plane
        put_taps(taps, 512 * x, plane, FINE_SHIFTS)
    for x in range(8):
        part = mm(weight, taps[:, 512 * x : 512 * x + 512])
        for a in range(3):
            out = x + 1 - a
            if 0 <= out < 8:
                piece = part[64 * a : 64 * a + 64]
                if x == max(out - 1, 0):
                    pre[out] = piece
                else:
                    pre[out] += piece
    placed = mm(jnp.concatenate(natural_planes(cot), axis=0), onehot(table[4:5, :512], 256)).astype(BF16)
    for x in range(8):
        cot_plane[x] = placed[64 * x : 64 * x + 64]
    down = onehot(table[5:6, :512], 256)
    for p in range(2):
        put_patches(cot_patch, mm(placed[:, 256 * p : 256 * p + 256], down).astype(BF16), p)
    up_back[...] = mm(w_up[...], cot_patch[...])
    for a in range(3):
        order = [(2 - a) * 9 + 8 - j for j in range(9)]
        w_adj[64 * a : 64 * a + 64, :] = transposed_blocks(w_coarse[...], order)
    for i in range(2):
        w_ups[64 * i : 64 * i + 64, :] = transposed_blocks(w_up[...], range(4 * i, 4 * i + 4))
        w_dns[64 * i : 64 * i + 64, :] = transposed_blocks(w_down[...], range(4 * i, 4 * i + 4))


def put_patches(dst, selected, pair):
    for x in range(8):
        for jl in range(4):
            at = ((x % 2) * 4 + jl) * 64
            lane = (x // 2) * 256 + pair * 128
            dst[at : at + 64, lane : lane + 128] = selected[64 * x : 64 * x + 64, 128 * jl : 128 * jl + 128]


def fine_outer(neighbours, table, from_lower, from_upper, edges, pre, w_fine, w_down,
               hidden, patch, coarse_pre, hidden1, pre_edge, ext_edge, taps):
    cells = table[1:2, :128]
    weight = tap_rows(w_fine)
    for side, a, base, payload in ((0, 0, 4, from_lower), (1, 2, 20, from_upper)):
        slots = arrived_slots(payload)
        code = jnp.concatenate([edge_code(v, cells, base, slots) for v in fine_slots(neighbours, table, a)], axis=1)
        pool = jnp.concatenate([edges[1 - side], payload[0:64, :], payload[64:128, :]], axis=1)
        plane = mm(pool, onehot(code, 512)).astype(BF16)
        ext_edge[side] = plane
        put_taps(taps, 512 * side, plane, FINE_SHIFTS)
        part = mm(weight[64 * a : 64 * a + 64], taps[:, 512 * side : 512 * side + 512])
        pre_edge[side] = pre[7 * side] + part
    for x in range(8):
        value = pre_edge[0] if x == 0 else pre_edge[1] if x == 7 else pre[x]
        hidden[x] = silu(value).astype(BF16)
    down = onehot(table[5:6, :512], 256)
    for p in range(2):
        rows = jnp.concatenate([hidden[x, :, 256 * p : 256 * p + 256] for x in range(8)], axis=0)
        put_patches(patch, mm(rows, down).astype(BF16), p)
    value = mm(w_down[...], patch[...])
    coarse_pre[...] = value
    hidden1[...] = silu(value).astype(BF16)


def by_rows(v):
    return jnp.concatenate([v[:, 256 * x : 256 * x + 256] for x in range(4)], axis=0)


def coarse_inner_conv(field, select, weight, taps, ext):
    whole = mm(by_rows(field), select).astype(BF16)
    for x in range(4):
        plane = whole[64 * x : 64 * x + 64]
        if ext is not None:
            ext[:, 256 * x : 256 * x + 256] = plane
        put_taps(taps, 256 * x, plane, COARSE_SHIFTS)
    part = mm(weight, taps[:, :1024])
    sums = []
    for x in range(4):
        total = part[64:128, 256 * x : 256 * x + 256]
        if x > 0:
            total = total + part[0:64, 256 * x - 256 : 256 * x]
        if x < 3:
            total = total + part[128:192, 256 * x + 256 : 256 * x + 512]
        sums.append(total)
    return jnp.concatenate(sums, axis=1)


def coarse_outer_conv(codes, side, own_plane, arrived, weight, taps, at):
    pool = jnp.concatenate([own_plane, arrived], axis=1)
    plane = mm(pool, onehot(codes[side : side + 1, :], 512)).astype(BF16)
    put_taps(taps, at, plane, COARSE_SHIFTS)
    return mm(weight[128 * side : 128 * side + 64], taps[:, at : at + 256]), plane


def coarse_inner(neighbours, table, from_lower, from_upper, hidden1, pre, pre_edge, w_coarse,
                 codes, ext, conv, fine_slope, taps):
    cells = table[3:4, :128]
    for row, a, base, payload in ((0, 0, 4, from_lower), (1, 2, 20, from_upper)):
        slots = arrived_slots(payload)
        code = [edge_code(v, cells, base, slots) for v in coarse_slots(neighbours, table, a)]
        codes[row : row + 1, :] = jnp.concatenate(code, axis=1)
    code = [local_code(v, cells) for v in coarse_slots(neighbours, table, 1)]
    codes[2:3, :] = jnp.concatenate(code, axis=1)
    codes[3:8, :] = jnp.full((5, 256), -1, I32)
    select = onehot(codes[2:3, :], 256)
    conv[...] = coarse_inner_conv(hidden1[...], select, tap_rows(w_coarse), taps, ext)
    for x in range(8):
        value = pre_edge[0] if x == 0 else pre_edge[1] if x == 7 else pre[x]
        fine_slope[x] = slope(value)


def coarse_outer(codes, hidden1, from_lower, from_upper, conv, up_back, w_coarse,
                 gated, delta, ext_edge, taps):
    weight = tap_rows(w_coarse)
    low, ext_edge[0] = coarse_outer_conv(codes, 0, hidden1[:, 768:], from_lower[...], weight, taps, 0)
    high, ext_edge[1] = coarse_outer_conv(codes, 1, hidden1[:, :256], from_upper[...], weight, taps, 256)
    value = conv[...]
    value = jnp.concatenate([value[:, :256] + low, value[:, 256:768], value[:, 768:] + high], axis=1)
    gated[...] = silu(value).astype(BF16)
    delta[...] = (up_back[...] * slope(value)).astype(BF16)


def decode(table, codes, gated, hidden, delta, cot_patch, ext, ext_edge, w_ups, w_adj,
           decoded, grads, back, taps, stack, spread):
    select = onehot(codes[2:3, :], 256)
    back[...] = coarse_inner_conv(delta[...], select, w_adj[...], taps, None)
    chosen = mm(by_rows(gated[...]), onehot(table[7:8, :1024], 256)).astype(BF16)
    for x in range(4):
        for jl in range(4):
            spread[64 * jl : 64 * jl + 64, 256 * x : 256 * x + 256] = (
                chosen[64 * x : 64 * x + 64, 256 * jl : 256 * jl + 256]
            )
    up = mm(w_ups[...], spread[...])
    compress = onehot(table[6:7, :128], 256)
    low = low_half((64, 128))
    for p in range(2):
        rows = jnp.concatenate([hidden[x, :, 256 * p : 256 * p + 256] for x in range(8)], axis=0)
        own = mm(rows, compress)
        for t in range(4):
            even, odd = [
                own[64 * x : 64 * x + 64] + up[64 * i : 64 * i + 64, 256 * t + 128 * p : 256 * t + 128 * p + 128]
                for i, x in ((0, 2 * t), (1, 2 * t + 1))
            ]
            decoded[2 * p, :, 128 * t : 128 * t + 128] = merge(low, even, odd).astype(BF16)
            decoded[2 * p + 1, :, 128 * t : 128 * t + 128] = merge_high(low, even, odd).astype(BF16)
    put_taps(taps, 0, ext_edge[0], COARSE_SHIFTS)
    for x in range(4):
        put_taps(taps, 256 + 256 * x, ext[:, 256 * x : 256 * x + 256], COARSE_SHIFTS)
    put_taps(taps, 1280, ext_edge[1], COARSE_SHIFTS)
    stack[...] = jnp.zeros(stack.shape, BF16)
    for a in range(3):
        stack[64 * a : 64 * a + 64, 256 * a : 256 * a + 1024] = delta[...]
    of_coarse = nt(taps[...], stack[...])
    of_up = jnp.concatenate([nt(cot_patch[...], gated[...]), jnp.zeros((64, 64), F32)], axis=0)
    grads[...] = jnp.concatenate([of_coarse, of_up], axis=1)


def finish(table, codes, delta, from_lower, from_upper, back, w_adj, coarse_pre, patch, w_dns, fine_slope,
           cot_plane, ext, ext_edge, grads, coarse_taps, spread, taps, stack):
    weight = w_adj[...]
    low, _ = coarse_outer_conv(codes, 0, delta[:, 768:], from_lower[...], weight, coarse_taps, 0)
    high, _ = coarse_outer_conv(codes, 1, delta[:, :256], from_upper[...], weight, coarse_taps, 256)
    value = back[...]
    value = jnp.concatenate([value[:, :256] + low, value[:, 256:768], value[:, 768:] + high], axis=1)
    down = (value * slope(coarse_pre[...])).astype(BF16)
    of_down = jnp.concatenate([nt(patch[...], down), jnp.zeros((64, 64), F32)], axis=0)
    chosen = mm(by_rows(down), onehot(table[8:9, :2048], 256)).astype(BF16)
    for x in range(4):
        for jl in range(4):
            spread[64 * jl : 64 * jl + 64, 512 * x : 512 * x + 512] = (
                chosen[64 * x : 64 * x + 64, 512 * jl : 512 * jl + 512]
            )
    for a in range(3):
        for plane in range(10):
            if not 0 <= plane - a < 8:
                stack[64 * a : 64 * a + 64, 512 * plane : 512 * plane + 512] = jnp.zeros((64, 512), BF16)
    for half in range(4):
        raised = mm(w_dns[...], spread[:, 512 * half : 512 * half + 512])
        for i in range(2):
            x = 2 * half + i
            total = cot_plane[x].astype(F32) + raised[64 * i : 64 * i + 64]
            fine = (total * fine_slope[x]).astype(BF16)
            for a in range(3):
                at = 512 * (x + a)
                stack[64 * a : 64 * a + 64, at : at + 512] = fine
    put_taps(taps, 0, ext_edge[0], FINE_SHIFTS)
    for x in range(8):
        put_taps(taps, 512 * x + 512, ext[x], FINE_SHIFTS)
    put_taps(taps, 4608, ext_edge[1], FINE_SHIFTS)
    grads[...] = jnp.concatenate([nt(taps[...], stack[...]), of_down], axis=1)


def unfold(factor, total, grad_fine, grad_down, grad_coarse, grad_up):
    for at, wide, narrow in ((0, grad_fine, grad_down), (256, grad_coarse, grad_up)):
        turned = (total[:, at : at + 256].astype(F32) * factor).T
        wide[...] = jnp.concatenate([turned[64 * a : 64 * a + 64, :] for a in range(3)], axis=1)
        narrow[...] = turned[192:256, :512]


VMEM_SPEC = pl.BlockSpec(memory_space=pltpu.VMEM)
SMEM_SPEC = pl.BlockSpec(memory_space=pltpu.SMEM)


def call(kernel, name, outs, scratch, *args):
    specs = [SMEM_SPEC if a.dtype == I32 and a.shape in ((4, 26), (2, 16)) else VMEM_SPEC for a in args]
    return pl.pallas_call(
        kernel,
        name=name,
        out_shape=[jax.ShapeDtypeStruct(s, t) for s, t in outs],
        in_specs=specs,
        out_specs=[VMEM_SPEC] * len(outs),
        scratch_shapes=[pltpu.VMEM(s, t) for s, t in scratch],
        compiler_params=pltpu.CompilerParams(vmem_limit_bytes=40 * 1024 * 1024),
    )(*args)


def passed_along(block, distance):
    devices = range(lax.axis_size("space"))
    route = [(i - distance, i) for i in devices if i - distance in devices]
    return lax.ppermute(block, "space", route)


def gray(i):
    return i ^ (i >> 1)


def ungray(g):
    i = 0
    while g:
        i ^= g
        g >>= 1
    return i


def stages(count):
    fields, offset, left = [], 0, count.bit_length() - 1
    for width in (1, 2, 2, 3):
        width = min(width, left)
        if width:
            fields.append((offset, width))
        offset, left = offset + width, left - width
    return [(offset, width, bit) for offset, width in fields for bit in range(width)]


def swap(x, stage):
    offset, width, bit = stage
    count = lax.axis_size(AXES)
    mask = ((1 << width) - 1) << offset
    pairs = []
    for i in range(count):
        other = ungray(gray((i & mask) >> offset) ^ (1 << bit))
        pairs.append((i, (i & ~mask) | (other << offset)))
    return lax.ppermute(x, AXES, pairs)


def my_bit(stage):
    offset, width, bit = stage
    place = (lax.axis_index(AXES) >> offset) & ((1 << width) - 1)
    return (gray(place) >> bit) & 1


def total_over_devices(x):
    todo = stages(lax.axis_size(AXES))
    split, whole = todo[:3], todo[3:]
    for stage in split:
        half = x.shape[0] // 2
        mine = my_bit(stage)
        keep = lax.dynamic_slice_in_dim(x, mine * half, half, 0)
        send = lax.dynamic_slice_in_dim(x, (1 - mine) * half, half, 0)
        x = keep.astype(F32) + swap(send.astype(BF16), stage).astype(F32)
    for stage in whole:
        rounded = x.astype(BF16)
        x = rounded.astype(F32) + swap(rounded, stage).astype(F32)
    x = x.astype(BF16)
    for stage in split[::-1]:
        first = my_bit(stage) == 0
        other = swap(x, stage)
        x = jnp.concatenate([jnp.where(first, x, other), jnp.where(first, other, x)], axis=0)
    return x


def shards(features, neighbours, send_list, w_fine, w_down, w_coarse, w_up, cotangent):
    feat, cot = features[0], cotangent[0]
    near, sends = neighbours[0], send_list[0, 0]
    table = jnp.asarray(TABLE)
    tile = (4, 64, 128)
    face = jax.ShapeDtypeStruct((144, 128), BF16)
    to_upper, to_lower = pl.pallas_call(
        pack_faces,
        name="pack_faces",
        grid=(1,),
        out_shape=[face, face],
        in_specs=[SMEM_SPEC, pl.BlockSpec(tile, lambda i: (0, 0, 0)), pl.BlockSpec(tile, lambda i: (0, 0, 3))],
        out_specs=[pl.BlockSpec((144, 128), lambda i: (0, 0))] * 2,
    )(sends, feat, feat)
    from_lower, from_upper = passed_along(to_upper, 1), passed_along(to_lower, -1)

    fine = (8, 64, 512)
    pre, ext0, edges, cot_plane, cot_patch, up_back, w_adj, w_ups, w_dns = call(
        fine_inner, "fine_inner",
        [(fine, F32), (fine, BF16), ((2, 64, 256), BF16), (fine, BF16), ((512, 1024), BF16), ((64, 1024), F32),
         ((192, 576), BF16), ((128, 256), BF16), ((128, 256), BF16)],
        [((576, 4096), BF16)],
        near, table, feat, cot, w_fine, w_up, w_down, w_coarse,
    )
    hidden0, patch0, coarse_pre, hidden1, pre_edge, ext0_edge = call(
        fine_outer, "fine_outer",
        [(fine, BF16), ((512, 1024), BF16), ((64, 1024), F32), ((64, 1024), BF16), ((2, 64, 512), F32),
         ((2, 64, 512), BF16)],
        [((576, 1024), BF16)],
        near, table, from_lower, from_upper, edges, pre, w_fine, w_down,
    )
    low1, high1 = passed_along(hidden1[:, 768:], 1), passed_along(hidden1[:, :256], -1)
    codes, ext1, conv, fine_slope = call(
        coarse_inner, "coarse_inner",
        [((8, 256), I32), ((64, 1024), BF16), ((64, 1024), F32), (fine, F32)],
        [((576, 1024), BF16)],
        near, table, from_lower, from_upper, hidden1, pre, pre_edge, w_coarse,
    )
    gated, delta_up, ext1_edge = call(
        coarse_outer, "coarse_outer",
        [((64, 1024), BF16), ((64, 1024), BF16), ((2, 64, 256), BF16)],
        [((576, 512), BF16)],
        codes, hidden1, low1, high1, conv, up_back, w_coarse,
    )
    low2, high2 = passed_along(delta_up[:, 768:], 1), passed_along(delta_up[:, :256], -1)
    decoded, grads_b, back = call(
        decode, "decode",
        [((4, 64, 512), BF16), ((576, 256), F32), ((64, 1024), F32)],
        [((576, 1536), BF16), ((192, 1536), BF16), ((256, 1024), BF16)],
        table, codes, gated, hidden0, delta_up, cot_patch, ext1, ext1_edge, w_ups, w_adj,
    )
    (grads_a,) = call(
        finish, "finish",
        [((576, 256), F32)],
        [((576, 512), BF16), ((256, 2048), BF16), ((576, 5120), BF16), ((192, 5120), BF16)],
        table, codes, delta_up, low2, high2, back, w_adj, coarse_pre, patch0, w_dns, fine_slope,
        cot_plane, ext0, ext0_edge,
    )
    total = total_over_devices(jnp.concatenate([grads_a, grads_b], axis=1))
    factor = 1.0 / math.sqrt(lax.axis_size(AXES) * 4 * 512)
    outs = call(
        lambda *refs: unfold(factor, *refs), "unfold",
        [(w_fine.shape, F32), (w_down.shape, F32), (w_coarse.shape, F32), (w_up.shape, F32)], [], total,
    )
    return (decoded[None], *outs)


def solution(mesh):
    in_specs = (
        P("rep", "space", None, None),
        P("rep", "space", None),
        P("rep", "space", None, None),
        P(),
        P(),
        P(),
        P(),
        P("rep", "space", None, None),
    )
    out_specs = (P("rep", "space", None, None), P(), P(), P(), P())
    return jax.shard_map(shards, mesh=mesh, in_specs=in_specs, out_specs=out_specs, check_vma=False)
```

time: 616 us -> 128 us (0.21)
  the two profiles are of different devices: /device:TPU:2 before, /device:TPU:1 now
where the time goes in v1:
time: 128 us; the launch traced here: 127 us
  starting transfers between devices  62.9 us (49%)
  waiting for transfers between devices  26.9 us (21%)
  local copies, waits for them, and re-layouts  19.4 us (15%)
  Pallas kernels  16.1 us (13%)
    ppermute x11, starting transfers between devices, swap(): return lax.ppermute(x, AXES, pairs)  47.8 us
    ppermute x11, waiting for transfers between devices, swap(): return lax.ppermute(x, AXES, pairs)  25.3 us
    unnamed x76, local copies, waits for them, and re-layouts  19.4 us
    ppermute x6, starting transfers between devices, passed_along(): return lax.ppermute(block, 'space', route)  15 us
    pallas_call x7, Pallas kernels, call(): pl.pallas_call(kernel, name=name, out_shape=[jax.ShapeDtypeStruct(s, t) f...  14.5 us
  transfers between devices with their start and end apart: 17, of which 12 were waited for; matrix products, arithmetic and copies ran while one was open for 0% of the time, Pallas kernels for 5%

profile of v1, /device:TPU:1, one launch (start us, length us, event | category | flops | bytes accessed | tf_op | source)
XLA Modules:
  0.0 126.9 jit_solution(9523046433192735638)
XLA Ops:
  0.6 1.6 %pack_faces.1 = (bf16[144,128]{1,0:T(8,128)(2,1)}, bf16[144,128]{1,0:T(8,128)(2,1)}) custom-call(s32[2,16]{1,0:T(2,128)} %bitcast.12, bf16[4,64,512]{2,1,0:T(8,128)(2,1)} %bitcast.5, bf16[4,64,512]{2,1,0:T(8,128)(2,1)} %bitcast.6), custom_call_target="tpu_custom_call" | custom-call | tf_op jit(solution)/shard_map/pack_faces/pallas_call | solution.py:476
  2.3 3.9 %collective-permute-start = (bf16[144,128]{1,0:T(8,128)(2,1)}, bf16[144,128]{1,0:T(8,128)(2,1)S(1)}, u32[]{:S(2)}, u32[]{:S(2)}) collective-permute-start(bf16[144,128]{1,0:T(8,128)(2,1)} %get-tuple-element.36), channel_id=1, source_target_pairs={{0,2},{2,4},{4,6},{6,8},{8,10},{10,12},{12,14},{14,16},{16,18},{18... | collective-permute-start | bytes 110600 | tf_op jit(solution)/shard_map/ppermute | solution.py:408
  6.2 1.3 %collective-permute-start.1 = (bf16[144,128]{1,0:T(8,128)(2,1)}, bf16[144,128]{1,0:T(8,128)(2,1)S(1)}, u32[]{:S(2)}, u32[]{:S(2)}) collective-permute-start(bf16[144,128]{1,0:T(8,128)(2,1)} %get-tuple-element.37), channel_id=1, source_target_pairs={{2,0},{4,2},{6,4},{8,6},{10,8},{12,10},{14,12},{16,14},{18,16},{20... | collective-permute-start | bytes 110600 | tf_op jit(solution)/shard_map/ppermute | solution.py:408
  14.6 3.2 %fine_inner.1 = (f32[8,64,512]{2,1,0:T(8,128)S(1)}, bf16[8,64,512]{2,1,0:T(8,128)(2,1)S(1)}, bf16[2,64,256]{2,1,0:T(8,128)(2,1)S(1)}, bf16[8,64,512]{2,1,0:T(8,1...) custom-call(s32[4,26]{1,0:T(4,128)S(1)} %bitcast.9, ...), custom_call_target="tpu_custom_call" | custom-call | tf_op jit(solution)/shard_map/fine_inner/pallas_call | solution.py:394
  20.2 2.3 %fine_outer.1 = (bf16[8,64,512]{2,1,0:T(8,128)(2,1)S(1)}, bf16[512,1024]{1,0:T(8,128)(2,1)S(1)}, f32[64,1024]{1,0:T(8,128)S(1)}, bf16[64,1024]{1,0:T(8,128)(2,1)...) custom-call(s32[4,26]{1,0:T(4,128)S(1)} %bitcast.10, s32[16,2048]{1,0:T(8,128)S(1)} %copy-done.1, ...), custom_call_target="tpu_custom_call" | custom-call | tf_op jit(solution)/shard_map/fine_outer/pallas_call | solution.py:394
  22.6 4.1 %collective-permute-start.2 = (bf16[64,256]{1,0:T(8,128)(2,1)S(1)}, bf16[64,256]{1,0:T(8,128)(2,1)S(1)}, u32[]{:S(2)}, u32[]{:S(2)}) collective-permute-start(bf16[64,256]{1,0:T(8,128)(2,1)S(1)} %get-tuple-element.76), channel_id=1, source_target_pairs={{0,2},{2,4},{4,6},{6,8},{8,10},{10,12},{12,14},{14,16},{16,18},{18... | collective-permute-start | bytes 98312 | tf_op jit(solution)/shard_map/ppermute | solution.py:408
  26.7 1.3 %collective-permute-start.3 = (bf16[64,256]{1,0:T(8,128)(2,1)S(1)}, bf16[64,256]{1,0:T(8,128)(2,1)S(1)}, u32[]{:S(2)}, u32[]{:S(2)}) collective-permute-start(bf16[64,256]{1,0:T(8,128)(2,1)S(1)} %get-tuple-element.75), channel_id=1, source_target_pairs={{2,0},{4,2},{6,4},{8,6},{10,8},{12,10},{14,12},{16,14},{18,16},{20... | collective-permute-start | bytes 98312 | tf_op jit(solution)/shard_map/ppermute | solution.py:408
  28.0 1.7 %coarse_inner.1 = (s32[8,256]{1,0:T(8,128)S(1)}, bf16[64,1024]{1,0:T(8,128)(2,1)S(1)}, f32[64,1024]{1,0:T(8,128)S(1)}, f32[8,64,512]{2,1,0:T(8,128)S(1)}) custom-call(s32[4,26]{1,0:T(4,128)S(1)} %bitcast.11, s32[16,2048]{1,0:T(8,128)S(1)} %copy-done.1, bf16[144,128]{1,0:T(8,128)(2,1)S(1)} %collective-permute-done.from_lower, ...), custom_call_target="tpu_custom_call" | custom-call | tf_op jit(solution)/shard_map/coarse_inner/pallas_call | solution.py:394
  29.8 1.6 %collective-permute-done.3.from_upper = bf16[64,256]{1,0:T(8,128)(2,1)S(1)} collective-permute-done((bf16[64,256]{1,0:T(8,128)(2,1)S(1)}, bf16[64,256]{1,0:T(8,128)(2,1)S(1)}, u32[]{:S(2)}, u32[]{:S(2)}) %collective-permute-start.3) | collective-permute-done | bytes 32800 | tf_op jit(solution)/shard_map/ppermute | solution.py:408
  33.6 3.1 %collective-permute-start.4 = (bf16[64,256]{1,0:T(8,128)(2,1)S(1)}, bf16[64,256]{1,0:T(8,128)(2,1)S(1)}, u32[]{:S(2)}, u32[]{:S(2)}) collective-permute-start(bf16[64,256]{1,0:T(8,128)(2,1)S(1)} %get-tuple-element.74), channel_id=1, source_target_pairs={{0,2},{2,4},{4,6},{6,8},{8,10},{10,12},{12,14},{14,16},{16,18},{18... | collective-permute-start | bytes 98312 | tf_op jit(solution)/shard_map/ppermute | solution.py:408
  36.7 1.3 %collective-permute-start.5 = (bf16[64,256]{1,0:T(8,128)(2,1)S(1)}, bf16[64,256]{1,0:T(8,128)(2,1)S(1)}, u32[]{:S(2)}, u32[]{:S(2)}) collective-permute-start(bf16[64,256]{1,0:T(8,128)(2,1)S(1)} %get-tuple-element.73), channel_id=1, source_target_pairs={{2,0},{4,2},{6,4},{8,6},{10,8},{12,10},{14,12},{16,14},{18,16},{20... | collective-permute-start | bytes 98312 | tf_op jit(solution)/shard_map/ppermute | solution.py:408
  43.0 1.8 %decode.1 = (bf16[4,64,512]{2,1,0:T(8,128)(2,1)}, f32[576,256]{1,0:T(8,128)S(1)}, f32[64,1024]{1,0:T(8,128)S(1)}) custom-call(s32[16,2048]{1,0:T(8,128)S(1)} %copy-done.1, s32[8,256]{1,0:T(8,128)S(1)} %get-tuple-element.42.codes, bf16[64,1024]{1,0:T(8,128)(2,1)S(1)} %copy-done.25, bf16[8,64,512]{2,1,0:T(8,128)(2,1)S(1)} %copy-done.15, ...), custom_call_target="tpu_custom_call" | custom-call | tf_op jit(solution)/shard_map/decode/pallas_call | solution.py:394
  48.5 3.2 %finish.1 = f32[576,256]{1,0:T(8,128)S(1)} custom-call(s32[16,2048]{1,0:T(8,128)S(1)} %copy-done.1, s32[8,256]{1,0:T(8,128)S(1)} %get-tuple-element.42.codes, bf16[64,1024]{1,0:T(8,128)(2,1)S(1)} %get-tuple-element.47.delta, bf16[64,256]{1,0:T(8,128)(2,1)S(1)} %copy-done.34, bf16[64,256]{1,0:T(8,128)(2,1)S(1)} %copy-done.36, ...), custom_call_target="tpu_custom_call" | custom-call | tf_op jit(solution)/shard_map/finish/pallas_call | solution.py:394
  51.8 3.0 %collective-permute-start.6 = (bf16[288,512]{1,0:T(8,128)(2,1)S(1)}, bf16[288,512]{1,0:T(8,128)(2,1)S(1)}, u32[]{:S(2)}, u32[]{:S(2)}) collective-permute-start(bf16[288,512]{1,0:T(8,128)(2,1)S(1)} %fusion.1), channel_id=1, source_target_pairs={{0,1},{1,0},{2,3},{3,2},{4,5},{5,4},{6,7},{7,6},{8,9},{9,8},{10,11... | collective-permute-start | bytes 884744 | tf_op jit(solution)/shard_map/ppermute | solution.py:441
  56.1 3.2 %collective-permute-start.7 = (bf16[144,512]{1,0:T(8,128)(2,1)S(1)}, bf16[144,512]{1,0:T(8,128)(2,1)S(1)}, u32[]{:S(2)}, u32[]{:S(2)}) collective-permute-start(bf16[144,512]{1,0:T(8,128)(2,1)S(1)} %dynamic-slice_convert_fusion), channel_id=1, source_target_pairs={{0,2},{1,3},{2,0},{3,1},{4,6},{5,7},{6,4},{7,5},{8,10},{9,11},{10,... | collective-permute-start | bytes 442376 | tf_op jit(solution)/shard_map/ppermute | solution.py:441
  59.3 3.9 %collective-permute-done.7 = bf16[144,512]{1,0:T(8,128)(2,1)S(1)} collective-permute-done((bf16[144,512]{1,0:T(8,128)(2,1)S(1)}, bf16[144,512]{1,0:T(8,128)(2,1)S(1)}, u32[]{:S(2)}, u32[]{:S(2)}) %collective-permute-start.7) | collective-permute-done | bytes 147488 | tf_op jit(solution)/shard_map/ppermute | solution.py:441
  63.3 6.1 %collective-permute-start.8 = (bf16[72,512]{1,0:T(8,128)(2,1)S(1)}, bf16[72,512]{1,0:T(8,128)(2,1)S(1)}, u32[]{:S(2)}, u32[]{:S(2)}) collective-permute-start(bf16[72,512]{1,0:T(8,128)(2,1)S(1)} %dynamic-slice_convert_fusion.1), channel_id=1, source_target_pairs={{0,6},{1,7},{2,4},{3,5},{4,2},{5,3},{6,0},{7,1},{8,14},{9,15},{10,... | collective-permute-start | bytes 221192 | tf_op jit(solution)/shard_map/ppermute | solution.py:441
  69.4 1.7 %collective-permute-done.8 = bf16[72,512]{1,0:T(8,128)(2,1)S(1)} collective-permute-done((bf16[72,512]{1,0:T(8,128)(2,1)S(1)}, bf16[72,512]{1,0:T(8,128)(2,1)S(1)}, u32[]{:S(2)}, u32[]{:S(2)}) %collective-permute-start.8) | collective-permute-done | bytes 73760 | tf_op jit(solution)/shard_map/ppermute | solution.py:441
  71.2 2.2 %collective-permute-start.9 = (bf16[72,512]{1,0:T(8,128)(2,1)S(1)}, bf16[72,512]{1,0:T(8,128)(2,1)S(1)}, u32[]{:S(2)}, u32[]{:S(2)}) collective-permute-start(bf16[72,512]{1,0:T(8,128)(2,1)S(1)} %add_convert_fusion.5), channel_id=1, source_target_pairs={{0,8},{1,9},{2,10},{3,11},{4,12},{5,13},{6,14},{7,15},{8,0},{9,1},... | collective-permute-start | bytes 221192 | tf_op jit(solution)/shard_map/ppermute | solution.py:441
  73.4 1.7 %collective-permute-done.9 = bf16[72,512]{1,0:T(8,128)(2,1)S(1)} collective-permute-done((bf16[72,512]{1,0:T(8,128)(2,1)S(1)}, bf16[72,512]{1,0:T(8,128)(2,1)S(1)}, u32[]{:S(2)}, u32[]{:S(2)}) %collective-permute-start.9) | collective-permute-done | bytes 73760 | tf_op jit(solution)/shard_map/ppermute | solution.py:441
  75.2 6.4 %collective-permute-start.10 = (bf16[72,512]{1,0:T(8,128)(2,1)S(1)}, bf16[72,512]{1,0:T(8,128)(2,1)S(1)}, u32[]{:S(2)}, u32[]{:S(2)}) collective-permute-start(bf16[72,512]{1,0:T(8,128)(2,1)S(1)} %add_convert_fusion.4), channel_id=1, source_target_pairs={{0,24},{1,25},{2,26},{3,27},{4,28},{5,29},{6,30},{7,31},{8,16},{9,... | collective-permute-start | bytes 221192 | tf_op jit(solution)/shard_map/ppermute | solution.py:441
  81.6 1.7 %collective-permute-done.10 = bf16[72,512]{1,0:T(8,128)(2,1)S(1)} collective-permute-done((bf16[72,512]{1,0:T(8,128)(2,1)S(1)}, bf16[72,512]{1,0:T(8,128)(2,1)S(1)}, u32[]{:S(2)}, u32[]{:S(2)}) %collective-permute-start.10) | collective-permute-done | bytes 73760 | tf_op jit(solution)/shard_map/ppermute | solution.py:441
  83.3 4.6 %collective-permute-start.11 = (bf16[72,512]{1,0:T(8,128)(2,1)S(1)}, bf16[72,512]{1,0:T(8,128)(2,1)S(1)}, u32[]{:S(2)}, u32[]{:S(2)}) collective-permute-start(bf16[72,512]{1,0:T(8,128)(2,1)S(1)} %add_convert_fusion.3), channel_id=1, source_target_pairs={{0,32},{1,33},{2,34},{3,35},{4,36},{5,37},{6,38},{7,39},{8,40},{9,... | collective-permute-start | bytes 221192 | tf_op jit(solution)/shard_map/ppermute | solution.py:441
  87.9 1.7 %collective-permute-done.11 = bf16[72,512]{1,0:T(8,128)(2,1)S(1)} collective-permute-done((bf16[72,512]{1,0:T(8,128)(2,1)S(1)}, bf16[72,512]{1,0:T(8,128)(2,1)S(1)}, u32[]{:S(2)}, u32[]{:S(2)}) %collective-permute-start.11) | collective-permute-done | bytes 73760 | tf_op jit(solution)/shard_map/ppermute | solution.py:441
  89.7 5.3 %collective-permute-start.12 = (bf16[72,512]{1,0:T(8,128)(2,1)S(1)}, bf16[72,512]{1,0:T(8,128)(2,1)S(1)}, u32[]{:S(2)}, u32[]{:S(2)}) collective-permute-start(bf16[72,512]{1,0:T(8,128)(2,1)S(1)} %add_convert_fusion.2), channel_id=1, source_target_pairs={{0,96},{1,97},{2,98},{3,99},{4,100},{5,101},{6,102},{7,103},{8,104... | collective-permute-start | bytes 221192 | tf_op jit(solution)/shard_map/ppermute | solution.py:441
  95.0 1.9 %collective-permute-done.12 = bf16[72,512]{1,0:T(8,128)(2,1)S(1)} collective-permute-done((bf16[72,512]{1,0:T(8,128)(2,1)S(1)}, bf16[72,512]{1,0:T(8,128)(2,1)S(1)}, u32[]{:S(2)}, u32[]{:S(2)}) %collective-permute-start.12) | collective-permute-done | bytes 73760 | tf_op jit(solution)/shard_map/ppermute | solution.py:441
  96.9 5.6 %collective-permute-start.13 = (bf16[72,512]{1,0:T(8,128)(2,1)S(1)}, bf16[72,512]{1,0:T(8,128)(2,1)S(1)}, u32[]{:S(2)}, u32[]{:S(2)}) collective-permute-start(bf16[72,512]{1,0:T(8,128)(2,1)S(1)} %add_convert_fusion.1), channel_id=1, source_target_pairs={{0,224},{1,225},{2,226},{3,227},{4,228},{5,229},{6,230},{7,231},{8... | collective-permute-start | bytes 221192 | tf_op jit(solution)/shard_map/ppermute | solution.py:441
  102.6 1.7 %collective-permute-done.13 = bf16[72,512]{1,0:T(8,128)(2,1)S(1)} collective-permute-done((bf16[72,512]{1,0:T(8,128)(2,1)S(1)}, bf16[72,512]{1,0:T(8,128)(2,1)S(1)}, u32[]{:S(2)}, u32[]{:S(2)}) %collective-permute-start.13) | collective-permute-done | bytes 73760 | tf_op jit(solution)/shard_map/ppermute | solution.py:441
  104.5 4.4 %collective-permute-done.14 = bf16[72,512]{1,0:T(8,128)(2,1)S(1)} collective-permute-done((bf16[72,512]{1,0:T(8,128)(2,1)S(1)}, bf16[72,512]{1,0:T(8,128)(2,1)S(1)}, u32[]{:S(2)}, u32[]{:S(2)}) %collective-permute-start.14) | collective-permute-done | bytes 73760 | tf_op jit(solution)/shard_map/ppermute | solution.py:441
  109.0 4.0 %collective-permute-done.15 = bf16[144,512]{1,0:T(8,128)(2,1)S(1)} collective-permute-done((bf16[144,512]{1,0:T(8,128)(2,1)S(1)}, bf16[144,512]{1,0:T(8,128)(2,1)S(1)}, u32[]{:S(2)}, u32[]{:S(2)}) %collective-permute-start.15) | collective-permute-done | bytes 147488 | tf_op jit(solution)/shard_map/ppermute | solution.py:441
  113.1 11.1 %collective-permute-start.16 = (bf16[288,512]{1,0:T(8,128)(2,1)S(1)}, bf16[288,512]{1,0:T(8,128)(2,1)S(1)}, u32[]{:S(2)}, u32[]{:S(2)}) collective-permute-start(bf16[288,512]{1,0:T(8,128)(2,1)S(1)} %pad_maximum_fusion.1), channel_id=1, source_target_pairs={{0,1},{1,0},{2,3},{3,2},{4,5},{5,4},{6,7},{7,6},{8,9},{9,8},{10,11... | collective-permute-start | bytes 884744 | tf_op jit(solution)/shard_map/ppermute | solution.py:441
  125.6 1.4 %unfold.1 = (f32[64,1728]{1,0:T(8,128)}, f32[64,512]{1,0:T(8,128)}, f32[64,1728]{1,0:T(8,128)}, f32[64,512]{1,0:T(8,128)}) custom-call(bf16[576,512]{1,0:T(8,128)(2,1)S(1)} %pad_maximum_fusion.refs_0_), custom_call_target="tpu_custom_call" | custom-call | tf_op jit(solution)/shard_map/unfold/pallas_call | solution.py:394
  (105 shorter events, 23.4 us)
Async XLA Ops:
  0.6 19.6 %copy-start.1 = (s32[16,2048]{1,0:T(8,128)S(1)}, s32[16,2048]{1,0:T(8,128)}, u32[]{:S(2)}) copy-start(s32[16,2048]{1,0:T(8,128)} %constant.26.clone.table) | copy-start | bytes 393220
  2.3 17.9 %collective-permute-start = (bf16[144,128]{1,0:T(8,128)(2,1)}, bf16[144,128]{1,0:T(8,128)(2,1)S(1)}, u32[]{:S(2)}, u32[]{:S(2)}) collective-permute-start(bf16[144,128]{1,0:T(8,128)(2,1)} %get-tuple-element.36), channel_id=1, source_target_pairs={{0,2},{2,4},{4,6},{6,8},{8,10},{10,12},{12,14},{14,16},{16,18},{18... | collective-permute-start | bytes 110600 | tf_op jit(solution)/shard_map/ppermute | solution.py:408
  6.2 14.0 %collective-permute-start.1 = (bf16[144,128]{1,0:T(8,128)(2,1)}, bf16[144,128]{1,0:T(8,128)(2,1)S(1)}, u32[]{:S(2)}, u32[]{:S(2)}) collective-permute-start(bf16[144,128]{1,0:T(8,128)(2,1)} %get-tuple-element.37), channel_id=1, source_target_pairs={{2,0},{4,2},{6,4},{8,6},{10,8},{12,10},{14,12},{16,14},{18,16},{20... | collective-permute-start | bytes 110600 | tf_op jit(solution)/shard_map/ppermute | solution.py:408
  20.2 9.6 %copy-start.10 = (bf16[8,64,512]{2,1,0:T(8,128)(2,1)}, bf16[8,64,512]{2,1,0:T(8,128)(2,1)S(1)}, u32[]{:S(2)}) copy-start(bf16[8,64,512]{2,1,0:T(8,128)(2,1)S(1)} %get-tuple-element.60.ext) | copy-start | bytes 1572868
  20.2 9.6 %copy-start.26 = (bf16[128,256]{1,0:T(8,128)(2,1)}, bf16[128,256]{1,0:T(8,128)(2,1)S(1)}, u32[]{:S(2)}) copy-start(bf16[128,256]{1,0:T(8,128)(2,1)S(1)} %get-tuple-element.57.w_dns) | copy-start | bytes 196612
  20.2 17.8 %copy-start.7 = (bf16[192,576]{1,0:T(8,128)(2,1)}, bf16[192,576]{1,0:T(8,128)(2,1)S(1)}, u32[]{:S(2)}) copy-start(bf16[192,576]{1,0:T(8,128)(2,1)S(1)} %get-tuple-element.52.w_adj) | copy-start | bytes 663556
  22.5 8.8 %copy-start.20 = (bf16[2,64,512]{2,1,0:T(8,128)(2,1)}, bf16[2,64,512]{2,1,0:T(8,128)(2,1)S(1)}, u32[]{:S(2)}) copy-start(bf16[2,64,512]{2,1,0:T(8,128)(2,1)S(1)} %get-tuple-element.61.ext_edge) | copy-start | bytes 393220
  22.5 9.7 %copy-start.14 = (bf16[8,64,512]{2,1,0:T(8,128)(2,1)}, bf16[8,64,512]{2,1,0:T(8,128)(2,1)S(1)}, u32[]{:S(2)}) copy-start(bf16[8,64,512]{2,1,0:T(8,128)(2,1)S(1)} %get-tuple-element.46.hidden) | copy-start | bytes 1572868
  22.6 9.7 %copy-start.17 = (f32[64,1024]{1,0:T(8,128)}, f32[64,1024]{1,0:T(8,128)S(1)}, u32[]{:S(2)}) copy-start(f32[64,1024]{1,0:T(8,128)S(1)} %get-tuple-element.55.coarse_pre) | copy-start | bytes 786436
  22.6 8.8 %copy-start.4 = (bf16[64,1728]{1,0:T(8,128)(2,1)S(1)}, bf16[64,1728]{1,0:T(8,128)(2,1)}, u32[]{:S(2)}) copy-start(bf16[64,1728]{1,0:T(8,128)(2,1)} %w_coarse.5) | copy-start | bytes 663556
  22.6 7.2 %collective-permute-start.2 = (bf16[64,256]{1,0:T(8,128)(2,1)S(1)}, bf16[64,256]{1,0:T(8,128)(2,1)S(1)}, u32[]{:S(2)}, u32[]{:S(2)}) collective-permute-start(bf16[64,256]{1,0:T(8,128)(2,1)S(1)} %get-tuple-element.76), channel_id=1, source_target_pairs={{0,2},{2,4},{4,6},{6,8},{8,10},{10,12},{12,14},{14,16},{16,18},{18... | collective-permute-start | bytes 98312 | tf_op jit(solution)/shard_map/ppermute | solution.py:408
  26.7 4.7 %collective-permute-start.3 = (bf16[64,256]{1,0:T(8,128)(2,1)S(1)}, bf16[64,256]{1,0:T(8,128)(2,1)S(1)}, u32[]{:S(2)}, u32[]{:S(2)}) collective-permute-start(bf16[64,256]{1,0:T(8,128)(2,1)S(1)} %get-tuple-element.75), channel_id=1, source_target_pairs={{2,0},{4,2},{6,4},{8,6},{10,8},{12,10},{14,12},{16,14},{18,16},{20... | collective-permute-start | bytes 98312 | tf_op jit(solution)/shard_map/ppermute | solution.py:408
  29.8 3.1 %copy-start.22 = (bf16[64,1024]{1,0:T(8,128)(2,1)}, bf16[64,1024]{1,0:T(8,128)(2,1)S(1)}, u32[]{:S(2)}) copy-start(bf16[64,1024]{1,0:T(8,128)(2,1)S(1)} %get-tuple-element.49.ext) | copy-start | bytes 393220
  29.8 8.2 %copy-start.30 = (bf16[128,256]{1,0:T(8,128)(2,1)S(1)}, bf16[128,256]{1,0:T(8,128)(2,1)}, u32[]{:S(2)}) copy-start(bf16[128,256]{1,0:T(8,128)(2,1)} %copy-done.29) | copy-start | bytes 196612
  33.6 11.2 %collective-permute-start.4 = (bf16[64,256]{1,0:T(8,128)(2,1)S(1)}, bf16[64,256]{1,0:T(8,128)(2,1)S(1)}, u32[]{:S(2)}, u32[]{:S(2)}) collective-permute-start(bf16[64,256]{1,0:T(8,128)(2,1)S(1)} %get-tuple-element.74), channel_id=1, source_target_pairs={{0,2},{2,4},{4,6},{6,8},{8,10},{10,12},{12,14},{14,16},{16,18},{18... | collective-permute-start | bytes 98312 | tf_op jit(solution)/shard_map/ppermute | solution.py:408
  36.7 8.7 %collective-permute-start.5 = (bf16[64,256]{1,0:T(8,128)(2,1)S(1)}, bf16[64,256]{1,0:T(8,128)(2,1)S(1)}, u32[]{:S(2)}, u32[]{:S(2)}) collective-permute-start(bf16[64,256]{1,0:T(8,128)(2,1)S(1)} %get-tuple-element.73), channel_id=1, source_target_pairs={{2,0},{4,2},{6,4},{8,6},{10,8},{12,10},{14,12},{16,14},{18,16},{20... | collective-permute-start | bytes 98312 | tf_op jit(solution)/shard_map/ppermute | solution.py:408
  42.9 3.1 %copy-start.11 = (bf16[8,64,512]{2,1,0:T(8,128)(2,1)S(1)}, bf16[8,64,512]{2,1,0:T(8,128)(2,1)}, u32[]{:S(2)}) copy-start(bf16[8,64,512]{2,1,0:T(8,128)(2,1)} %copy-done.10) | copy-start | bytes 1572868
  42.9 3.1 %copy-start.13 = (bf16[8,64,512]{2,1,0:T(8,128)(2,1)S(1)}, bf16[8,64,512]{2,1,0:T(8,128)(2,1)}, u32[]{:S(2)}) copy-start(bf16[8,64,512]{2,1,0:T(8,128)(2,1)} %copy-done.12) | copy-start | bytes 1572868
  42.9 3.1 %copy-start.18 = (f32[64,1024]{1,0:T(8,128)S(1)}, f32[64,1024]{1,0:T(8,128)}, u32[]{:S(2)}) copy-start(f32[64,1024]{1,0:T(8,128)} %copy-done.17) | copy-start | bytes 786436
  42.9 3.1 %copy-start.21 = (bf16[2,64,512]{2,1,0:T(8,128)(2,1)S(1)}, bf16[2,64,512]{2,1,0:T(8,128)(2,1)}, u32[]{:S(2)}) copy-start(bf16[2,64,512]{2,1,0:T(8,128)(2,1)} %copy-done.20) | copy-start | bytes 393220
  42.9 3.1 %copy-start.27 = (bf16[128,256]{1,0:T(8,128)(2,1)S(1)}, bf16[128,256]{1,0:T(8,128)(2,1)}, u32[]{:S(2)}) copy-start(bf16[128,256]{1,0:T(8,128)(2,1)} %copy-done.26) | copy-start | bytes 196612
  51.8 4.2 %collective-permute-start.6 = (bf16[288,512]{1,0:T(8,128)(2,1)S(1)}, bf16[288,512]{1,0:T(8,128)(2,1)S(1)}, u32[]{:S(2)}, u32[]{:S(2)}) collective-permute-start(bf16[288,512]{1,0:T(8,128)(2,1)S(1)} %fusion.1), channel_id=1, source_target_pairs={{0,1},{1,0},{2,3},{3,2},{4,5},{5,4},{6,7},{7,6},{8,9},{9,8},{10,11... | collective-permute-start | bytes 884744 | tf_op jit(solution)/shard_map/ppermute | solution.py:441
  56.1 7.1 %collective-permute-start.7 = (bf16[144,512]{1,0:T(8,128)(2,1)S(1)}, bf16[144,512]{1,0:T(8,128)(2,1)S(1)}, u32[]{:S(2)}, u32[]{:S(2)}) collective-permute-start(bf16[144,512]{1,0:T(8,128)(2,1)S(1)} %dynamic-slice_convert_fusion), channel_id=1, source_target_pairs={{0,2},{1,3},{2,0},{3,1},{4,6},{5,7},{6,4},{7,5},{8,10},{9,11},{10,... | collective-permute-start | bytes 442376 | tf_op jit(solution)/shard_map/ppermute | solution.py:441
  63.3 7.9 %collective-permute-start.8 = (bf16[72,512]{1,0:T(8,128)(2,1)S(1)}, bf16[72,512]{1,0:T(8,128)(2,1)S(1)}, u32[]{:S(2)}, u32[]{:S(2)}) collective-permute-start(bf16[72,512]{1,0:T(8,128)(2,1)S(1)} %dynamic-slice_convert_fusion.1), channel_id=1, source_target_pairs={{0,6},{1,7},{2,4},{3,5},{4,2},{5,3},{6,0},{7,1},{8,14},{9,15},{10,... | collective-permute-start | bytes 221192 | tf_op jit(solution)/shard_map/ppermute | solution.py:441
  71.2 4.0 %collective-permute-start.9 = (bf16[72,512]{1,0:T(8,128)(2,1)S(1)}, bf16[72,512]{1,0:T(8,128)(2,1)S(1)}, u32[]{:S(2)}, u32[]{:S(2)}) collective-permute-start(bf16[72,512]{1,0:T(8,128)(2,1)S(1)} %add_convert_fusion.5), channel_id=1, source_target_pairs={{0,8},{1,9},{2,10},{3,11},{4,12},{5,13},{6,14},{7,15},{8,0},{9,1},... | collective-permute-start | bytes 221192 | tf_op jit(solution)/shard_map/ppermute | solution.py:441
  75.2 8.1 %collective-permute-start.10 = (bf16[72,512]{1,0:T(8,128)(2,1)S(1)}, bf16[72,512]{1,0:T(8,128)(2,1)S(1)}, u32[]{:S(2)}, u32[]{:S(2)}) collective-permute-start(bf16[72,512]{1,0:T(8,128)(2,1)S(1)} %add_convert_fusion.4), channel_id=1, source_target_pairs={{0,24},{1,25},{2,26},{3,27},{4,28},{5,29},{6,30},{7,31},{8,16},{9,... | collective-permute-start | bytes 221192 | tf_op jit(solution)/shard_map/ppermute | solution.py:441
  83.3 6.3 %collective-permute-start.11 = (bf16[72,512]{1,0:T(8,128)(2,1)S(1)}, bf16[72,512]{1,0:T(8,128)(2,1)S(1)}, u32[]{:S(2)}, u32[]{:S(2)}) collective-permute-start(bf16[72,512]{1,0:T(8,128)(2,1)S(1)} %add_convert_fusion.3), channel_id=1, source_target_pairs={{0,32},{1,33},{2,34},{3,35},{4,36},{5,37},{6,38},{7,39},{8,40},{9,... | collective-permute-start | bytes 221192 | tf_op jit(solution)/shard_map/ppermute | solution.py:441
  89.7 7.2 %collective-permute-start.12 = (bf16[72,512]{1,0:T(8,128)(2,1)S(1)}, bf16[72,512]{1,0:T(8,128)(2,1)S(1)}, u32[]{:S(2)}, u32[]{:S(2)}) collective-permute-start(bf16[72,512]{1,0:T(8,128)(2,1)S(1)} %add_convert_fusion.2), channel_id=1, source_target_pairs={{0,96},{1,97},{2,98},{3,99},{4,100},{5,101},{6,102},{7,103},{8,104... | collective-permute-start | bytes 221192 | tf_op jit(solution)/shard_map/ppermute | solution.py:441
  96.9 7.4 %collective-permute-start.13 = (bf16[72,512]{1,0:T(8,128)(2,1)S(1)}, bf16[72,512]{1,0:T(8,128)(2,1)S(1)}, u32[]{:S(2)}, u32[]{:S(2)}) collective-permute-start(bf16[72,512]{1,0:T(8,128)(2,1)S(1)} %add_convert_fusion.1), channel_id=1, source_target_pairs={{0,224},{1,225},{2,226},{3,227},{4,228},{5,229},{6,230},{7,231},{8... | collective-permute-start | bytes 221192 | tf_op jit(solution)/shard_map/ppermute | solution.py:441
  104.4 4.5 %collective-permute-start.14 = (bf16[72,512]{1,0:T(8,128)(2,1)S(1)}, bf16[72,512]{1,0:T(8,128)(2,1)S(1)}, u32[]{:S(2)}, u32[]{:S(2)}) collective-permute-start(bf16[72,512]{1,0:T(8,128)(2,1)S(1)} %add_convert_fusion), channel_id=1, source_target_pairs={{0,6},{1,7},{2,4},{3,5},{4,2},{5,3},{6,0},{7,1},{8,14},{9,15},{10,... | collective-permute-start | bytes 221192 | tf_op jit(solution)/shard_map/ppermute | solution.py:441
  108.9 4.1 %collective-permute-start.15 = (bf16[144,512]{1,0:T(8,128)(2,1)S(1)}, bf16[144,512]{1,0:T(8,128)(2,1)S(1)}, u32[]{:S(2)}, u32[]{:S(2)}) collective-permute-start(bf16[144,512]{1,0:T(8,128)(2,1)S(1)} %pad_maximum_fusion.2), channel_id=1, source_target_pairs={{0,2},{1,3},{2,0},{3,1},{4,6},{5,7},{6,4},{7,5},{8,10},{9,11},{10,... | collective-permute-start | bytes 442376 | tf_op jit(solution)/shard_map/ppermute | solution.py:441
  113.1 12.3 %collective-permute-start.16 = (bf16[288,512]{1,0:T(8,128)(2,1)S(1)}, bf16[288,512]{1,0:T(8,128)(2,1)S(1)}, u32[]{:S(2)}, u32[]{:S(2)}) collective-permute-start(bf16[288,512]{1,0:T(8,128)(2,1)S(1)} %pad_maximum_fusion.1), channel_id=1, source_target_pairs={{0,1},{1,0},{2,3},{3,2},{4,5},{5,4},{6,7},{7,6},{8,9},{9,8},{10,11... | collective-permute-start | bytes 884744 | tf_op jit(solution)/shard_map/ppermute | solution.py:441
  (23 other events, 19.4 us)

commit v2 on v1

--- a/solution.py
+++ b/solution.py
@@ -6,12 +6,14 @@
 from jax import lax
 from jax.experimental import pallas as pl
 from jax.experimental.pallas import tpu as pltpu
+from jax.sharding import Mesh
 from jax.sharding import PartitionSpec as P
 
 F32 = jnp.float32
 BF16 = jnp.bfloat16
 I32 = jnp.int32
-AXES = ("space", "rep")
+CHIPS = ("z", "y", "x")
+AXES = ("z", "y", "x", "core")
 FINE_SHIFTS = [10 * (c - 1) + (e - 1) for c in range(3) for e in range(3)]
 COARSE_SHIFTS = [6 * (c - 1) + (e - 1) for c in range(3) for e in range(3)]
 
@@ -180,8 +182,8 @@
         out[128:144, :] = slots.astype(F32).astype(BF16)
 
 
-def fine_inner(neighbours, table, feat, cot, w_fine, w_up, w_down, w_coarse,
-               pre, ext, edges, cot_plane, cot_patch, up_back, w_adj, w_ups, w_dns, taps):
+def fine_inner(neighbours, table, w_fine, w_down, w_coarse, w_up, feat, cot,
+               pre, edges, up_back, ext, cot_plane, cot_patch, w_adj, w_ups, w_dns, taps):
     planes = natural_planes(feat)
     edges[0], edges[1] = planes[0], planes[7]
     cells = table[1:2, :128]
@@ -226,7 +228,7 @@
 
 
 def fine_outer(neighbours, table, from_lower, from_upper, edges, pre, w_fine, w_down,
-               hidden, patch, coarse_pre, hidden1, pre_edge, ext_edge, taps):
+               hidden, patch, coarse_pre, hidden1, pre_edge, ext_edge, to_upper, to_lower, taps):
     cells = table[1:2, :128]
     weight = tap_rows(w_fine)
     for side, a, base, payload in ((0, 0, 4, from_lower), (1, 2, 20, from_upper)):
@@ -247,7 +249,9 @@
         put_patches(patch, mm(rows, down).astype(BF16), p)
     value = mm(w_down[...], patch[...])
     coarse_pre[...] = value
-    hidden1[...] = silu(value).astype(BF16)
+    value = silu(value).astype(BF16)
+    hidden1[...] = value
+    to_upper[...], to_lower[...] = value[:, 768:], value[:, :256]
 
 
 def by_rows(v):
@@ -280,8 +284,9 @@
     return mm(weight[128 * side : 128 * side + 64], taps[:, at : at + 256]), plane
 
 
-def coarse_inner(neighbours, table, from_lower, from_upper, hidden1, pre, pre_edge, w_coarse,
-                 codes, ext, conv, fine_slope, taps):
+def coarse_inner(neighbours, table, from_lower, from_upper, hidden1, pre, pre_edge, w_coarse, coarse_pre,
+                 codes, ext, conv, fine_slope, coarse_slope, taps):
+    coarse_slope[...] = slope(coarse_pre[...])
     cells = table[3:4, :128]
     for row, a, base, payload in ((0, 0, 4, from_lower), (1, 2, 20, from_upper)):
         slots = arrived_slots(payload)
@@ -298,17 +303,19 @@
 
 
 def coarse_outer(codes, hidden1, from_lower, from_upper, conv, up_back, w_coarse,
-                 gated, delta, ext_edge, taps):
+                 gated, delta, ext_edge, to_upper, to_lower, taps):
     weight = tap_rows(w_coarse)
     low, ext_edge[0] = coarse_outer_conv(codes, 0, hidden1[:, 768:], from_lower[...], weight, taps, 0)
     high, ext_edge[1] = coarse_outer_conv(codes, 1, hidden1[:, :256], from_upper[...], weight, taps, 256)
     value = conv[...]
     value = jnp.concatenate([value[:, :256] + low, value[:, 256:768], value[:, 768:] + high], axis=1)
     gated[...] = silu(value).astype(BF16)
-    delta[...] = (up_back[...] * slope(value)).astype(BF16)
-
-
-def decode(table, codes, gated, hidden, delta, cot_patch, ext, ext_edge, w_ups, w_adj,
+    value = (up_back[...] * slope(value)).astype(BF16)
+    delta[...] = value
+    to_upper[...], to_lower[...] = value[:, 768:], value[:, :256]
+
+
+def decode(table, codes, gated, delta, ext, ext_edge, hidden, cot_patch, w_ups, w_adj,
            decoded, grads, back, taps, stack, spread):
     select = onehot(codes[2:3, :], 256)
     back[...] = coarse_inner_conv(delta[...], select, w_adj[...], taps, None)
@@ -340,17 +347,20 @@
         stack[64 * a : 64 * a + 64, 256 * a : 256 * a + 1024] = delta[...]
     of_coarse = nt(taps[...], stack[...])
     of_up = jnp.concatenate([nt(cot_patch[...], gated[...]), jnp.zeros((64, 64), F32)], axis=0)
-    grads[...] = jnp.concatenate([of_coarse, of_up], axis=1)
-
-
-def finish(table, codes, delta, from_lower, from_upper, back, w_adj, coarse_pre, patch, w_dns, fine_slope,
+    put_grads(grads, of_coarse, of_up)
+
+
+def finish(ready, table, codes, delta, from_lower, from_upper, back, w_adj, coarse_slope, patch, w_dns, fine_slope,
            cot_plane, ext, ext_edge, grads, coarse_taps, spread, taps, stack):
+    ready[0]()
     weight = w_adj[...]
     low, _ = coarse_outer_conv(codes, 0, delta[:, 768:], from_lower[...], weight, coarse_taps, 0)
     high, _ = coarse_outer_conv(codes, 1, delta[:, :256], from_upper[...], weight, coarse_taps, 256)
     value = back[...]
     value = jnp.concatenate([value[:, :256] + low, value[:, 256:768], value[:, 768:] + high], axis=1)
-    down = (value * slope(coarse_pre[...])).astype(BF16)
+    ready[1]()
+    down = (value * coarse_slope[...]).astype(BF16)
+    ready[2]()
     of_down = jnp.concatenate([nt(patch[...], down), jnp.zeros((64, 64), F32)], axis=0)
     chosen = mm(by_rows(down), onehot(table[8:9, :2048], 256)).astype(BF16)
     for x in range(4):
@@ -362,6 +372,8 @@
         for plane in range(10):
             if not 0 <= plane - a < 8:
                 stack[64 * a : 64 * a + 64, 512 * plane : 512 * plane + 512] = jnp.zeros((64, 512), BF16)
+    for wait in ready[3:]:
+        wait()
     for half in range(4):
         raised = mm(w_dns[...], spread[:, 512 * half : 512 * half + 512])
         for i in range(2):
@@ -375,96 +387,122 @@
     for x in range(8):
         put_taps(taps, 512 * x + 512, ext[x], FINE_SHIFTS)
     put_taps(taps, 4608, ext_edge[1], FINE_SHIFTS)
-    grads[...] = jnp.concatenate([nt(taps[...], stack[...]), of_down], axis=1)
+    put_grads(grads, nt(taps[...], stack[...]), of_down)
+
+
+def put_grads(grads, wide, narrow):
+    grads[0:576, :] = wide[:, :128]
+    grads[576:1152, :] = jnp.concatenate([wide[:, 128:], narrow], axis=1)
 
 
 def unfold(factor, total, grad_fine, grad_down, grad_coarse, grad_up):
-    for at, wide, narrow in ((0, grad_fine, grad_down), (256, grad_coarse, grad_up)):
-        turned = (total[:, at : at + 256].astype(F32) * factor).T
+    for at, wide, narrow in ((0, grad_fine, grad_down), (1152, grad_coarse, grad_up)):
+        both = jnp.concatenate([total[at : at + 576, :], total[at + 576 : at + 1152, :]], axis=1)
+        turned = (both.astype(F32) * factor).T
         wide[...] = jnp.concatenate([turned[64 * a : 64 * a + 64, :] for a in range(3)], axis=1)
         narrow[...] = turned[192:256, :512]
 
 
+GRANT = 53 * 1024 * 1024
 VMEM_SPEC = pl.BlockSpec(memory_space=pltpu.VMEM)
 SMEM_SPEC = pl.BlockSpec(memory_space=pltpu.SMEM)
-
-
-def call(kernel, name, outs, scratch, *args):
-    specs = [SMEM_SPEC if a.dtype == I32 and a.shape in ((4, 26), (2, 16)) else VMEM_SPEC for a in args]
+HBM_SPEC = pl.BlockSpec(memory_space=pltpu.HBM)
+
+
+def whole(shape):
+    return pl.BlockSpec(shape, lambda i: (0,) * len(shape))
+
+
+def place(shape, kind):
+    size = math.prod(shape) * jnp.dtype(kind).itemsize
+    return VMEM_SPEC if size <= 64 * 1024 or shape == (1152, 128) else whole(shape)
+
+
+def call(kernel, name, outs, scratch, near, far=(), late=False):
+    counts = (len(near), len(far), len(outs), len(scratch), len(far))
+    far_outs = [k for k, (away, _, _) in enumerate(outs) if away]
+
+    def body(*refs):
+        groups, at = [], 0
+        for count in counts:
+            groups.append(refs[at : at + count])
+            at += count
+        near_refs, far_refs, out_refs, own, landed = groups
+        staged, (in_sem, out_sem) = refs[at : at + len(far_outs)], refs[at + len(far_outs) :]
+        arriving = [pltpu.make_async_copy(s, d, in_sem.at[k]) for k, (s, d) in enumerate(zip(far_refs, landed))]
+        for copy in arriving:
+            copy.start()
+        results = list(out_refs)
+        for k, buffer in zip(far_outs, staged):
+            results[k] = buffer
+        if late:
+            kernel([copy.wait for copy in arriving], *near_refs, *landed, *results, *own)
+        else:
+            for copy in arriving:
+                copy.wait()
+            kernel(*near_refs, *landed, *results, *own)
+        leaving = [
+            pltpu.make_async_copy(buffer, out_refs[k], out_sem.at[n])
+            for n, (k, buffer) in enumerate(zip(far_outs, staged))
+        ]
+        for copy in leaving:
+            copy.start()
+        for copy in leaving:
+            copy.wait()
+
+    small = ((4, 26), (2, 16))
     return pl.pallas_call(
-        kernel,
+        body,
         name=name,
-        out_shape=[jax.ShapeDtypeStruct(s, t) for s, t in outs],
-        in_specs=specs,
-        out_specs=[VMEM_SPEC] * len(outs),
-        scratch_shapes=[pltpu.VMEM(s, t) for s, t in scratch],
-        compiler_params=pltpu.CompilerParams(vmem_limit_bytes=40 * 1024 * 1024),
-    )(*args)
+        out_shape=[jax.ShapeDtypeStruct(shape, kind) for _, shape, kind in outs],
+        grid=(1,),
+        in_specs=[SMEM_SPEC if x.shape in small else place(x.shape, x.dtype) for x in near] + [HBM_SPEC] * len(far),
+        out_specs=[HBM_SPEC if away else place(shape, kind) for away, shape, kind in outs],
+        scratch_shapes=[pltpu.VMEM(shape, kind) for shape, kind in scratch]
+        + [pltpu.VMEM(x.shape, x.dtype) for x in far]
+        + [pltpu.VMEM(outs[k][1], outs[k][2]) for k in far_outs]
+        + [pltpu.SemaphoreType.DMA((max(len(far), 1),)), pltpu.SemaphoreType.DMA((max(len(far_outs), 1),))],
+        compiler_params=pltpu.CompilerParams(vmem_limit_bytes=GRANT),
+    )(*near, *far)
 
 
 def passed_along(block, distance):
-    devices = range(lax.axis_size("space"))
+    devices = range(lax.axis_size(CHIPS))
     route = [(i - distance, i) for i in devices if i - distance in devices]
-    return lax.ppermute(block, "space", route)
-
-
-def gray(i):
-    return i ^ (i >> 1)
-
-
-def ungray(g):
-    i = 0
-    while g:
-        i ^= g
-        g >>= 1
-    return i
-
-
-def stages(count):
-    fields, offset, left = [], 0, count.bit_length() - 1
-    for width in (1, 2, 2, 3):
-        width = min(width, left)
-        if width:
-            fields.append((offset, width))
-        offset, left = offset + width, left - width
-    return [(offset, width, bit) for offset, width in fields for bit in range(width)]
-
-
-def swap(x, stage):
-    offset, width, bit = stage
-    count = lax.axis_size(AXES)
-    mask = ((1 << width) - 1) << offset
-    pairs = []
-    for i in range(count):
-        other = ungray(gray((i & mask) >> offset) ^ (1 << bit))
-        pairs.append((i, (i & ~mask) | (other << offset)))
-    return lax.ppermute(x, AXES, pairs)
-
-
-def my_bit(stage):
-    offset, width, bit = stage
-    place = (lax.axis_index(AXES) >> offset) & ((1 << width) - 1)
-    return (gray(place) >> bit) & 1
+    return lax.ppermute(block, CHIPS, route)
+
+
+def other_core(x):
+    return lax.ppermute(x, "core", [(0, 1), (1, 0)])
+
+
+def dealt(x, axes):
+    count = lax.axis_size(axes)
+    return lax.all_to_all(x.reshape(count, -1, 128), axes, 0, 0, tiled=True)
+
+
+def told(x, axes):
+    return dealt(jnp.broadcast_to(x, (lax.axis_size(axes), *x.shape)), axes)
+
+
+def summed(blocks):
+    total = blocks[0].astype(F32)
+    for k in range(1, blocks.shape[0]):
+        total = total + blocks[k].astype(F32)
+    return total
 
 
 def total_over_devices(x):
-    todo = stages(lax.axis_size(AXES))
-    split, whole = todo[:3], todo[3:]
-    for stage in split:
-        half = x.shape[0] // 2
-        mine = my_bit(stage)
-        keep = lax.dynamic_slice_in_dim(x, mine * half, half, 0)
-        send = lax.dynamic_slice_in_dim(x, (1 - mine) * half, half, 0)
-        x = keep.astype(F32) + swap(send.astype(BF16), stage).astype(F32)
-    for stage in whole:
-        rounded = x.astype(BF16)
-        x = rounded.astype(F32) + swap(rounded, stage).astype(F32)
-    x = x.astype(BF16)
-    for stage in split[::-1]:
-        first = my_bit(stage) == 0
-        other = swap(x, stage)
-        x = jnp.concatenate([jnp.where(first, x, other), jnp.where(first, other, x)], axis=0)
-    return x
+    core = lax.axis_index("core")
+    half = x.shape[0] // 2
+    keep = lax.dynamic_slice_in_dim(x, core * half, half, 0)
+    send = lax.dynamic_slice_in_dim(x, (1 - core) * half, half, 0)
+    x = keep + other_core(send.astype(BF16)).astype(F32)
+    x = summed(dealt(x.astype(BF16), ("y", "x")))
+    x = summed(told(x.astype(BF16), "z"))
+    x = told(x.astype(BF16), ("y", "x")).reshape(half, 128)
+    other = other_core(x)
+    return jnp.concatenate([jnp.where(core == 0, x, other), jnp.where(core == 0, other, x)], axis=0)
 
 
 def shards(features, neighbours, send_list, w_fine, w_down, w_coarse, w_up, cotangent):
@@ -480,70 +518,75 @@
         out_shape=[face, face],
         in_specs=[SMEM_SPEC, pl.BlockSpec(tile, lambda i: (0, 0, 0)), pl.BlockSpec(tile, lambda i: (0, 0, 3))],
         out_specs=[pl.BlockSpec((144, 128), lambda i: (0, 0))] * 2,
+        compiler_params=pltpu.CompilerParams(vmem_limit_bytes=60 * 1024 * 1024),
     )(sends, feat, feat)
     from_lower, from_upper = passed_along(to_upper, 1), passed_along(to_lower, -1)
 
     fine = (8, 64, 512)
-    pre, ext0, edges, cot_plane, cot_patch, up_back, w_adj, w_ups, w_dns = call(
+    pre, edges, up_back, ext0, cot_plane, cot_patch, w_adj, w_ups, w_dns = call(
         fine_inner, "fine_inner",
-        [(fine, F32), (fine, BF16), ((2, 64, 256), BF16), (fine, BF16), ((512, 1024), BF16), ((64, 1024), F32),
-         ((192, 576), BF16), ((128, 256), BF16), ((128, 256), BF16)],
+        [(0, fine, F32), (0, (2, 64, 256), BF16), (0, (64, 1024), F32), (0, fine, BF16), (0, fine, BF16),
+         (0, (512, 1024), BF16), (0, (192, 576), BF16), (0, (128, 256), BF16), (0, (128, 256), BF16)],
         [((576, 4096), BF16)],
-        near, table, feat, cot, w_fine, w_up, w_down, w_coarse,
-    )
-    hidden0, patch0, coarse_pre, hidden1, pre_edge, ext0_edge = call(
+        [near, table, w_fine, w_down, w_coarse], [w_up, feat, cot],
+    )
+    hidden0, patch0, coarse_pre, hidden1, pre_edge, ext0_edge, to_upper, to_lower = call(
         fine_outer, "fine_outer",
-        [(fine, BF16), ((512, 1024), BF16), ((64, 1024), F32), ((64, 1024), BF16), ((2, 64, 512), F32),
-         ((2, 64, 512), BF16)],
+        [(0, fine, BF16), (0, (512, 1024), BF16), (0, (64, 1024), F32), (0, (64, 1024), BF16), (0, (2, 64, 512), F32),
+         (0, (2, 64, 512), BF16), (0, (64, 256), BF16), (0, (64, 256), BF16)],
         [((576, 1024), BF16)],
-        near, table, from_lower, from_upper, edges, pre, w_fine, w_down,
-    )
-    low1, high1 = passed_along(hidden1[:, 768:], 1), passed_along(hidden1[:, :256], -1)
-    codes, ext1, conv, fine_slope = call(
+        [near, table, from_lower, from_upper, edges, pre, w_fine, w_down],
+    )
+    low1, high1 = passed_along(to_upper, 1), passed_along(to_lower, -1)
+    codes, ext1, conv, fine_slope, coarse_slope = call(
         coarse_inner, "coarse_inner",
-        [((8, 256), I32), ((64, 1024), BF16), ((64, 1024), F32), (fine, F32)],
+        [(0, (8, 256), I32), (0, (64, 1024), BF16), (0, (64, 1024), F32), (0, fine, F32), (0, (64, 1024), F32)],
         [((576, 1024), BF16)],
-        near, table, from_lower, from_upper, hidden1, pre, pre_edge, w_coarse,
-    )
-    gated, delta_up, ext1_edge = call(
+        [near, table, from_lower, from_upper, hidden1, pre, pre_edge, w_coarse, coarse_pre],
+    )
+    gated, delta_up, ext1_edge, to_upper, to_lower = call(
         coarse_outer, "coarse_outer",
-        [((64, 1024), BF16), ((64, 1024), BF16), ((2, 64, 256), BF16)],
+        [(0, (64, 1024), BF16), (0, (64, 1024), BF16), (0, (2, 64, 256), BF16), (0, (64, 256), BF16), (0, (64, 256), BF16)],
         [((576, 512), BF16)],
-        codes, hidden1, low1, high1, conv, up_back, w_coarse,
-    )
-    low2, high2 = passed_along(delta_up[:, 768:], 1), passed_along(delta_up[:, :256], -1)
+        [codes, hidden1, low1, high1, conv, up_back, w_coarse],
+    )
+    low2, high2 = passed_along(to_upper, 1), passed_along(to_lower, -1)
     decoded, grads_b, back = call(
         decode, "decode",
-        [((4, 64, 512), BF16), ((576, 256), F32), ((64, 1024), F32)],
+        [(0, (4, 64, 512), BF16), (0, (1152, 128), F32), (0, (64, 1024), F32)],
         [((576, 1536), BF16), ((192, 1536), BF16), ((256, 1024), BF16)],
-        table, codes, gated, hidden0, delta_up, cot_patch, ext1, ext1_edge, w_ups, w_adj,
+        [table, codes, gated, delta_up, ext1, ext1_edge], [hidden0, cot_patch, w_ups, w_adj],
     )
     (grads_a,) = call(
         finish, "finish",
-        [((576, 256), F32)],
+        [(0, (1152, 128), F32)],
         [((576, 512), BF16), ((256, 2048), BF16), ((576, 5120), BF16), ((192, 5120), BF16)],
-        table, codes, delta_up, low2, high2, back, w_adj, coarse_pre, patch0, w_dns, fine_slope,
-        cot_plane, ext0, ext0_edge,
-    )
-    total = total_over_devices(jnp.concatenate([grads_a, grads_b], axis=1))
+        [table, codes, delta_up, low2, high2, back],
+        [w_adj, coarse_slope, patch0, w_dns, fine_slope, cot_plane, ext0, ext0_edge], late=True,
+    )
+    total = total_over_devices(jnp.concatenate([grads_a, grads_b], axis=0))
     factor = 1.0 / math.sqrt(lax.axis_size(AXES) * 4 * 512)
     outs = call(
         lambda *refs: unfold(factor, *refs), "unfold",
-        [(w_fine.shape, F32), (w_down.shape, F32), (w_coarse.shape, F32), (w_up.shape, F32)], [], total,
+        [(0, w_fine.shape, F32), (0, w_down.shape, F32), (0, w_coarse.shape, F32), (0, w_up.shape, F32)], [], [total],
     )
     return (decoded[None], *outs)
 
 
 def solution(mesh):
+    chips = mesh.devices.shape[0]
+    x = min(4, chips)
+    y = min(4, chips // x)
+    grid = Mesh(mesh.devices.reshape(chips // (x * y), y, x, -1), AXES)
     in_specs = (
-        P("rep", "space", None, None),
-        P("rep", "space", None),
-        P("rep", "space", None, None),
+        P("core", CHIPS, None, None),
+        P("core", CHIPS, None),
+        P("core", CHIPS, None, None),
         P(),
         P(),
         P(),
         P(),
-        P("rep", "space", None, None),
-    )
-    out_specs = (P("rep", "space", None, None), P(), P(), P(), P())
-    return jax.shard_map(shards, mesh=mesh, in_specs=in_specs, out_specs=out_specs, check_vma=False)
+        P("core", CHIPS, None, None),
+    )
+    out_specs = (P("core", CHIPS, None, None), P(), P(), P(), P())
+    return jax.shard_map(shards, mesh=grid, in_specs=in_specs, out_specs=out_specs, check_vma=False)

time: 128 us -> 118 us (0.922)
  blocking collectives: 0 us -> 56.3 us
  starting transfers between devices: 62.9 us -> 21.1 us
  waiting for transfers between devices: 26.9 us -> 2.43 us
  local copies, waits for them, and re-layouts: 19.4 us -> 5.92 us
  Pallas kernels: 16.1 us -> 29.1 us
  other arithmetic: 0.51 us -> 1.89 us
    all_to_all x0 -> x3, blocking collectives: none -> 56.3 us  [dealt(): return lax.all_to_all(x.reshape(count, -1, 128), axes, 0, 0, tiled=True)]
    ppermute x17 -> x8, starting transfers between devices: 62.9 us -> 21.1 us  [the longest x6 15.8 us: passed_along(): return lax.ppermute(block, CHIPS, route)]
    ppermute x17 -> x8, waiting for transfers between devices: 26.9 us -> 2.43 us  [the longest x2 2.42 us: other_core(): return lax.ppermute(x, 'core', [(0, 1), (1, 0)])]
    unnamed x76 -> x24, local copies, waits for them, and re-layouts: 19.4 us -> 5.86 us
    pallas_call x7, Pallas kernels: 14.5 us -> 27.5 us  [call(): pl.pallas_call(body, name=name, out_shape=[jax.ShapeDtypeStruct(shape, ki...]
    convert_element_type x7 -> x4, other arithmetic: 0.16 us -> 1.79 us  [the longest x1 1.36 us: total_over_devices(): x = keep + other_core(send.astype(BF16)).astype(F32)]
  transfers between devices with their start and end apart: 17 -> 8, of which waited for: 12 -> 2; matrix products, arithmetic and copies ran while one was open for 0% -> 0% of each run, Pallas kernels for 5% -> 12%
where the time goes in v2:
time: 118 us
  blocking collectives  56.3 us (48%)
  Pallas kernels  29.1 us (25%)
  starting transfers between devices  21.1 us (18%)
  local copies, waits for them, and re-layouts  5.92 us (5%)
  waiting for transfers between devices  2.43 us (2%)
  other arithmetic  1.89 us (2%)
    all_to_all x3, blocking collectives, dealt(): return lax.all_to_all(x.reshape(count, -1, 128), axes, 0, 0, tiled=True)  56.3 us
    pallas_call x7, Pallas kernels, call(): pl.pallas_call(body, name=name, out_shape=[jax.ShapeDtypeStruct(shape, ki...  27.5 us
    ppermute x6, starting transfers between devices, passed_along(): return lax.ppermute(block, CHIPS, route)  15.8 us
    unnamed x24, local copies, waits for them, and re-layouts  5.86 us
    ppermute x2, starting transfers between devices, other_core(): return lax.ppermute(x, 'core', [(0, 1), (1, 0)])  5.34 us
    ppermute x2, waiting for transfers between devices, other_core(): return lax.ppermute(x, 'core', [(0, 1), (1, 0)])  2.42 us
  transfers between devices with their start and end apart: 8, of which 2 were waited for; matrix products, arithmetic and copies ran while one was open for 0% of the time, Pallas kernels for 12%

profile of v2, /device:TPU:1, one launch (start us, length us, event | category | flops | bytes accessed | tf_op | source)
XLA Modules:
  0.0 117.6 jit_solution(15206255020450320397)
XLA Ops:
  0.6 1.6 %pack_faces.1 = (bf16[144,128]{1,0:T(8,128)(2,1)}, bf16[144,128]{1,0:T(8,128)(2,1)}) custom-call(s32[2,16]{1,0:T(2,128)} %bitcast.27, bf16[4,64,512]{2,1,0:T(8,128)(2,1)} %bitcast.21, bf16[4,64,512]{2,1,0:T(8,128)(2,1)} %bitcast.22), custom_call_target="tpu_custom_call" | custom-call | tf_op jit(solution)/shard_map/pack_faces/pallas_call | solution.py:514
  2.2 3.9 %collective-permute-start = (bf16[144,128]{1,0:T(8,128)(2,1)}, bf16[144,128]{1,0:T(8,128)(2,1)S(1)}, u32[]{:S(2)}, u32[]{:S(2)}) collective-permute-start(bf16[144,128]{1,0:T(8,128)(2,1)} %get-tuple-element.41), channel_id=1, source_target_pairs={{0,2},{2,4},{4,6},{6,8},{8,10},{10,12},{12,14},{14,16},{16,18},{18... | collective-permute-start | bytes 110600 | tf_op jit(solution)/shard_map/ppermute | solution.py:472
  6.2 1.3 %collective-permute-start.1 = (bf16[144,128]{1,0:T(8,128)(2,1)}, bf16[144,128]{1,0:T(8,128)(2,1)S(1)}, u32[]{:S(2)}, u32[]{:S(2)}) collective-permute-start(bf16[144,128]{1,0:T(8,128)(2,1)} %get-tuple-element.42), channel_id=1, source_target_pairs={{2,0},{4,2},{6,4},{8,6},{10,8},{12,10},{14,12},{16,14},{18,16},{20... | collective-permute-start | bytes 110600 | tf_op jit(solution)/shard_map/ppermute | solution.py:472
  7.5 0.0 copy-start
  7.5 0.9 copy-done
  8.4 0.9 copy-done.2
  9.3 0.9 copy-done.5
  10.3 0.8 copy-done.6
  11.1 0.8 copy-done.8
  11.9 0.7 copy-done.9
  12.6 5.9 %fine_inner.1 = (f32[8,64,512]{2,1,0:T(8,128)}, bf16[2,64,256]{2,1,0:T(8,128)(2,1)S(1)}, f32[64,1024]{1,0:T(8,128)}, bf16[8,64,512]{2,1,0:T(8,128)(2,1)}, bf16[8...) custom-call(s32[4,26]{1,0:T(4,128)S(1)} %bitcast.18, ...), custom_call_target="tpu_custom_call" | custom-call | tf_op jit(solution)/shard_map/fine_inner/pallas_call | solution.py:454
  18.6 4.2 %fine_outer.1 = (bf16[8,64,512]{2,1,0:T(8,128)(2,1)}, bf16[512,1024]{1,0:T(8,128)(2,1)}, f32[64,1024]{1,0:T(8,128)}, bf16[64,1024]{1,0:T(8,128)(2,1)S(1)}, f32[2...) custom-call(s32[4,26]{1,0:T(4,128)S(1)} %bitcast.19, ...), custom_call_target="tpu_custom_call" | custom-call | tf_op jit(solution)/shard_map/fine_outer/pallas_call | solution.py:454
  22.7 4.0 %collective-permute-start.2 = (bf16[64,256]{1,0:T(8,128)(2,1)S(1)}, bf16[64,256]{1,0:T(8,128)(2,1)S(1)}, u32[]{:S(2)}, u32[]{:S(2)}) collective-permute-start(bf16[64,256]{1,0:T(8,128)(2,1)S(1)} %get-tuple-element.49), channel_id=1, source_target_pairs={{0,2},{2,4},{4,6},{6,8},{8,10},{10,12},{12,14},{14,16},{16,18},{18... | collective-permute-start | bytes 98312 | tf_op jit(solution)/shard_map/ppermute | solution.py:472
  26.7 1.3 %collective-permute-start.3 = (bf16[64,256]{1,0:T(8,128)(2,1)S(1)}, bf16[64,256]{1,0:T(8,128)(2,1)S(1)}, u32[]{:S(2)}, u32[]{:S(2)}) collective-permute-start(bf16[64,256]{1,0:T(8,128)(2,1)S(1)} %get-tuple-element.50), channel_id=1, source_target_pairs={{2,0},{4,2},{6,4},{8,6},{10,8},{12,10},{14,12},{16,14},{18,16},{20... | collective-permute-start | bytes 98312 | tf_op jit(solution)/shard_map/ppermute | solution.py:472
  28.1 3.6 %coarse_inner.1 = (s32[8,256]{1,0:T(8,128)S(1)}, bf16[64,1024]{1,0:T(8,128)(2,1)S(1)}, f32[64,1024]{1,0:T(8,128)S(1)}, f32[8,64,512]{2,1,0:T(8,128)}, f32[64,1024]{1,0:T(8,128)}) custom-call(s32[4,26]{1,0:T(4,128)S(1)} %bitcast.20, s32[16,2048]{1,0:T(8,128)S(1)} %copy-done, bf16[144,128]{1,0:T(8,128)(2,1)S(1)} %collective-permute-done.refs_2_, ...), custom_call_target="tpu_custom_call" | custom-call | tf_op jit(solution)/shard_map/coarse_inner/pallas_call | solution.py:454
  31.7 0.7 copy-done.7
  32.4 2.0 %coarse_outer.1 = (bf16[64,1024]{1,0:T(8,128)(2,1)S(1)}, bf16[64,1024]{1,0:T(8,128)(2,1)S(1)}, bf16[2,64,256]{2,1,0:T(8,128)(2,1)S(1)}, bf16[64,256]{1,0:T(8,128)(2,1)S(1)}, bf16[64,256]{1,0:T(8,128)(2,1)S(1)}) custom-call(s32[8,256]{1,0:T(8,128)S(1)} %get-tuple-element.48.refs_0_.refs_1_, bf16[64,1024]{1,0:T(8,128)(2,1)S(1)} %get-tuple-element.45.refs_4_.refs_1_, ...), custom_call_target="tpu_custom_call" | custom-call | tf_op jit(solution)/shard_map/coarse_outer/pallas_call | solution.py:454
  34.4 4.0 %collective-permute-start.4 = (bf16[64,256]{1,0:T(8,128)(2,1)S(1)}, bf16[64,256]{1,0:T(8,128)(2,1)S(1)}, u32[]{:S(2)}, u32[]{:S(2)}) collective-permute-start(bf16[64,256]{1,0:T(8,128)(2,1)S(1)} %get-tuple-element.62), channel_id=1, source_target_pairs={{0,2},{2,4},{4,6},{6,8},{8,10},{10,12},{12,14},{14,16},{16,18},{18... | collective-permute-start | bytes 98312 | tf_op jit(solution)/shard_map/ppermute | solution.py:472
  38.4 1.3 %collective-permute-start.5 = (bf16[64,256]{1,0:T(8,128)(2,1)S(1)}, bf16[64,256]{1,0:T(8,128)(2,1)S(1)}, u32[]{:S(2)}, u32[]{:S(2)}) collective-permute-start(bf16[64,256]{1,0:T(8,128)(2,1)S(1)} %get-tuple-element.63), channel_id=1, source_target_pairs={{2,0},{4,2},{6,4},{8,6},{10,8},{12,10},{14,12},{16,14},{18,16},{20... | collective-permute-start | bytes 98312 | tf_op jit(solution)/shard_map/ppermute | solution.py:472
  39.7 4.2 %decode.1 = (bf16[4,64,512]{2,1,0:T(8,128)(2,1)}, f32[1152,128]{1,0:T(8,128)}, f32[64,1024]{1,0:T(8,128)}) custom-call(s32[16,2048]{1,0:T(8,128)S(1)} %copy-done.1, s32[8,256]{1,0:T(8,128)S(1)} %get-tuple-element.48.refs_0_.refs_1_, bf16[64,1024]{1,0:T(8,128)(2,1)S(1)} %get-tuple-element.53.refs_2_, bf16[64,1024]{1,0:T(8,128)(2,1)S(1)} %get-tuple-element.54.refs_3_.refs_2_, ...), custom_call_target="tpu_custom_call" | custom-call | tf_op jit(solution)/shard_map/decode/pallas_call | solution.py:454
  43.9 6.3 %finish.1 = f32[1152,128]{1,0:T(8,128)} custom-call(s32[16,2048]{1,0:T(8,128)S(1)} %copy-done.1, s32[8,256]{1,0:T(8,128)S(1)} %get-tuple-element.48.refs_0_.refs_1_, bf16[64,1024]{1,0:T(8,128)(2,1)S(1)} %get-tuple-element.54.refs_3_.refs_2_, bf16[64,256]{1,0:T(8,128)(2,1)S(1)} %collective-permute-done.4.refs_3_, ...), custom_call_target="tpu_custom_call" | custom-call | tf_op jit(solution)/shard_map/finish/pallas_call | solution.py:454
  50.2 1.4 %fusion.1 = bf16[1152,128]{1,0:T(8,128)(2,1)S(1)} fusion(s32[]{:T(128)S(6)} %select_n.20, f32[1152,128]{1,0:T(8,128)} %finish.1, f32[1152,128]{1,0:T(8,128)S(1)} %copy-done.11), kind=kLoop, calls=%fused_computation.5 | loop fusion | flops 589824 | bytes 1474564 | tf_op jit(solution)/shard_map/convert_element_type | solution.py:500
  51.5 1.3 %collective-permute-start.6 = (bf16[1152,128]{1,0:T(8,128)(2,1)S(1)}, bf16[1152,128]{1,0:T(8,128)(2,1)S(1)}, u32[]{:S(2)}, u32[]{:S(2)}) collective-permute-start(bf16[1152,128]{1,0:T(8,128)(2,1)S(1)} %fusion.1), channel_id=1, source_target_pairs={{0,1},{1,0},{2,3},{3,2},{4,5},{5,4},{6,7},{7,6},{8,9},{9,8},{10,11... | collective-permute-start | bytes 884744 | tf_op jit(solution)/shard_map/ppermute | solution.py:476
  52.9 1.2 %collective-permute-done.6 = bf16[1152,128]{1,0:T(8,128)(2,1)S(1)} collective-permute-done((bf16[1152,128]{1,0:T(8,128)(2,1)S(1)}, bf16[1152,128]{1,0:T(8,128)(2,1)S(1)}, u32[]{:S(2)}, u32[]{:S(2)}) %collective-permute-start.6) | collective-permute-done | bytes 294944 | tf_op jit(solution)/shard_map/ppermute | solution.py:476
  54.1 0.3 fusion.4
  54.4 27.2 %all_to_all.15 = bf16[16,72,128]{2,1,0:T(8,128)(2,1)S(1)} all-to-all(bf16[16,72,128]{2,1,0:T(8,128)(2,1)S(1)} %bitcast.25), channel_id=1, replica_groups=mesh['z'=8,'y'=4,'x'=4,'core'=2] {'y','x'}, dimensions={0} | all-to-all | bytes 589824 | tf_op jit(solution)/shard_map/all_to_all | solution.py:481
  81.7 18.4 %all_to_all.16 = bf16[8,72,128]{2,1,0:T(8,128)(2,1)S(1)} all-to-all(bf16[8,72,128]{2,1,0:T(8,128)(2,1)S(1)} %broadcast_in_dim.10), channel_id=1, replica_groups=mesh['z'=8,'y'=4,'x'=4,'core'=2] {'z'}, dimensions={0} | all-to-all | bytes 294912 | tf_op jit(solution)/shard_map/all_to_all | solution.py:481
  100.2 10.6 %all_to_all.17 = bf16[16,72,128]{2,1,0:T(8,128)(2,1)S(1)} all-to-all(bf16[16,72,128]{2,1,0:T(8,128)(2,1)S(1)} %broadcast_in_dim.11), channel_id=1, replica_groups=mesh['z'=8,'y'=4,'x'=4,'core'=2] {'y','x'}, dimensions={0} | all-to-all | bytes 589824 | tf_op jit(solution)/shard_map/all_to_all | solution.py:481
  110.9 4.0 %collective-permute-start.7 = (bf16[1152,128]{1,0:T(8,128)(2,1)S(1)}, bf16[1152,128]{1,0:T(8,128)(2,1)S(1)}, u32[]{:S(2)}, u32[]{:S(2)}) collective-permute-start(bf16[1152,128]{1,0:T(8,128)(2,1)S(1)} %bitcast.24), channel_id=1, source_target_pairs={{0,1},{1,0},{2,3},{3,2},{4,5},{5,4},{6,7},{7,6},{8,9},{9,8},{10,11... | collective-permute-start | bytes 884744 | tf_op jit(solution)/shard_map/ppermute | solution.py:476
  114.9 1.2 %collective-permute-done.7 = bf16[1152,128]{1,0:T(8,128)(2,1)S(1)} collective-permute-done((bf16[1152,128]{1,0:T(8,128)(2,1)S(1)}, bf16[1152,128]{1,0:T(8,128)(2,1)S(1)}, u32[]{:S(2)}, u32[]{:S(2)}) %collective-permute-start.7) | collective-permute-done | bytes 294944 | tf_op jit(solution)/shard_map/ppermute | solution.py:476
  116.1 0.1 broadcast_select_fusion.1
  116.2 1.4 %unfold.1 = (f32[64,1728]{1,0:T(8,128)}, f32[64,512]{1,0:T(8,128)}, f32[64,1728]{1,0:T(8,128)}, f32[64,512]{1,0:T(8,128)}) custom-call(bf16[2304,128]{1,0:T(8,128)(2,1)S(1)} %pad_maximum_fusion.refs_0_), custom_call_target="tpu_custom_call" | custom-call | tf_op jit(solution)/shard_map/unfold/pallas_call | solution.py:454
  (27 shorter events, 0.2 us)
Async XLA Ops:
  2.2 16.3 %collective-permute-start = (bf16[144,128]{1,0:T(8,128)(2,1)}, bf16[144,128]{1,0:T(8,128)(2,1)S(1)}, u32[]{:S(2)}, u32[]{:S(2)}) collective-permute-start(bf16[144,128]{1,0:T(8,128)(2,1)} %get-tuple-element.41), channel_id=1, source_target_pairs={{0,2},{2,4},{4,6},{6,8},{8,10},{10,12},{12,14},{14,16},{16,18},{18... | collective-permute-start | bytes 110600 | tf_op jit(solution)/shard_map/ppermute | solution.py:472
  6.2 12.4 %collective-permute-start.1 = (bf16[144,128]{1,0:T(8,128)(2,1)}, bf16[144,128]{1,0:T(8,128)(2,1)S(1)}, u32[]{:S(2)}, u32[]{:S(2)}) collective-permute-start(bf16[144,128]{1,0:T(8,128)(2,1)} %get-tuple-element.42), channel_id=1, source_target_pairs={{2,0},{4,2},{6,4},{8,6},{10,8},{12,10},{14,12},{16,14},{18,16},{20... | collective-permute-start | bytes 110600 | tf_op jit(solution)/shard_map/ppermute | solution.py:472
  7.5 0.9 copy-start
  8.4 0.9 copy-start.2
  9.3 0.9 copy-start.5
  10.3 0.8 copy-start.6
  11.1 0.8 copy-start.8
  11.9 0.7 copy-start.9
  18.5 9.5 %copy-start.3 = (bf16[64,1728]{1,0:T(8,128)(2,1)S(1)}, bf16[64,1728]{1,0:T(8,128)(2,1)}, u32[]{:S(2)}) copy-start(bf16[64,1728]{1,0:T(8,128)(2,1)} %refs_6_.3) | copy-start | bytes 663556
  22.7 9.7 %collective-permute-start.2 = (bf16[64,256]{1,0:T(8,128)(2,1)S(1)}, bf16[64,256]{1,0:T(8,128)(2,1)S(1)}, u32[]{:S(2)}, u32[]{:S(2)}) collective-permute-start(bf16[64,256]{1,0:T(8,128)(2,1)S(1)} %get-tuple-element.49), channel_id=1, source_target_pairs={{0,2},{2,4},{4,6},{6,8},{8,10},{10,12},{12,14},{14,16},{16,18},{18... | collective-permute-start | bytes 98312 | tf_op jit(solution)/shard_map/ppermute | solution.py:472
  26.7 5.7 %collective-permute-start.3 = (bf16[64,256]{1,0:T(8,128)(2,1)S(1)}, bf16[64,256]{1,0:T(8,128)(2,1)S(1)}, u32[]{:S(2)}, u32[]{:S(2)}) collective-permute-start(bf16[64,256]{1,0:T(8,128)(2,1)S(1)} %get-tuple-element.50), channel_id=1, source_target_pairs={{2,0},{4,2},{6,4},{8,6},{10,8},{12,10},{14,12},{16,14},{18,16},{20... | collective-permute-start | bytes 98312 | tf_op jit(solution)/shard_map/ppermute | solution.py:472
  28.1 11.6 %copy-start.1 = (s32[16,2048]{1,0:T(8,128)S(1)}, s32[16,2048]{1,0:T(8,128)}, u32[]{:S(2)}) copy-start(s32[16,2048]{1,0:T(8,128)} %constant.14.clone.refs_1_.refs_0_) | copy-start | bytes 393220
  28.1 11.6 %copy-start.4 = (bf16[192,576]{1,0:T(8,128)(2,1)S(1)}, bf16[192,576]{1,0:T(8,128)(2,1)}, u32[]{:S(2)}) copy-start(bf16[192,576]{1,0:T(8,128)(2,1)} %get-tuple-element.60.refs_9_.refs_6_) | copy-start | bytes 663556
  31.7 0.7 copy-start.7
  34.4 9.5 %collective-permute-start.4 = (bf16[64,256]{1,0:T(8,128)(2,1)S(1)}, bf16[64,256]{1,0:T(8,128)(2,1)S(1)}, u32[]{:S(2)}, u32[]{:S(2)}) collective-permute-start(bf16[64,256]{1,0:T(8,128)(2,1)S(1)} %get-tuple-element.62), channel_id=1, source_target_pairs={{0,2},{2,4},{4,6},{6,8},{8,10},{10,12},{12,14},{14,16},{16,18},{18... | collective-permute-start | bytes 98312 | tf_op jit(solution)/shard_map/ppermute | solution.py:472
  38.4 5.5 %collective-permute-start.5 = (bf16[64,256]{1,0:T(8,128)(2,1)S(1)}, bf16[64,256]{1,0:T(8,128)(2,1)S(1)}, u32[]{:S(2)}, u32[]{:S(2)}) collective-permute-start(bf16[64,256]{1,0:T(8,128)(2,1)S(1)} %get-tuple-element.63), channel_id=1, source_target_pairs={{2,0},{4,2},{6,4},{8,6},{10,8},{12,10},{14,12},{16,14},{18,16},{20... | collective-permute-start | bytes 98312 | tf_op jit(solution)/shard_map/ppermute | solution.py:472
  43.9 6.3 %copy-start.11 = (f32[1152,128]{1,0:T(8,128)S(1)}, f32[1152,128]{1,0:T(8,128)}, u32[]{:S(2)}) copy-start(f32[1152,128]{1,0:T(8,128)} %get-tuple-element.72) | copy-start | bytes 1769476
  50.2 3.9 %copy-start.10 = (f32[1152,128]{1,0:T(8,128)S(1)}, f32[1152,128]{1,0:T(8,128)}, u32[]{:S(2)}) copy-start(f32[1152,128]{1,0:T(8,128)} %finish.1) | copy-start | bytes 1769476
  51.5 2.5 %collective-permute-start.6 = (bf16[1152,128]{1,0:T(8,128)(2,1)S(1)}, bf16[1152,128]{1,0:T(8,128)(2,1)S(1)}, u32[]{:S(2)}, u32[]{:S(2)}) collective-permute-start(bf16[1152,128]{1,0:T(8,128)(2,1)S(1)} %fusion.1), channel_id=1, source_target_pairs={{0,1},{1,0},{2,3},{3,2},{4,5},{5,4},{6,7},{7,6},{8,9},{9,8},{10,11... | collective-permute-start | bytes 884744 | tf_op jit(solution)/shard_map/ppermute | solution.py:476
  110.9 5.2 %collective-permute-start.7 = (bf16[1152,128]{1,0:T(8,128)(2,1)S(1)}, bf16[1152,128]{1,0:T(8,128)(2,1)S(1)}, u32[]{:S(2)}, u32[]{:S(2)}) collective-permute-start(bf16[1152,128]{1,0:T(8,128)(2,1)S(1)} %bitcast.24), channel_id=1, source_target_pairs={{0,1},{1,0},{2,3},{3,2},{4,5},{5,4},{6,7},{7,6},{8,9},{9,8},{10,11... | collective-permute-start | bytes 884744 | tf_op jit(solution)/shard_map/ppermute | solution.py:476

commit v3 on v2

--- a/solution.py
+++ b/solution.py
@@ -166,7 +166,7 @@
     return jnp.concatenate([wt[64 * k : 64 * k + 64, :] for k in order], axis=1).astype(BF16)
 
 
-def pack_faces(sends, low_tile, high_tile, to_upper, to_lower):
+def pack_faces(core, sends, low_tile, high_tile, to_upper, to_lower):
     low = low_half((64, 128))
     for p in range(2):
         to_upper[64 * p : 64 * p + 64, :] = merge_high(low, high_tile[2 * p], high_tile[2 * p + 1])
@@ -350,17 +350,14 @@
     put_grads(grads, of_coarse, of_up)
 
 
-def finish(ready, table, codes, delta, from_lower, from_upper, back, w_adj, coarse_slope, patch, w_dns, fine_slope,
-           cot_plane, ext, ext_edge, grads, coarse_taps, spread, taps, stack):
-    ready[0]()
+def finish(core, table, codes, delta, from_lower, from_upper, back, w_adj, coarse_slope, patch, w_dns, fine_slope,
+           cot_plane, ext, ext_edge, grads_b, keep, send, coarse_taps, spread, taps, stack, grads):
     weight = w_adj[...]
     low, _ = coarse_outer_conv(codes, 0, delta[:, 768:], from_lower[...], weight, coarse_taps, 0)
     high, _ = coarse_outer_conv(codes, 1, delta[:, :256], from_upper[...], weight, coarse_taps, 256)
     value = back[...]
     value = jnp.concatenate([value[:, :256] + low, value[:, 256:768], value[:, 768:] + high], axis=1)
-    ready[1]()
     down = (value * coarse_slope[...]).astype(BF16)
-    ready[2]()
     of_down = jnp.concatenate([nt(patch[...], down), jnp.zeros((64, 64), F32)], axis=0)
     chosen = mm(by_rows(down), onehot(table[8:9, :2048], 256)).astype(BF16)
     for x in range(4):
@@ -372,8 +369,6 @@
         for plane in range(10):
             if not 0 <= plane - a < 8:
                 stack[64 * a : 64 * a + 64, 512 * plane : 512 * plane + 512] = jnp.zeros((64, 512), BF16)
-    for wait in ready[3:]:
-        wait()
     for half in range(4):
         raised = mm(w_dns[...], spread[:, 512 * half : 512 * half + 512])
         for i in range(2):
@@ -388,6 +383,17 @@
         put_taps(taps, 512 * x + 512, ext[x], FINE_SHIFTS)
     put_taps(taps, 4608, ext_edge[1], FINE_SHIFTS)
     put_grads(grads, nt(taps[...], stack[...]), of_down)
+    first = core[0] == 0
+
+    @pl.when(first)
+    def _():
+        keep[...] = grads[...]
+        send[...] = grads_b[...].astype(BF16)
+
+    @pl.when(jnp.logical_not(first))
+    def _():
+        keep[...] = grads_b[...]
+        send[...] = grads[...].astype(BF16)
 
 
 def put_grads(grads, wide, narrow):
@@ -395,30 +401,32 @@
     grads[576:1152, :] = jnp.concatenate([wide[:, 128:], narrow], axis=1)
 
 
-def unfold(factor, total, grad_fine, grad_down, grad_coarse, grad_up):
-    for at, wide, narrow in ((0, grad_fine, grad_down), (1152, grad_coarse, grad_up)):
-        both = jnp.concatenate([total[at : at + 576, :], total[at + 576 : at + 1152, :]], axis=1)
+def unfold(factor, core, own, other, grad_fine, grad_down, grad_coarse, grad_up):
+    def spell(half, wide, narrow):
+        both = jnp.concatenate([half[0:576, :], half[576:1152, :]], axis=1)
         turned = (both.astype(F32) * factor).T
         wide[...] = jnp.concatenate([turned[64 * a : 64 * a + 64, :] for a in range(3)], axis=1)
         narrow[...] = turned[192:256, :512]
 
-
-GRANT = 53 * 1024 * 1024
+    first = core[0] == 0
+
+    @pl.when(first)
+    def _():
+        spell(own, grad_fine, grad_down)
+        spell(other, grad_coarse, grad_up)
+
+    @pl.when(jnp.logical_not(first))
+    def _():
+        spell(other, grad_fine, grad_down)
+        spell(own, grad_coarse, grad_up)
+
+
 VMEM_SPEC = pl.BlockSpec(memory_space=pltpu.VMEM)
 SMEM_SPEC = pl.BlockSpec(memory_space=pltpu.SMEM)
 HBM_SPEC = pl.BlockSpec(memory_space=pltpu.HBM)
 
 
-def whole(shape):
-    return pl.BlockSpec(shape, lambda i: (0,) * len(shape))
-
-
-def place(shape, kind):
-    size = math.prod(shape) * jnp.dtype(kind).itemsize
-    return VMEM_SPEC if size <= 64 * 1024 or shape == (1152, 128) else whole(shape)
-
-
-def call(kernel, name, outs, scratch, near, far=(), late=False):
+def call(kernel, name, megabytes, outs, scratch, near, far=(), late=False):
     counts = (len(near), len(far), len(outs), len(scratch), len(far))
     far_outs = [k for k, (away, _, _) in enumerate(outs) if away]
 
@@ -450,19 +458,18 @@
         for copy in leaving:
             copy.wait()
 
-    small = ((4, 26), (2, 16))
+    small = ((4, 26), (1,))
     return pl.pallas_call(
         body,
         name=name,
         out_shape=[jax.ShapeDtypeStruct(shape, kind) for _, shape, kind in outs],
-        grid=(1,),
-        in_specs=[SMEM_SPEC if x.shape in small else place(x.shape, x.dtype) for x in near] + [HBM_SPEC] * len(far),
-        out_specs=[HBM_SPEC if away else place(shape, kind) for away, shape, kind in outs],
+        in_specs=[SMEM_SPEC if x.shape in small else VMEM_SPEC for x in near] + [HBM_SPEC] * len(far),
+        out_specs=[HBM_SPEC if away else VMEM_SPEC for away, _, _ in outs],
         scratch_shapes=[pltpu.VMEM(shape, kind) for shape, kind in scratch]
         + [pltpu.VMEM(x.shape, x.dtype) for x in far]
         + [pltpu.VMEM(outs[k][1], outs[k][2]) for k in far_outs]
         + [pltpu.SemaphoreType.DMA((max(len(far), 1),)), pltpu.SemaphoreType.DMA((max(len(far_outs), 1),))],
-        compiler_params=pltpu.CompilerParams(vmem_limit_bytes=GRANT),
+        compiler_params=pltpu.CompilerParams(vmem_limit_bytes=megabytes * 1024 * 1024),
     )(*near, *far)
 
 
@@ -492,22 +499,17 @@
     return total
 
 
-def total_over_devices(x):
-    core = lax.axis_index("core")
-    half = x.shape[0] // 2
-    keep = lax.dynamic_slice_in_dim(x, core * half, half, 0)
-    send = lax.dynamic_slice_in_dim(x, (1 - core) * half, half, 0)
-    x = keep + other_core(send.astype(BF16)).astype(F32)
+def total_over_devices(keep, send):
+    x = keep + other_core(send).astype(F32)
     x = summed(dealt(x.astype(BF16), ("y", "x")))
     x = summed(told(x.astype(BF16), "z"))
-    x = told(x.astype(BF16), ("y", "x")).reshape(half, 128)
-    other = other_core(x)
-    return jnp.concatenate([jnp.where(core == 0, x, other), jnp.where(core == 0, other, x)], axis=0)
+    return told(x.astype(BF16), ("y", "x")).reshape(keep.shape)
 
 
 def shards(features, neighbours, send_list, w_fine, w_down, w_coarse, w_up, cotangent):
     feat, cot = features[0], cotangent[0]
     near, sends = neighbours[0], send_list[0, 0]
+    core = lax.axis_index("core").astype(I32).reshape(1)
     table = jnp.asarray(TABLE)
     tile = (4, 64, 128)
     face = jax.ShapeDtypeStruct((144, 128), BF16)
@@ -516,22 +518,22 @@
         name="pack_faces",
         grid=(1,),
         out_shape=[face, face],
-        in_specs=[SMEM_SPEC, pl.BlockSpec(tile, lambda i: (0, 0, 0)), pl.BlockSpec(tile, lambda i: (0, 0, 3))],
+        in_specs=[SMEM_SPEC, SMEM_SPEC, pl.BlockSpec(tile, lambda i: (0, 0, 0)), pl.BlockSpec(tile, lambda i: (0, 0, 3))],
         out_specs=[pl.BlockSpec((144, 128), lambda i: (0, 0))] * 2,
         compiler_params=pltpu.CompilerParams(vmem_limit_bytes=60 * 1024 * 1024),
-    )(sends, feat, feat)
+    )(core, sends, feat, feat)
     from_lower, from_upper = passed_along(to_upper, 1), passed_along(to_lower, -1)
 
     fine = (8, 64, 512)
     pre, edges, up_back, ext0, cot_plane, cot_patch, w_adj, w_ups, w_dns = call(
-        fine_inner, "fine_inner",
+        fine_inner, "fine_inner", 8,
         [(0, fine, F32), (0, (2, 64, 256), BF16), (0, (64, 1024), F32), (0, fine, BF16), (0, fine, BF16),
          (0, (512, 1024), BF16), (0, (192, 576), BF16), (0, (128, 256), BF16), (0, (128, 256), BF16)],
         [((576, 4096), BF16)],
-        [near, table, w_fine, w_down, w_coarse], [w_up, feat, cot],
+        [near, table, w_fine, w_down, w_coarse, w_up, feat, cot],
     )
     hidden0, patch0, coarse_pre, hidden1, pre_edge, ext0_edge, to_upper, to_lower = call(
-        fine_outer, "fine_outer",
+        fine_outer, "fine_outer", 4,
         [(0, fine, BF16), (0, (512, 1024), BF16), (0, (64, 1024), F32), (0, (64, 1024), BF16), (0, (2, 64, 512), F32),
          (0, (2, 64, 512), BF16), (0, (64, 256), BF16), (0, (64, 256), BF16)],
         [((576, 1024), BF16)],
@@ -539,36 +541,36 @@
     )
     low1, high1 = passed_along(to_upper, 1), passed_along(to_lower, -1)
     codes, ext1, conv, fine_slope, coarse_slope = call(
-        coarse_inner, "coarse_inner",
+        coarse_inner, "coarse_inner", 4,
         [(0, (8, 256), I32), (0, (64, 1024), BF16), (0, (64, 1024), F32), (0, fine, F32), (0, (64, 1024), F32)],
         [((576, 1024), BF16)],
         [near, table, from_lower, from_upper, hidden1, pre, pre_edge, w_coarse, coarse_pre],
     )
     gated, delta_up, ext1_edge, to_upper, to_lower = call(
-        coarse_outer, "coarse_outer",
+        coarse_outer, "coarse_outer", 3,
         [(0, (64, 1024), BF16), (0, (64, 1024), BF16), (0, (2, 64, 256), BF16), (0, (64, 256), BF16), (0, (64, 256), BF16)],
         [((576, 512), BF16)],
         [codes, hidden1, low1, high1, conv, up_back, w_coarse],
     )
     low2, high2 = passed_along(to_upper, 1), passed_along(to_lower, -1)
     decoded, grads_b, back = call(
-        decode, "decode",
+        decode, "decode", 6,
         [(0, (4, 64, 512), BF16), (0, (1152, 128), F32), (0, (64, 1024), F32)],
         [((576, 1536), BF16), ((192, 1536), BF16), ((256, 1024), BF16)],
-        [table, codes, gated, delta_up, ext1, ext1_edge], [hidden0, cot_patch, w_ups, w_adj],
-    )
-    (grads_a,) = call(
-        finish, "finish",
-        [(0, (1152, 128), F32)],
-        [((576, 512), BF16), ((256, 2048), BF16), ((576, 5120), BF16), ((192, 5120), BF16)],
-        [table, codes, delta_up, low2, high2, back],
-        [w_adj, coarse_slope, patch0, w_dns, fine_slope, cot_plane, ext0, ext0_edge], late=True,
-    )
-    total = total_over_devices(jnp.concatenate([grads_a, grads_b], axis=0))
+        [table, codes, gated, delta_up, ext1, ext1_edge, hidden0, cot_patch, w_ups, w_adj],
+    )
+    keep, send = call(
+        finish, "finish", 12,
+        [(0, (1152, 128), F32), (0, (1152, 128), BF16)],
+        [((576, 512), BF16), ((256, 2048), BF16), ((576, 5120), BF16), ((192, 5120), BF16), ((1152, 128), F32)],
+        [core, table, codes, delta_up, low2, high2, back, w_adj, coarse_slope, patch0, w_dns, fine_slope, cot_plane, ext0,
+         ext0_edge, grads_b],
+    )
+    total = total_over_devices(keep, send)
     factor = 1.0 / math.sqrt(lax.axis_size(AXES) * 4 * 512)
     outs = call(
-        lambda *refs: unfold(factor, *refs), "unfold",
-        [(0, w_fine.shape, F32), (0, w_down.shape, F32), (0, w_coarse.shape, F32), (0, w_up.shape, F32)], [], [total],
+        lambda *refs: unfold(factor, *refs), "unfold", 3,
+        [(0, w_fine.shape, F32), (0, w_down.shape, F32), (0, w_coarse.shape, F32), (0, w_up.shape, F32)], [], [core, total, other_core(total)],
     )
     return (decoded[None], *outs)
 

time: 118 us -> 104 us (0.88)
  Pallas kernels: 29.1 us -> 16.6 us
  waiting for transfers between devices: 2.43 us -> 6.69 us
  local copies, waits for them, and re-layouts: 5.92 us -> 2.91 us
  blocking collectives: 56.3 us -> 54 us
  other arithmetic: 1.89 us -> 0.14 us
  starting transfers between devices: 21.1 us -> 22.6 us
    pallas_call x7, Pallas kernels: 27.5 us -> 15 us  [call(): pl.pallas_call(body, name=name, out_shape=[jax.ShapeDtypeStruct(shape, ki...]
    ppermute x6, waiting for transfers between devices: 0.02 us -> 4.27 us  [passed_along(): return lax.ppermute(block, CHIPS, route)]
    unnamed x24 -> x16, local copies, waits for them, and re-layouts: 5.86 us -> 2.85 us
    ppermute x2, starting transfers between devices: 5.34 us -> 7.63 us  [other_core(): return lax.ppermute(x, 'core', [(0, 1), (1, 0)])]
    all_to_all x3, blocking collectives: 56.3 us -> 54 us  [dealt(): return lax.all_to_all(x.reshape(count, -1, 128), axes, 0, 0, tiled=True)]
    convert_element_type x2 -> x1, other arithmetic: 1.39 us -> 0.03 us  [total_over_devices(): return told(x.astype(BF16), ('y', 'x')).reshape(keep.shape)]
  transfers between devices with their start and end apart: 8 -> 8, of which waited for: 2 -> 4; matrix products, arithmetic and copies ran while one was open for 0% -> 0% of each run, Pallas kernels for 12% -> 7%
where the time goes in v3:
time: 104 us
  blocking collectives  54 us (52%)
  starting transfers between devices  22.6 us (22%)
  Pallas kernels  16.6 us (16%)
  waiting for transfers between devices  6.69 us (6%)
  local copies, waits for them, and re-layouts  2.91 us (3%)
    all_to_all x3, blocking collectives, dealt(): return lax.all_to_all(x.reshape(count, -1, 128), axes, 0, 0, tiled=True)  54 us
    pallas_call x7, Pallas kernels, call(): pl.pallas_call(body, name=name, out_shape=[jax.ShapeDtypeStruct(shape, ki...  15 us
    ppermute x6, starting transfers between devices, passed_along(): return lax.ppermute(block, CHIPS, route)  14.9 us
    ppermute x2, starting transfers between devices, other_core(): return lax.ppermute(x, 'core', [(0, 1), (1, 0)])  7.63 us
    ppermute x6, waiting for transfers between devices, passed_along(): return lax.ppermute(block, CHIPS, route)  4.27 us
    unnamed x16, local copies, waits for them, and re-layouts  2.85 us
    ppermute x2, waiting for transfers between devices, other_core(): return lax.ppermute(x, 'core', [(0, 1), (1, 0)])  2.42 us
  transfers between devices with their start and end apart: 8, of which 4 were waited for; matrix products, arithmetic and copies ran while one was open for 0% of the time, Pallas kernels for 7%

profile of v3, /device:TPU:1, one launch (start us, length us, event | category | flops | bytes accessed | tf_op | source)
XLA Modules:
  0.0 103.8 jit_solution(13457973169042437987)
XLA Ops:
  0.6 0.0 copy-start
  0.7 1.7 %pack_faces.1 = (bf16[144,128]{1,0:T(8,128)(2,1)}, bf16[144,128]{1,0:T(8,128)(2,1)}) custom-call(s32[1]{0:T(128)} %bitcast.1.core.refs_0_, s32[2,16]{1,0:T(2,128)} %bitcast.27, bf16[4,64,512]{2,1,0:T(8,128)(2,1)} %bitcast.17, bf16[4,64,512]{2,1,0:T(8,128)(2,1)} %bitcast.18), custom_call_target="tpu_custom_call" | custom-call | tf_op jit(solution)/shard_map/pack_faces/pallas_call | solution.py:516
  2.3 3.9 %collective-permute-start = (bf16[144,128]{1,0:T(8,128)(2,1)}, bf16[144,128]{1,0:T(8,128)(2,1)S(1)}, u32[]{:S(2)}, u32[]{:S(2)}) collective-permute-start(bf16[144,128]{1,0:T(8,128)(2,1)} %get-tuple-element.43), channel_id=1, source_target_pairs={{0,2},{2,4},{4,6},{6,8},{8,10},{10,12},{12,14},{14,16},{16,18},{18... | collective-permute-start | bytes 110600 | tf_op jit(solution)/shard_map/ppermute | solution.py:479
  6.3 0.0 copy-start.7
  6.3 1.3 %collective-permute-start.1 = (bf16[144,128]{1,0:T(8,128)(2,1)}, bf16[144,128]{1,0:T(8,128)(2,1)S(1)}, u32[]{:S(2)}, u32[]{:S(2)}) collective-permute-start(bf16[144,128]{1,0:T(8,128)(2,1)} %get-tuple-element.44), channel_id=1, source_target_pairs={{2,0},{4,2},{6,4},{8,6},{10,8},{12,10},{14,12},{16,14},{18,16},{20... | collective-permute-start | bytes 110600 | tf_op jit(solution)/shard_map/ppermute | solution.py:479
  7.6 0.0 copy-start.2
  7.7 0.9 copy-done.2
  8.6 0.9 copy-done.3
  9.5 0.9 copy-done.4
  10.5 3.2 %fine_inner.1 = (f32[8,64,512]{2,1,0:T(8,128)S(1)}, bf16[2,64,256]{2,1,0:T(8,128)(2,1)S(1)}, f32[64,1024]{1,0:T(8,128)S(1)}, bf16[8,64,512]{2,1,0:T(8,128)(2,1)S...) custom-call(s32[4,26]{1,0:T(4,128)S(1)} %bitcast.23, ...), custom_call_target="tpu_custom_call" | custom-call | tf_op jit(solution)/shard_map/fine_inner/pallas_call | solution.py:462
  13.7 0.0 collective-permute-done.1.refs_3_
  13.7 2.3 %fine_outer.1 = (bf16[8,64,512]{2,1,0:T(8,128)(2,1)S(1)}, bf16[512,1024]{1,0:T(8,128)(2,1)S(1)}, f32[64,1024]{1,0:T(8,128)S(1)}, bf16[64,1024]{1,0:T(8,128)(2,1)...) custom-call(s32[4,26]{1,0:T(4,128)S(1)} %bitcast.24, ...), custom_call_target="tpu_custom_call" | custom-call | tf_op jit(solution)/shard_map/fine_outer/pallas_call | solution.py:462
  16.0 4.0 %collective-permute-start.2 = (bf16[64,256]{1,0:T(8,128)(2,1)S(1)}, bf16[64,256]{1,0:T(8,128)(2,1)S(1)}, u32[]{:S(2)}, u32[]{:S(2)}) collective-permute-start(bf16[64,256]{1,0:T(8,128)(2,1)S(1)} %get-tuple-element.51), channel_id=1, source_target_pairs={{0,2},{2,4},{4,6},{6,8},{8,10},{10,12},{12,14},{14,16},{16,18},{18... | collective-permute-start | bytes 98312 | tf_op jit(solution)/shard_map/ppermute | solution.py:479
  20.0 1.3 %collective-permute-start.3 = (bf16[64,256]{1,0:T(8,128)(2,1)S(1)}, bf16[64,256]{1,0:T(8,128)(2,1)S(1)}, u32[]{:S(2)}, u32[]{:S(2)}) collective-permute-start(bf16[64,256]{1,0:T(8,128)(2,1)S(1)} %get-tuple-element.52), channel_id=1, source_target_pairs={{2,0},{4,2},{6,4},{8,6},{10,8},{12,10},{14,12},{16,14},{18,16},{20... | collective-permute-start | bytes 98312 | tf_op jit(solution)/shard_map/ppermute | solution.py:479
  21.3 1.9 %coarse_inner.1 = (s32[8,256]{1,0:T(8,128)S(1)}, bf16[64,1024]{1,0:T(8,128)(2,1)S(1)}, f32[64,1024]{1,0:T(8,128)S(1)}, f32[8,64,512]{2,1,0:T(8,128)S(1)}, f32[64,1024]{1,0:T(8,128)S(1)}) custom-call(s32[4,26]{1,0:T(4,128)S(1)} %bitcast.25, s32[16,2048]{1,0:T(8,128)S(1)} %copy-done, bf16[144,128]{1,0:T(8,128)(2,1)S(1)} %collective-permute-done.refs_2_, ...), custom_call_target="tpu_custom_call" | custom-call | tf_op jit(solution)/shard_map/coarse_inner/pallas_call | solution.py:462
  23.2 0.0 collective-permute-done.2.refs_2_
  23.2 1.5 %collective-permute-done.3.refs_3_ = bf16[64,256]{1,0:T(8,128)(2,1)S(1)} collective-permute-done((bf16[64,256]{1,0:T(8,128)(2,1)S(1)}, bf16[64,256]{1,0:T(8,128)(2,1)S(1)}, u32[]{:S(2)}, u32[]{:S(2)}) %collective-permute-start.3) | collective-permute-done | bytes 32800 | tf_op jit(solution)/shard_map/ppermute | solution.py:479
  24.7 0.9 coarse_outer.1
  25.6 3.1 %collective-permute-start.4 = (bf16[64,256]{1,0:T(8,128)(2,1)S(1)}, bf16[64,256]{1,0:T(8,128)(2,1)S(1)}, u32[]{:S(2)}, u32[]{:S(2)}) collective-permute-start(bf16[64,256]{1,0:T(8,128)(2,1)S(1)} %get-tuple-element.64), channel_id=1, source_target_pairs={{0,2},{2,4},{4,6},{6,8},{8,10},{10,12},{12,14},{14,16},{16,18},{18... | collective-permute-start | bytes 98312 | tf_op jit(solution)/shard_map/ppermute | solution.py:479
  28.7 1.3 %collective-permute-start.5 = (bf16[64,256]{1,0:T(8,128)(2,1)S(1)}, bf16[64,256]{1,0:T(8,128)(2,1)S(1)}, u32[]{:S(2)}, u32[]{:S(2)}) collective-permute-start(bf16[64,256]{1,0:T(8,128)(2,1)S(1)} %get-tuple-element.65), channel_id=1, source_target_pairs={{2,0},{4,2},{6,4},{8,6},{10,8},{12,10},{14,12},{16,14},{18,16},{20... | collective-permute-start | bytes 98312 | tf_op jit(solution)/shard_map/ppermute | solution.py:479
  30.0 1.9 %decode.1 = (bf16[4,64,512]{2,1,0:T(8,128)(2,1)}, f32[1152,128]{1,0:T(8,128)S(1)}, f32[64,1024]{1,0:T(8,128)S(1)}) custom-call(s32[16,2048]{1,0:T(8,128)S(1)} %copy-done, s32[8,256]{1,0:T(8,128)S(1)} %get-tuple-element.50.refs_0_.refs_1_.refs_2_, bf16[64,1024]{1,0:T(8,128)(2,1)S(1)} %get-tuple-element.55.refs_2_, ...), custom_call_target="tpu_custom_call" | custom-call | tf_op jit(solution)/shard_map/decode/pallas_call | solution.py:462
  31.9 2.8 %collective-permute-done.5.refs_5_ = bf16[64,256]{1,0:T(8,128)(2,1)S(1)} collective-permute-done((bf16[64,256]{1,0:T(8,128)(2,1)S(1)}, bf16[64,256]{1,0:T(8,128)(2,1)S(1)}, u32[]{:S(2)}, u32[]{:S(2)}) %collective-permute-start.5) | collective-permute-done | bytes 32800 | tf_op jit(solution)/shard_map/ppermute | solution.py:479
  34.7 3.3 %finish.1 = (f32[1152,128]{1,0:T(8,128)S(1)}, bf16[1152,128]{1,0:T(8,128)(2,1)S(1)}) custom-call(s32[1]{0:T(128)} %bitcast.1.core.refs_0_, s32[16,2048]{1,0:T(8,128)S(1)} %copy-done, s32[8,256]{1,0:T(8,128)S(1)} %get-tuple-element.50.refs_0_.refs_1_.refs_2_, bf16[64,1024]{1,0:T(8,128)(2,1)S(1)} %get-tuple-element.56.refs_3_, ...), custom_call_target="tpu_custom_call" | custom-call | tf_op jit(solution)/shard_map/finish/pallas_call | solution.py:462
  38.0 3.6 %collective-permute-start.6 = (bf16[1152,128]{1,0:T(8,128)(2,1)S(1)}, bf16[1152,128]{1,0:T(8,128)(2,1)S(1)}, u32[]{:S(2)}, u32[]{:S(2)}) collective-permute-start(bf16[1152,128]{1,0:T(8,128)(2,1)S(1)} %get-tuple-element.76), channel_id=1, source_target_pairs={{0,1},{1,0},{2,3},{3,2},{4,5},{5,4},{6,7},{7,6},{8,9},{9,8},{10,11... | collective-permute-start | bytes 884744 | tf_op jit(solution)/shard_map/ppermute | solution.py:483
  41.6 1.2 %collective-permute-done.6 = bf16[1152,128]{1,0:T(8,128)(2,1)S(1)} collective-permute-done((bf16[1152,128]{1,0:T(8,128)(2,1)S(1)}, bf16[1152,128]{1,0:T(8,128)(2,1)S(1)}, u32[]{:S(2)}, u32[]{:S(2)}) %collective-permute-start.6) | collective-permute-done | bytes 294944 | tf_op jit(solution)/shard_map/ppermute | solution.py:483
  42.8 0.1 add_convert_fusion
  42.9 25.0 %all_to_all.15 = bf16[16,72,128]{2,1,0:T(8,128)(2,1)S(1)} all-to-all(bf16[16,72,128]{2,1,0:T(8,128)(2,1)S(1)} %bitcast.26), channel_id=1, replica_groups=mesh['z'=8,'y'=4,'x'=4,'core'=2] {'y','x'}, dimensions={0} | all-to-all | bytes 589824 | tf_op jit(solution)/shard_map/all_to_all | solution.py:488
  67.9 18.4 %all_to_all.16 = bf16[8,72,128]{2,1,0:T(8,128)(2,1)S(1)} all-to-all(bf16[8,72,128]{2,1,0:T(8,128)(2,1)S(1)} %broadcast_in_dim.10), channel_id=1, replica_groups=mesh['z'=8,'y'=4,'x'=4,'core'=2] {'z'}, dimensions={0} | all-to-all | bytes 294912 | tf_op jit(solution)/shard_map/all_to_all | solution.py:488
  86.4 10.6 %all_to_all.17 = bf16[16,72,128]{2,1,0:T(8,128)(2,1)S(1)} all-to-all(bf16[16,72,128]{2,1,0:T(8,128)(2,1)S(1)} %broadcast_in_dim.11), channel_id=1, replica_groups=mesh['z'=8,'y'=4,'x'=4,'core'=2] {'y','x'}, dimensions={0} | all-to-all | bytes 589824 | tf_op jit(solution)/shard_map/all_to_all | solution.py:488
  97.1 4.0 %collective-permute-start.7 = (bf16[1152,128]{1,0:T(8,128)(2,1)S(1)}, bf16[1152,128]{1,0:T(8,128)(2,1)S(1)}, u32[]{:S(2)}, u32[]{:S(2)}) collective-permute-start(bf16[1152,128]{1,0:T(8,128)(2,1)S(1)} %bitcast.20), channel_id=1, source_target_pairs={{0,1},{1,0},{2,3},{3,2},{4,5},{5,4},{6,7},{7,6},{8,9},{9,8},{10,11... | collective-permute-start | bytes 884744 | tf_op jit(solution)/shard_map/ppermute | solution.py:483
  101.1 1.2 %collective-permute-done.7.refs_2_ = bf16[1152,128]{1,0:T(8,128)(2,1)S(1)} collective-permute-done((bf16[1152,128]{1,0:T(8,128)(2,1)S(1)}, bf16[1152,128]{1,0:T(8,128)(2,1)S(1)}, u32[]{:S(2)}, u32[]{:S(2)}) %collective-permute-start.7) | collective-permute-done | bytes 294944 | tf_op jit(solution)/shard_map/ppermute | solution.py:483
  102.3 1.5 %unfold.1 = (f32[64,1728]{1,0:T(8,128)}, f32[64,512]{1,0:T(8,128)}, f32[64,1728]{1,0:T(8,128)}, f32[64,512]{1,0:T(8,128)}) custom-call(s32[1]{0:T(128)} %bitcast.1.core.refs_0_, bf16[1152,128]{1,0:T(8,128)(2,1)S(1)} %bitcast.21, bf16[1152,128]{1,0:T(8,128)(2,1)S(1)} %collective-permute-done.7.refs_2_), custom_call_target="tpu_custom_call" | custom-call | tf_op jit(solution)/shard_map/unfold/pallas_call | solution.py:462
  (16 shorter events, 0.2 us)
Async XLA Ops:
  0.6 7.0 %copy-start = (s32[16,2048]{1,0:T(8,128)S(1)}, s32[16,2048]{1,0:T(8,128)}, u32[]{:S(2)}) copy-start(s32[16,2048]{1,0:T(8,128)} %constant.6.clone.refs_1_.refs_0_) | copy-start | bytes 393220
  0.6 7.0 %copy-start.1 = (bf16[1,4,64,512]{3,2,1,0:T(8,128)(2,1)S(1)}, bf16[1,4,64,512]{3,2,1,0:T(8,128)(2,1)}, u32[]{:S(2)}) copy-start(bf16[1,4,64,512]{3,2,1,0:T(8,128)(2,1)} %param.9) | copy-start | bytes 786436
  0.7 7.0 %copy-start.5 = (bf16[64,512]{1,0:T(8,128)(2,1)S(1)}, bf16[64,512]{1,0:T(8,128)(2,1)}, u32[]{:S(2)}) copy-start(bf16[64,512]{1,0:T(8,128)(2,1)} %refs_7_.2) | copy-start | bytes 196612
  0.7 7.0 %copy-start.6 = (bf16[64,512]{1,0:T(8,128)(2,1)S(1)}, bf16[64,512]{1,0:T(8,128)(2,1)}, u32[]{:S(2)}) copy-start(bf16[64,512]{1,0:T(8,128)(2,1)} %refs_5_.1) | copy-start | bytes 196612
  2.3 11.3 %collective-permute-start = (bf16[144,128]{1,0:T(8,128)(2,1)}, bf16[144,128]{1,0:T(8,128)(2,1)S(1)}, u32[]{:S(2)}, u32[]{:S(2)}) collective-permute-start(bf16[144,128]{1,0:T(8,128)(2,1)} %get-tuple-element.43), channel_id=1, source_target_pairs={{0,2},{2,4},{4,6},{6,8},{8,10},{10,12},{12,14},{14,16},{16,18},{18... | collective-permute-start | bytes 110600 | tf_op jit(solution)/shard_map/ppermute | solution.py:479
  6.3 1.4 %copy-start.7 = (s32[1,4,26]{2,1,0:T(4,128)S(1)}, s32[1,4,26]{2,1,0:T(4,128)}, u32[]{:S(2)}) copy-start(s32[1,4,26]{2,1,0:T(4,128)} %param.10) | copy-start | bytes 1252
  6.3 7.4 %collective-permute-start.1 = (bf16[144,128]{1,0:T(8,128)(2,1)}, bf16[144,128]{1,0:T(8,128)(2,1)S(1)}, u32[]{:S(2)}, u32[]{:S(2)}) collective-permute-start(bf16[144,128]{1,0:T(8,128)(2,1)} %get-tuple-element.44), channel_id=1, source_target_pairs={{2,0},{4,2},{6,4},{8,6},{10,8},{12,10},{14,12},{16,14},{18,16},{20... | collective-permute-start | bytes 110600 | tf_op jit(solution)/shard_map/ppermute | solution.py:479
  7.6 0.9 copy-start.2
  8.6 0.9 copy-start.3
  9.5 0.9 copy-start.4
  16.0 7.2 %collective-permute-start.2 = (bf16[64,256]{1,0:T(8,128)(2,1)S(1)}, bf16[64,256]{1,0:T(8,128)(2,1)S(1)}, u32[]{:S(2)}, u32[]{:S(2)}) collective-permute-start(bf16[64,256]{1,0:T(8,128)(2,1)S(1)} %get-tuple-element.51), channel_id=1, source_target_pairs={{0,2},{2,4},{4,6},{6,8},{8,10},{10,12},{12,14},{14,16},{16,18},{18... | collective-permute-start | bytes 98312 | tf_op jit(solution)/shard_map/ppermute | solution.py:479
  20.0 4.7 %collective-permute-start.3 = (bf16[64,256]{1,0:T(8,128)(2,1)S(1)}, bf16[64,256]{1,0:T(8,128)(2,1)S(1)}, u32[]{:S(2)}, u32[]{:S(2)}) collective-permute-start(bf16[64,256]{1,0:T(8,128)(2,1)S(1)} %get-tuple-element.52), channel_id=1, source_target_pairs={{2,0},{4,2},{6,4},{8,6},{10,8},{12,10},{14,12},{16,14},{18,16},{20... | collective-permute-start | bytes 98312 | tf_op jit(solution)/shard_map/ppermute | solution.py:479
  25.6 6.3 %collective-permute-start.4 = (bf16[64,256]{1,0:T(8,128)(2,1)S(1)}, bf16[64,256]{1,0:T(8,128)(2,1)S(1)}, u32[]{:S(2)}, u32[]{:S(2)}) collective-permute-start(bf16[64,256]{1,0:T(8,128)(2,1)S(1)} %get-tuple-element.64), channel_id=1, source_target_pairs={{0,2},{2,4},{4,6},{6,8},{8,10},{10,12},{12,14},{14,16},{16,18},{18... | collective-permute-start | bytes 98312 | tf_op jit(solution)/shard_map/ppermute | solution.py:479
  28.7 6.0 %collective-permute-start.5 = (bf16[64,256]{1,0:T(8,128)(2,1)S(1)}, bf16[64,256]{1,0:T(8,128)(2,1)S(1)}, u32[]{:S(2)}, u32[]{:S(2)}) collective-permute-start(bf16[64,256]{1,0:T(8,128)(2,1)S(1)} %get-tuple-element.65), channel_id=1, source_target_pairs={{2,0},{4,2},{6,4},{8,6},{10,8},{12,10},{14,12},{16,14},{18,16},{20... | collective-permute-start | bytes 98312 | tf_op jit(solution)/shard_map/ppermute | solution.py:479
  38.0 4.8 %collective-permute-start.6 = (bf16[1152,128]{1,0:T(8,128)(2,1)S(1)}, bf16[1152,128]{1,0:T(8,128)(2,1)S(1)}, u32[]{:S(2)}, u32[]{:S(2)}) collective-permute-start(bf16[1152,128]{1,0:T(8,128)(2,1)S(1)} %get-tuple-element.76), channel_id=1, source_target_pairs={{0,1},{1,0},{2,3},{3,2},{4,5},{5,4},{6,7},{7,6},{8,9},{9,8},{10,11... | collective-permute-start | bytes 884744 | tf_op jit(solution)/shard_map/ppermute | solution.py:483
  97.1 5.2 %collective-permute-start.7 = (bf16[1152,128]{1,0:T(8,128)(2,1)S(1)}, bf16[1152,128]{1,0:T(8,128)(2,1)S(1)}, u32[]{:S(2)}, u32[]{:S(2)}) collective-permute-start(bf16[1152,128]{1,0:T(8,128)(2,1)S(1)} %bitcast.20), channel_id=1, source_target_pairs={{0,1},{1,0},{2,3},{3,2},{4,5},{5,4},{6,7},{7,6},{8,9},{9,8},{10,11... | collective-permute-start | bytes 884744 | tf_op jit(solution)/shard_map/ppermute | solution.py:483

commit v4 on v3

--- a/solution.py
+++ b/solution.py
@@ -51,6 +51,11 @@
                 hit = own & (y % 2 == j) & (z % 2 == l)
                 at = (2 * j + l) * 512 + 128 * b
                 table[8, at : at + 128] = np.where(hit, 64 * b + 6 * (y // 2 + 1) + z // 2 + 1, -1)
+    real = np.flatnonzero(cown)
+    for half in range(2):
+        for b in range(4):
+            table[9, 64 * half + 16 * b : 64 * half + 16 * b + 16] = 256 * half + 64 * b + real
+            table[10, 256 * half + 64 * b + real] = 64 * half + 16 * b + np.arange(16)
     for b in range(2):
         table[6, 64 * b : 64 * b + 64] = 128 * b + 10 * (w // 8 + 1) + w % 8 + 1
     return table
@@ -164,6 +169,13 @@
 def transposed_blocks(w, order):
     wt = w.astype(F32).T
     return jnp.concatenate([wt[64 * k : 64 * k + 64, :] for k in order], axis=1).astype(BF16)
+
+
+def slot_of(sends, side, block):
+    slot = jnp.int32(-1)
+    for s in range(16):
+        slot = jnp.where(sends[side, s] == block, s, slot)
+    return slot
 
 
 def pack_faces(core, sends, low_tile, high_tile, to_upper, to_lower):
@@ -175,10 +187,7 @@
     for side, out in ((0, to_upper), (1, to_lower)):
         slots = jnp.full((16, 128), -1, I32)
         for j in range(4):
-            slot = jnp.int32(-1)
-            for s in range(16):
-                slot = jnp.where(sends[side, s] == j, s, slot)
-            slots = jnp.where(rows == j, slot, slots)
+            slots = jnp.where(rows == j, slot_of(sends, side, j), slots)
         out[128:144, :] = slots.astype(F32).astype(BF16)
 
 
@@ -227,7 +236,16 @@
             dst[at : at + 64, lane : lane + 128] = selected[64 * x : 64 * x + 64, 128 * jl : 128 * jl + 128]
 
 
-def fine_outer(neighbours, table, from_lower, from_upper, edges, pre, w_fine, w_down,
+def boundary(table, hidden1, up_back, edge, inner):
+    exact = up_back[:, 256 * edge : 256 * edge + 256]
+    high = exact.astype(BF16)
+    low = (exact - high.astype(F32)).astype(BF16)
+    top = jnp.concatenate([hidden1[:, 256 * p : 256 * p + 256] for p in (edge, inner)], axis=1)
+    both = jnp.concatenate([top, jnp.concatenate([high, low], axis=1)], axis=0)
+    return mm(both, onehot(table[9:10, :128], 512)).astype(BF16)
+
+
+def fine_outer(neighbours, table, from_lower, from_upper, edges, pre, w_fine, w_down, up_back,
                hidden, patch, coarse_pre, hidden1, pre_edge, ext_edge, to_upper, to_lower, taps):
     cells = table[1:2, :128]
     weight = tap_rows(w_fine)
@@ -251,7 +269,9 @@
     coarse_pre[...] = value
     value = silu(value).astype(BF16)
     hidden1[...] = value
-    to_upper[...], to_lower[...] = value[:, 768:], value[:, :256]
+    exact = up_back[...]
+    to_upper[...] = boundary(table, value, exact, 3, 2)
+    to_lower[...] = boundary(table, value, exact, 0, 1)
 
 
 def by_rows(v):
@@ -284,7 +304,26 @@
     return mm(weight[128 * side : 128 * side + 64], taps[:, at : at + 256]), plane
 
 
-def coarse_inner(neighbours, table, from_lower, from_upper, hidden1, pre, pre_edge, w_coarse, coarse_pre,
+def peer_codes(table, slots, own_slots):
+    direction, cells = table[2:3, :128], table[3:4, :128]
+    low = low_half((1, 128))
+    down = jnp.where(direction >= 6, 1, jnp.where(direction >= 3, 0, -1))
+    across = direction - 3 * (down + 1) - 1
+    codes = ([], [])
+    for pair in range(2):
+        place = jnp.where(low, slots[2 * pair : 2 * pair + 1], slots[2 * pair + 1 : 2 * pair + 2])
+        y, z = (place >> 2) + down, (place & 3) + across
+        inside = (direction >= 0) & (y >= 0) & (y < 4) & (z >= 0) & (z < 4)
+        wanted = jnp.where(inside, y * 4 + z, -2)
+        for found, candidates in zip(codes, ([slots[j : j + 1] for j in range(4)], own_slots)):
+            code = jnp.full((1, 128), -1, I32)
+            for j in range(4):
+                code = jnp.where(wanted == candidates[j], 64 * j + cells, code)
+            found.append(code)
+    return [jnp.concatenate(code, axis=1) for code in codes]
+
+
+def coarse_inner(neighbours, sends, table, from_lower, from_upper, hidden1, pre, pre_edge, w_coarse, coarse_pre,
                  codes, ext, conv, fine_slope, coarse_slope, taps):
     coarse_slope[...] = slope(coarse_pre[...])
     cells = table[3:4, :128]
@@ -292,9 +331,12 @@
         slots = arrived_slots(payload)
         code = [edge_code(v, cells, base, slots) for v in coarse_slots(neighbours, table, a)]
         codes[row : row + 1, :] = jnp.concatenate(code, axis=1)
+        theirs, ours = peer_codes(table, slots, [slot_of(sends, 1 - row, m) for m in range(4)])
+        codes[3 + row : 4 + row, :] = theirs
+        codes[5 + row : 6 + row, :] = ours
     code = [local_code(v, cells) for v in coarse_slots(neighbours, table, 1)]
     codes[2:3, :] = jnp.concatenate(code, axis=1)
-    codes[3:8, :] = jnp.full((5, 256), -1, I32)
+    codes[7:8, :] = jnp.full((1, 256), -1, I32)
     select = onehot(codes[2:3, :], 256)
     conv[...] = coarse_inner_conv(hidden1[...], select, tap_rows(w_coarse), taps, ext)
     for x in range(8):
@@ -302,17 +344,32 @@
         fine_slope[x] = slope(value)
 
 
-def coarse_outer(codes, hidden1, from_lower, from_upper, conv, up_back, w_coarse,
-                 gated, delta, ext_edge, to_upper, to_lower, taps):
+def coarse_outer(codes, table, hidden1, from_lower, from_upper, conv, up_back, w_coarse,
+                 gated, delta, ext_edge, delta_lower, delta_upper, taps, peer_taps):
     weight = tap_rows(w_coarse)
-    low, ext_edge[0] = coarse_outer_conv(codes, 0, hidden1[:, 768:], from_lower[...], weight, taps, 0)
-    high, ext_edge[1] = coarse_outer_conv(codes, 1, hidden1[:, :256], from_upper[...], weight, taps, 256)
+    spread = onehot(table[10:11, :512], 128)
+    edge = []
+    for side, payload, own, result in (
+        (0, from_lower, hidden1[:, 768:], delta_lower),
+        (1, from_upper, hidden1[:, :256], delta_upper),
+    ):
+        full = mm(payload[...], spread)
+        top = full[:64].astype(BF16)
+        part, ext_edge[side] = coarse_outer_conv(codes, side, own, top[:, :256], weight, taps, 256 * side)
+        edge.append(part)
+        select = onehot(codes[3 + side : 4 + side, :], 256)
+        rows = mm(jnp.concatenate([top[:, :256], top[:, 256:]], axis=0), select).astype(BF16)
+        facing = hidden1[:, :256] if side == 0 else hidden1[:, 768:]
+        beyond = mm(facing, onehot(codes[5 + side : 6 + side, :], 256)).astype(BF16)
+        order = (rows[64:], rows[:64], beyond) if side == 0 else (beyond, rows[:64], rows[64:])
+        for a, plane in enumerate(order):
+            put_taps(peer_taps.at[576 * a : 576 * a + 576], 256 * side, plane, COARSE_SHIFTS)
+        value = mm(w_coarse[...], peer_taps[:, 256 * side : 256 * side + 256])
+        result[...] = ((full[64:, :256] + full[64:, 256:]) * slope(value)).astype(BF16)
     value = conv[...]
-    value = jnp.concatenate([value[:, :256] + low, value[:, 256:768], value[:, 768:] + high], axis=1)
+    value = jnp.concatenate([value[:, :256] + edge[0], value[:, 256:768], value[:, 768:] + edge[1]], axis=1)
     gated[...] = silu(value).astype(BF16)
-    value = (up_back[...] * slope(value)).astype(BF16)
-    delta[...] = value
-    to_upper[...], to_lower[...] = value[:, 768:], value[:, :256]
+    delta[...] = (up_back[...] * slope(value)).astype(BF16)
 
 
 def decode(table, codes, gated, delta, ext, ext_edge, hidden, cot_patch, w_ups, w_adj,
@@ -458,7 +515,7 @@
         for copy in leaving:
             copy.wait()
 
-    small = ((4, 26), (1,))
+    small = ((4, 26), (2, 16), (1,))
     return pl.pallas_call(
         body,
         name=name,
@@ -535,24 +592,23 @@
     hidden0, patch0, coarse_pre, hidden1, pre_edge, ext0_edge, to_upper, to_lower = call(
         fine_outer, "fine_outer", 4,
         [(0, fine, BF16), (0, (512, 1024), BF16), (0, (64, 1024), F32), (0, (64, 1024), BF16), (0, (2, 64, 512), F32),
-         (0, (2, 64, 512), BF16), (0, (64, 256), BF16), (0, (64, 256), BF16)],
+         (0, (2, 64, 512), BF16), (0, (128, 128), BF16), (0, (128, 128), BF16)],
         [((576, 1024), BF16)],
-        [near, table, from_lower, from_upper, edges, pre, w_fine, w_down],
+        [near, table, from_lower, from_upper, edges, pre, w_fine, w_down, up_back],
     )
     low1, high1 = passed_along(to_upper, 1), passed_along(to_lower, -1)
     codes, ext1, conv, fine_slope, coarse_slope = call(
         coarse_inner, "coarse_inner", 4,
         [(0, (8, 256), I32), (0, (64, 1024), BF16), (0, (64, 1024), F32), (0, fine, F32), (0, (64, 1024), F32)],
         [((576, 1024), BF16)],
-        [near, table, from_lower, from_upper, hidden1, pre, pre_edge, w_coarse, coarse_pre],
-    )
-    gated, delta_up, ext1_edge, to_upper, to_lower = call(
-        coarse_outer, "coarse_outer", 3,
+        [near, sends, table, from_lower, from_upper, hidden1, pre, pre_edge, w_coarse, coarse_pre],
+    )
+    gated, delta_up, ext1_edge, low2, high2 = call(
+        coarse_outer, "coarse_outer", 5,
         [(0, (64, 1024), BF16), (0, (64, 1024), BF16), (0, (2, 64, 256), BF16), (0, (64, 256), BF16), (0, (64, 256), BF16)],
-        [((576, 512), BF16)],
-        [codes, hidden1, low1, high1, conv, up_back, w_coarse],
-    )
-    low2, high2 = passed_along(to_upper, 1), passed_along(to_lower, -1)
+        [((576, 512), BF16), ((1728, 512), BF16)],
+        [codes, table, hidden1, low1, high1, conv, up_back, w_coarse],
+    )
     decoded, grads_b, back = call(
         decode, "decode", 6,
         [(0, (4, 64, 512), BF16), (0, (1152, 128), F32), (0, (64, 1024), F32)],

time: 104 us -> 93.9 us (0.903)
  starting transfers between devices: 22.6 us -> 17.2 us
  waiting for transfers between devices: 6.69 us -> 3.19 us
  blocking collectives: 54 us -> 50.8 us
  Pallas kernels: 16.6 us -> 17.7 us
    ppermute x6 -> x4, starting transfers between devices: 14.9 us -> 10.5 us  [passed_along(): return lax.ppermute(block, CHIPS, route)]
    ppermute x6 -> x4, waiting for transfers between devices: 4.27 us -> 0.77 us  [passed_along(): return lax.ppermute(block, CHIPS, route)]
    all_to_all x3, blocking collectives: 54 us -> 50.8 us  [dealt(): return lax.all_to_all(x.reshape(count, -1, 128), axes, 0, 0, tiled=True)]
    pallas_call x7, Pallas kernels: 15 us -> 16 us  [call(): pl.pallas_call(body, name=name, out_shape=[jax.ShapeDtypeStruct(shape, ki...]
    unnamed x16 -> x18, local copies, waits for them, and re-layouts: 2.85 us -> 3.52 us
  transfers between devices with their start and end apart: 8 -> 6, of which waited for: 4 -> 3; matrix products, arithmetic and copies ran while one was open for 0% -> 0% of each run, Pallas kernels for 7% -> 5%
where the time goes in v4:
time: 93.9 us; the launch traced here: 93.5 us
  blocking collectives  50.8 us (54%)
  Pallas kernels  17.7 us (19%)
  starting transfers between devices  17.2 us (18%)
  local copies, waits for them, and re-layouts  3.58 us (4%)
  waiting for transfers between devices  3.19 us (3%)
    all_to_all x3, blocking collectives, dealt(): return lax.all_to_all(x.reshape(count, -1, 128), axes, 0, 0, tiled=True)  50.8 us
    pallas_call x7, Pallas kernels, call(): pl.pallas_call(body, name=name, out_shape=[jax.ShapeDtypeStruct(shape, ki...  16 us
    ppermute x4, starting transfers between devices, passed_along(): return lax.ppermute(block, CHIPS, route)  10.5 us
    ppermute x2, starting transfers between devices, other_core(): return lax.ppermute(x, 'core', [(0, 1), (1, 0)])  6.75 us
    unnamed x18, local copies, waits for them, and re-layouts  3.52 us
    ppermute x2, waiting for transfers between devices, other_core(): return lax.ppermute(x, 'core', [(0, 1), (1, 0)])  2.42 us
  transfers between devices with their start and end apart: 6, of which 3 were waited for; matrix products, arithmetic and copies ran while one was open for 0% of the time, Pallas kernels for 5%

profile of v4, /device:TPU:1, one launch (start us, length us, event | category | flops | bytes accessed | tf_op | source)
XLA Modules:
  0.0 93.5 jit_solution(2612141297516465562)
XLA Ops:
  0.6 0.0 copy-start
  0.7 1.7 %pack_faces.1 = (bf16[144,128]{1,0:T(8,128)(2,1)}, bf16[144,128]{1,0:T(8,128)(2,1)}) custom-call(s32[1]{0:T(128)} %bitcast.2.core.refs_0_, s32[2,16]{1,0:T(2,128)} %bitcast.26, bf16[4,64,512]{2,1,0:T(8,128)(2,1)} %bitcast.17, bf16[4,64,512]{2,1,0:T(8,128)(2,1)} %bitcast.18), custom_call_target="tpu_custom_call" | custom-call | tf_op jit(solution)/shard_map/pack_faces/pallas_call | solution.py:573
  2.3 3.9 %collective-permute-start = (bf16[144,128]{1,0:T(8,128)(2,1)}, bf16[144,128]{1,0:T(8,128)(2,1)S(1)}, u32[]{:S(2)}, u32[]{:S(2)}) collective-permute-start(bf16[144,128]{1,0:T(8,128)(2,1)} %get-tuple-element.43), channel_id=1, source_target_pairs={{0,2},{2,4},{4,6},{6,8},{8,10},{10,12},{12,14},{14,16},{16,18},{18... | collective-permute-start | bytes 110600 | tf_op jit(solution)/shard_map/ppermute | solution.py:536
  6.3 0.0 copy-start.7
  6.3 1.3 %collective-permute-start.1 = (bf16[144,128]{1,0:T(8,128)(2,1)}, bf16[144,128]{1,0:T(8,128)(2,1)S(1)}, u32[]{:S(2)}, u32[]{:S(2)}) collective-permute-start(bf16[144,128]{1,0:T(8,128)(2,1)} %get-tuple-element.44), channel_id=1, source_target_pairs={{2,0},{4,2},{6,4},{8,6},{10,8},{12,10},{14,12},{16,14},{18,16},{20... | collective-permute-start | bytes 110600 | tf_op jit(solution)/shard_map/ppermute | solution.py:536
  7.6 0.0 copy-start.2
  7.6 0.9 copy-done.2
  8.6 0.9 %copy-done.3 = bf16[64,1728]{1,0:T(8,128)(2,1)S(1)} copy-done((bf16[64,1728]{1,0:T(8,128)(2,1)S(1)}, bf16[64,1728]{1,0:T(8,128)(2,1)}, u32[]{:S(2)}) %copy-start.3) | copy-done | bytes 221208
  9.5 0.9 %copy-done.4 = bf16[1,4,64,512]{3,2,1,0:T(8,128)(2,1)S(1)} copy-done((bf16[1,4,64,512]{3,2,1,0:T(8,128)(2,1)S(1)}, bf16[1,4,64,512]{3,2,1,0:T(8,128)(2,1)}, u32[]{:S(2)}) %copy-start.4) | copy-done | bytes 262168
  10.5 3.2 %fine_inner.1 = (f32[8,64,512]{2,1,0:T(8,128)S(1)}, bf16[2,64,256]{2,1,0:T(8,128)(2,1)S(1)}, f32[64,1024]{1,0:T(8,128)S(1)}, bf16[8,64,512]{2,1,0:T(8,128)(2,1)S...) custom-call(s32[4,26]{1,0:T(4,128)S(1)} %bitcast.23, ...), custom_call_target="tpu_custom_call" | custom-call | tf_op jit(solution)/shard_map/fine_inner/pallas_call | solution.py:519
  13.7 0.0 collective-permute-done.refs_2_.refs_3_
  13.7 0.0 collective-permute-done.1.refs_3_.refs_4_
  13.7 2.5 %fine_outer.1 = (bf16[8,64,512]{2,1,0:T(8,128)(2,1)S(1)}, bf16[512,1024]{1,0:T(8,128)(2,1)S(1)}, f32[64,1024]{1,0:T(8,128)S(1)}, bf16[64,1024]{1,0:T(8,128)(2,1)...) custom-call(s32[4,26]{1,0:T(4,128)S(1)} %bitcast.24, ...), custom_call_target="tpu_custom_call" | custom-call | tf_op jit(solution)/shard_map/fine_outer/pallas_call | solution.py:519
  16.2 4.0 %collective-permute-start.2 = (bf16[128,128]{1,0:T(8,128)(2,1)S(1)}, bf16[128,128]{1,0:T(8,128)(2,1)S(1)}, u32[]{:S(2)}, u32[]{:S(2)}) collective-permute-start(bf16[128,128]{1,0:T(8,128)(2,1)S(1)} %get-tuple-element.52), channel_id=1, source_target_pairs={{0,2},{2,4},{4,6},{6,8},{8,10},{10,12},{12,14},{14,16},{16,18},{18... | collective-permute-start | bytes 98312 | tf_op jit(solution)/shard_map/ppermute | solution.py:536
  20.2 1.3 %collective-permute-start.3 = (bf16[128,128]{1,0:T(8,128)(2,1)S(1)}, bf16[128,128]{1,0:T(8,128)(2,1)S(1)}, u32[]{:S(2)}, u32[]{:S(2)}) collective-permute-start(bf16[128,128]{1,0:T(8,128)(2,1)S(1)} %get-tuple-element.53), channel_id=1, source_target_pairs={{2,0},{4,2},{6,4},{8,6},{10,8},{12,10},{14,12},{16,14},{18,16},{20... | collective-permute-start | bytes 98312 | tf_op jit(solution)/shard_map/ppermute | solution.py:536
  21.5 0.0 copy-start.8
  21.5 0.7 copy-done.8
  22.2 1.9 %coarse_inner.1 = (s32[8,256]{1,0:T(8,128)S(1)}, bf16[64,1024]{1,0:T(8,128)(2,1)S(1)}, f32[64,1024]{1,0:T(8,128)S(1)}, f32[8,64,512]{2,1,0:T(8,128)S(1)}, f32[64,1024]{1,0:T(8,128)S(1)}) custom-call(s32[4,26]{1,0:T(4,128)S(1)} %bitcast.25, s32[2,16]{1,0:T(2,128)S(1)} %bitcast.27, s32[16,2048]{1,0:T(8,128)S(1)} %copy-done, ...), custom_call_target="tpu_custom_call" | custom-call | tf_op jit(solution)/shard_map/coarse_inner/pallas_call | solution.py:519
  24.1 0.0 collective-permute-done.2.refs_3_
  24.1 0.8 collective-permute-done.3.refs_4_
  24.9 1.7 %coarse_outer.1 = (bf16[64,1024]{1,0:T(8,128)(2,1)S(1)}, bf16[64,1024]{1,0:T(8,128)(2,1)S(1)}, bf16[2,64,256]{2,1,0:T(8,128)(2,1)S(1)}, bf16[64,256]{1,0:T(8,128)(2,1)S(1)}, bf16[64,256]{1,0:T(8,128)(2,1)S(1)}) custom-call(s32[8,256]{1,0:T(8,128)S(1)} %get-tuple-element.51.refs_0_.refs_1_.refs_2_, s32[16,2048]{1,0:T(8,128)S(1)} %copy-done, ...), custom_call_target="tpu_custom_call" | custom-call | tf_op jit(solution)/shard_map/coarse_outer/pallas_call | solution.py:519
  26.6 1.9 %decode.1 = (bf16[4,64,512]{2,1,0:T(8,128)(2,1)}, f32[1152,128]{1,0:T(8,128)S(1)}, f32[64,1024]{1,0:T(8,128)S(1)}) custom-call(s32[16,2048]{1,0:T(8,128)S(1)} %copy-done, s32[8,256]{1,0:T(8,128)S(1)} %get-tuple-element.51.refs_0_.refs_1_.refs_2_, bf16[64,1024]{1,0:T(8,128)(2,1)S(1)} %get-tuple-element.55.refs_2_, ...), custom_call_target="tpu_custom_call" | custom-call | tf_op jit(solution)/shard_map/decode/pallas_call | solution.py:519
  28.5 3.3 %finish.1 = (f32[1152,128]{1,0:T(8,128)S(1)}, bf16[1152,128]{1,0:T(8,128)(2,1)S(1)}) custom-call(s32[1]{0:T(128)} %bitcast.2.core.refs_0_, s32[16,2048]{1,0:T(8,128)S(1)} %copy-done, s32[8,256]{1,0:T(8,128)S(1)} %get-tuple-element.51.refs_0_.refs_1_.refs_2_, bf16[64,1024]{1,0:T(8,128)(2,1)S(1)} %get-tuple-element.56.refs_3_, ...), custom_call_target="tpu_custom_call" | custom-call | tf_op jit(solution)/shard_map/finish/pallas_call | solution.py:519
  31.8 2.7 %collective-permute-start.4 = (bf16[1152,128]{1,0:T(8,128)(2,1)S(1)}, bf16[1152,128]{1,0:T(8,128)(2,1)S(1)}, u32[]{:S(2)}, u32[]{:S(2)}) collective-permute-start(bf16[1152,128]{1,0:T(8,128)(2,1)S(1)} %get-tuple-element.76), channel_id=1, source_target_pairs={{0,1},{1,0},{2,3},{3,2},{4,5},{5,4},{6,7},{7,6},{8,9},{9,8},{10,11... | collective-permute-start | bytes 884744 | tf_op jit(solution)/shard_map/ppermute | solution.py:540
  34.5 1.2 %collective-permute-done.4 = bf16[1152,128]{1,0:T(8,128)(2,1)S(1)} collective-permute-done((bf16[1152,128]{1,0:T(8,128)(2,1)S(1)}, bf16[1152,128]{1,0:T(8,128)(2,1)S(1)}, u32[]{:S(2)}, u32[]{:S(2)}) %collective-permute-start.4) | collective-permute-done | bytes 294944 | tf_op jit(solution)/shard_map/ppermute | solution.py:540
  35.7 0.1 add_convert_fusion
  35.8 23.0 %all_to_all.15 = bf16[16,72,128]{2,1,0:T(8,128)(2,1)S(1)} all-to-all(bf16[16,72,128]{2,1,0:T(8,128)(2,1)S(1)} %bitcast.28), channel_id=1, replica_groups=mesh['z'=8,'y'=4,'x'=4,'core'=2] {'y','x'}, dimensions={0} | all-to-all | bytes 589824 | tf_op jit(solution)/shard_map/all_to_all | solution.py:545
  58.9 17.2 %all_to_all.16 = bf16[8,72,128]{2,1,0:T(8,128)(2,1)S(1)} all-to-all(bf16[8,72,128]{2,1,0:T(8,128)(2,1)S(1)} %broadcast_in_dim.10), channel_id=1, replica_groups=mesh['z'=8,'y'=4,'x'=4,'core'=2] {'z'}, dimensions={0} | all-to-all | bytes 294912 | tf_op jit(solution)/shard_map/all_to_all | solution.py:545
  76.1 10.6 %all_to_all.17 = bf16[16,72,128]{2,1,0:T(8,128)(2,1)S(1)} all-to-all(bf16[16,72,128]{2,1,0:T(8,128)(2,1)S(1)} %broadcast_in_dim.11), channel_id=1, replica_groups=mesh['z'=8,'y'=4,'x'=4,'core'=2] {'y','x'}, dimensions={0} | all-to-all | bytes 589824 | tf_op jit(solution)/shard_map/all_to_all | solution.py:545
  86.8 4.0 %collective-permute-start.5 = (bf16[1152,128]{1,0:T(8,128)(2,1)S(1)}, bf16[1152,128]{1,0:T(8,128)(2,1)S(1)}, u32[]{:S(2)}, u32[]{:S(2)}) collective-permute-start(bf16[1152,128]{1,0:T(8,128)(2,1)S(1)} %bitcast.20), channel_id=1, source_target_pairs={{0,1},{1,0},{2,3},{3,2},{4,5},{5,4},{6,7},{7,6},{8,9},{9,8},{10,11... | collective-permute-start | bytes 884744 | tf_op jit(solution)/shard_map/ppermute | solution.py:540
  90.8 1.2 %collective-permute-done.5.refs_2_ = bf16[1152,128]{1,0:T(8,128)(2,1)S(1)} collective-permute-done((bf16[1152,128]{1,0:T(8,128)(2,1)S(1)}, bf16[1152,128]{1,0:T(8,128)(2,1)S(1)}, u32[]{:S(2)}, u32[]{:S(2)}) %collective-permute-start.5) | collective-permute-done | bytes 294944 | tf_op jit(solution)/shard_map/ppermute | solution.py:540
  92.0 1.5 %unfold.1 = (f32[64,1728]{1,0:T(8,128)}, f32[64,512]{1,0:T(8,128)}, f32[64,1728]{1,0:T(8,128)}, f32[64,512]{1,0:T(8,128)}) custom-call(s32[1]{0:T(128)} %bitcast.2.core.refs_0_, bf16[1152,128]{1,0:T(8,128)(2,1)S(1)} %bitcast.21, bf16[1152,128]{1,0:T(8,128)(2,1)S(1)} %collective-permute-done.5.refs_2_), custom_call_target="tpu_custom_call" | custom-call | tf_op jit(solution)/shard_map/unfold/pallas_call | solution.py:519
  (14 shorter events, 0.2 us)
Async XLA Ops:
  0.6 7.0 %copy-start = (s32[16,2048]{1,0:T(8,128)S(1)}, s32[16,2048]{1,0:T(8,128)}, u32[]{:S(2)}) copy-start(s32[16,2048]{1,0:T(8,128)} %constant.6.clone.refs_1_.refs_2_.refs_0_) | copy-start | bytes 393220
  0.6 7.0 %copy-start.1 = (bf16[1,4,64,512]{3,2,1,0:T(8,128)(2,1)S(1)}, bf16[1,4,64,512]{3,2,1,0:T(8,128)(2,1)}, u32[]{:S(2)}) copy-start(bf16[1,4,64,512]{3,2,1,0:T(8,128)(2,1)} %param.9) | copy-start | bytes 786436
  0.7 7.0 %copy-start.5 = (bf16[64,512]{1,0:T(8,128)(2,1)S(1)}, bf16[64,512]{1,0:T(8,128)(2,1)}, u32[]{:S(2)}) copy-start(bf16[64,512]{1,0:T(8,128)(2,1)} %refs_7_.2) | copy-start | bytes 196612
  0.7 7.0 %copy-start.6 = (bf16[64,512]{1,0:T(8,128)(2,1)S(1)}, bf16[64,512]{1,0:T(8,128)(2,1)}, u32[]{:S(2)}) copy-start(bf16[64,512]{1,0:T(8,128)(2,1)} %refs_5_.1) | copy-start | bytes 196612
  2.3 11.4 %collective-permute-start = (bf16[144,128]{1,0:T(8,128)(2,1)}, bf16[144,128]{1,0:T(8,128)(2,1)S(1)}, u32[]{:S(2)}, u32[]{:S(2)}) collective-permute-start(bf16[144,128]{1,0:T(8,128)(2,1)} %get-tuple-element.43), channel_id=1, source_target_pairs={{0,2},{2,4},{4,6},{6,8},{8,10},{10,12},{12,14},{14,16},{16,18},{18... | collective-permute-start | bytes 110600 | tf_op jit(solution)/shard_map/ppermute | solution.py:536
  6.3 1.4 %copy-start.7 = (s32[1,4,26]{2,1,0:T(4,128)S(1)}, s32[1,4,26]{2,1,0:T(4,128)}, u32[]{:S(2)}) copy-start(s32[1,4,26]{2,1,0:T(4,128)} %param.10) | copy-start | bytes 1252
  6.3 7.4 %collective-permute-start.1 = (bf16[144,128]{1,0:T(8,128)(2,1)}, bf16[144,128]{1,0:T(8,128)(2,1)S(1)}, u32[]{:S(2)}, u32[]{:S(2)}) collective-permute-start(bf16[144,128]{1,0:T(8,128)(2,1)} %get-tuple-element.44), channel_id=1, source_target_pairs={{2,0},{4,2},{6,4},{8,6},{10,8},{12,10},{14,12},{16,14},{18,16},{20... | collective-permute-start | bytes 110600 | tf_op jit(solution)/shard_map/ppermute | solution.py:536
  7.6 0.9 %copy-start.2 = (bf16[64,1728]{1,0:T(8,128)(2,1)S(1)}, bf16[64,1728]{1,0:T(8,128)(2,1)}, u32[]{:S(2)}) copy-start(bf16[64,1728]{1,0:T(8,128)(2,1)} %refs_7_.3) | copy-start | bytes 663556
  8.6 0.9 %copy-start.3 = (bf16[64,1728]{1,0:T(8,128)(2,1)S(1)}, bf16[64,1728]{1,0:T(8,128)(2,1)}, u32[]{:S(2)}) copy-start(bf16[64,1728]{1,0:T(8,128)(2,1)} %refs_6_.1) | copy-start | bytes 663556
  9.5 0.9 %copy-start.4 = (bf16[1,4,64,512]{3,2,1,0:T(8,128)(2,1)S(1)}, bf16[1,4,64,512]{3,2,1,0:T(8,128)(2,1)}, u32[]{:S(2)}) copy-start(bf16[1,4,64,512]{3,2,1,0:T(8,128)(2,1)} %param.16) | copy-start | bytes 786436
  16.2 7.9 %collective-permute-start.2 = (bf16[128,128]{1,0:T(8,128)(2,1)S(1)}, bf16[128,128]{1,0:T(8,128)(2,1)S(1)}, u32[]{:S(2)}, u32[]{:S(2)}) collective-permute-start(bf16[128,128]{1,0:T(8,128)(2,1)S(1)} %get-tuple-element.52), channel_id=1, source_target_pairs={{0,2},{2,4},{4,6},{6,8},{8,10},{10,12},{12,14},{14,16},{16,18},{18... | collective-permute-start | bytes 98312 | tf_op jit(solution)/shard_map/ppermute | solution.py:536
  20.2 4.7 %collective-permute-start.3 = (bf16[128,128]{1,0:T(8,128)(2,1)S(1)}, bf16[128,128]{1,0:T(8,128)(2,1)S(1)}, u32[]{:S(2)}, u32[]{:S(2)}) collective-permute-start(bf16[128,128]{1,0:T(8,128)(2,1)S(1)} %get-tuple-element.53), channel_id=1, source_target_pairs={{2,0},{4,2},{6,4},{8,6},{10,8},{12,10},{14,12},{16,14},{18,16},{20... | collective-permute-start | bytes 98312 | tf_op jit(solution)/shard_map/ppermute | solution.py:536
  21.5 0.7 copy-start.8
  31.8 3.9 %collective-permute-start.4 = (bf16[1152,128]{1,0:T(8,128)(2,1)S(1)}, bf16[1152,128]{1,0:T(8,128)(2,1)S(1)}, u32[]{:S(2)}, u32[]{:S(2)}) collective-permute-start(bf16[1152,128]{1,0:T(8,128)(2,1)S(1)} %get-tuple-element.76), channel_id=1, source_target_pairs={{0,1},{1,0},{2,3},{3,2},{4,5},{5,4},{6,7},{7,6},{8,9},{9,8},{10,11... | collective-permute-start | bytes 884744 | tf_op jit(solution)/shard_map/ppermute | solution.py:540
  86.8 5.2 %collective-permute-start.5 = (bf16[1152,128]{1,0:T(8,128)(2,1)S(1)}, bf16[1152,128]{1,0:T(8,128)(2,1)S(1)}, u32[]{:S(2)}, u32[]{:S(2)}) collective-permute-start(bf16[1152,128]{1,0:T(8,128)(2,1)S(1)} %bitcast.20), channel_id=1, source_target_pairs={{0,1},{1,0},{2,3},{3,2},{4,5},{5,4},{6,7},{7,6},{8,9},{9,8},{10,11... | collective-permute-start | bytes 884744 | tf_op jit(solution)/shard_map/ppermute | solution.py:540

commit v5 on v4

--- a/solution.py
+++ b/solution.py
@@ -192,7 +192,7 @@
 
 
 def fine_inner(neighbours, table, w_fine, w_down, w_coarse, w_up, feat, cot,
-               pre, edges, up_back, ext, cot_plane, cot_patch, w_adj, w_ups, w_dns, taps):
+               pre, edges, up_back, taps, cot_plane, cot_patch, w_adj, w_ups, w_dns):
     planes = natural_planes(feat)
     edges[0], edges[1] = planes[0], planes[7]
     cells = table[1:2, :128]
@@ -201,7 +201,6 @@
     weight = tap_rows(w_fine)
     for x in range(8):
         plane = whole[64 * x : 64 * x + 64]
-        ext[x] = plane
         put_taps(taps, 512 * x, plane, FINE_SHIFTS)
     for x in range(8):
         part = mm(weight, taps[:, 512 * x : 512 * x + 512])
@@ -246,7 +245,7 @@
 
 
 def fine_outer(neighbours, table, from_lower, from_upper, edges, pre, w_fine, w_down, up_back,
-               hidden, patch, coarse_pre, hidden1, pre_edge, ext_edge, to_upper, to_lower, taps):
+               hidden, patch, coarse_pre, hidden1, pre_edge, taps, to_upper, to_lower):
     cells = table[1:2, :128]
     weight = tap_rows(w_fine)
     for side, a, base, payload in ((0, 0, 4, from_lower), (1, 2, 20, from_upper)):
@@ -254,7 +253,6 @@
         code = jnp.concatenate([edge_code(v, cells, base, slots) for v in fine_slots(neighbours, table, a)], axis=1)
         pool = jnp.concatenate([edges[1 - side], payload[0:64, :], payload[64:128, :]], axis=1)
         plane = mm(pool, onehot(code, 512)).astype(BF16)
-        ext_edge[side] = plane
         put_taps(taps, 512 * side, plane, FINE_SHIFTS)
         part = mm(weight[64 * a : 64 * a + 64], taps[:, 512 * side : 512 * side + 512])
         pre_edge[side] = pre[7 * side] + part
@@ -278,12 +276,10 @@
     return jnp.concatenate([v[:, 256 * x : 256 * x + 256] for x in range(4)], axis=0)
 
 
-def coarse_inner_conv(field, select, weight, taps, ext):
+def coarse_inner_conv(field, select, weight, taps):
     whole = mm(by_rows(field), select).astype(BF16)
     for x in range(4):
         plane = whole[64 * x : 64 * x + 64]
-        if ext is not None:
-            ext[:, 256 * x : 256 * x + 256] = plane
         put_taps(taps, 256 * x, plane, COARSE_SHIFTS)
     part = mm(weight, taps[:, :1024])
     sums = []
@@ -301,7 +297,7 @@
     pool = jnp.concatenate([own_plane, arrived], axis=1)
     plane = mm(pool, onehot(codes[side : side + 1, :], 512)).astype(BF16)
     put_taps(taps, at, plane, COARSE_SHIFTS)
-    return mm(weight[128 * side : 128 * side + 64], taps[:, at : at + 256]), plane
+    return mm(weight[128 * side : 128 * side + 64], taps[:, at : at + 256])
 
 
 def peer_codes(table, slots, own_slots):
@@ -324,7 +320,7 @@
 
 
 def coarse_inner(neighbours, sends, table, from_lower, from_upper, hidden1, pre, pre_edge, w_coarse, coarse_pre,
-                 codes, ext, conv, fine_slope, coarse_slope, taps):
+                 codes, taps, conv, fine_slope, coarse_slope):
     coarse_slope[...] = slope(coarse_pre[...])
     cells = table[3:4, :128]
     for row, a, base, payload in ((0, 0, 4, from_lower), (1, 2, 20, from_upper)):
@@ -338,14 +334,14 @@
     codes[2:3, :] = jnp.concatenate(code, axis=1)
     codes[7:8, :] = jnp.full((1, 256), -1, I32)
     select = onehot(codes[2:3, :], 256)
-    conv[...] = coarse_inner_conv(hidden1[...], select, tap_rows(w_coarse), taps, ext)
+    conv[...] = coarse_inner_conv(hidden1[...], select, tap_rows(w_coarse), taps)
     for x in range(8):
         value = pre_edge[0] if x == 0 else pre_edge[1] if x == 7 else pre[x]
         fine_slope[x] = slope(value)
 
 
 def coarse_outer(codes, table, hidden1, from_lower, from_upper, conv, up_back, w_coarse,
-                 gated, delta, ext_edge, delta_lower, delta_upper, taps, peer_taps):
+                 gated, delta, taps, delta_lower, delta_upper, peer_taps):
     weight = tap_rows(w_coarse)
     spread = onehot(table[10:11, :512], 128)
     edge = []
@@ -355,7 +351,7 @@
     ):
         full = mm(payload[...], spread)
         top = full[:64].astype(BF16)
-        part, ext_edge[side] = coarse_outer_conv(codes, side, own, top[:, :256], weight, taps, 256 * side)
+        part = coarse_outer_conv(codes, side, own, top[:, :256], weight, taps, 256 * side)
         edge.append(part)
         select = onehot(codes[3 + side : 4 + side, :], 256)
         rows = mm(jnp.concatenate([top[:, :256], top[:, 256:]], axis=0), select).astype(BF16)
@@ -372,10 +368,27 @@
     delta[...] = (up_back[...] * slope(value)).astype(BF16)
 
 
-def decode(table, codes, gated, delta, ext, ext_edge, hidden, cot_patch, w_ups, w_adj,
-           decoded, grads, back, taps, stack, spread):
+def tap_gradient(taps, stack, edge_taps, first, last):
+    own = nt(taps, stack)
+    width = first.shape[1]
+    low, high = nt(edge_taps[:, :width], first), nt(edge_taps[:, width:], last)
+    return jnp.concatenate([own[:, :64] + low, own[:, 64:128], own[:, 128:] + high], axis=1)
+
+
+def turn(codes, gated, delta, taps, edge_taps, cot_patch, w_adj, grads, back, delta_taps, stack):
     select = onehot(codes[2:3, :], 256)
-    back[...] = coarse_inner_conv(delta[...], select, w_adj[...], taps, None)
+    back[...] = coarse_inner_conv(delta[...], select, w_adj[...], delta_taps)
+    stack[0:64, 768:1024] = jnp.zeros((64, 256), BF16)
+    stack[128:192, 0:256] = jnp.zeros((64, 256), BF16)
+    stack[0:64, 0:768] = delta[:, 256:]
+    stack[64:128, :] = delta[...]
+    stack[128:192, 256:1024] = delta[:, :768]
+    of_coarse = tap_gradient(taps[...], stack[...], edge_taps, delta[:, :256], delta[:, 768:])
+    of_up = jnp.concatenate([nt(cot_patch[...], gated[...]), jnp.zeros((64, 64), F32)], axis=0)
+    put_grads(grads, of_coarse, of_up)
+
+
+def decode(table, gated, hidden, w_ups, decoded, spread):
     chosen = mm(by_rows(gated[...]), onehot(table[7:8, :1024], 256)).astype(BF16)
     for x in range(4):
         for jl in range(4):
@@ -395,23 +408,13 @@
             ]
             decoded[2 * p, :, 128 * t : 128 * t + 128] = merge(low, even, odd).astype(BF16)
             decoded[2 * p + 1, :, 128 * t : 128 * t + 128] = merge_high(low, even, odd).astype(BF16)
-    put_taps(taps, 0, ext_edge[0], COARSE_SHIFTS)
-    for x in range(4):
-        put_taps(taps, 256 + 256 * x, ext[:, 256 * x : 256 * x + 256], COARSE_SHIFTS)
-    put_taps(taps, 1280, ext_edge[1], COARSE_SHIFTS)
-    stack[...] = jnp.zeros(stack.shape, BF16)
-    for a in range(3):
-        stack[64 * a : 64 * a + 64, 256 * a : 256 * a + 1024] = delta[...]
-    of_coarse = nt(taps[...], stack[...])
-    of_up = jnp.concatenate([nt(cot_patch[...], gated[...]), jnp.zeros((64, 64), F32)], axis=0)
-    put_grads(grads, of_coarse, of_up)
 
 
 def finish(core, table, codes, delta, from_lower, from_upper, back, w_adj, coarse_slope, patch, w_dns, fine_slope,
-           cot_plane, ext, ext_edge, grads_b, keep, send, coarse_taps, spread, taps, stack, grads):
+           cot_plane, taps, edge_taps, grads_b, keep, send, coarse_taps, spread, stack, grads):
     weight = w_adj[...]
-    low, _ = coarse_outer_conv(codes, 0, delta[:, 768:], from_lower[...], weight, coarse_taps, 0)
-    high, _ = coarse_outer_conv(codes, 1, delta[:, :256], from_upper[...], weight, coarse_taps, 256)
+    low = coarse_outer_conv(codes, 0, delta[:, 768:], from_lower[...], weight, coarse_taps, 0)
+    high = coarse_outer_conv(codes, 1, delta[:, :256], from_upper[...], weight, coarse_taps, 256)
     value = back[...]
     value = jnp.concatenate([value[:, :256] + low, value[:, 256:768], value[:, 768:] + high], axis=1)
     down = (value * coarse_slope[...]).astype(BF16)
@@ -422,10 +425,8 @@
             spread[64 * jl : 64 * jl + 64, 512 * x : 512 * x + 512] = (
                 chosen[64 * x : 64 * x + 64, 512 * jl : 512 * jl + 512]
             )
-    for a in range(3):
-        for plane in range(10):
-            if not 0 <= plane - a < 8:
-                stack[64 * a : 64 * a + 64, 512 * plane : 512 * plane + 512] = jnp.zeros((64, 512), BF16)
+    stack[0:64, 3584:4096] = jnp.zeros((64, 512), BF16)
+    stack[128:192, 0:512] = jnp.zeros((64, 512), BF16)
     for half in range(4):
         raised = mm(w_dns[...], spread[:, 512 * half : 512 * half + 512])
         for i in range(2):
@@ -433,13 +434,11 @@
             total = cot_plane[x].astype(F32) + raised[64 * i : 64 * i + 64]
             fine = (total * fine_slope[x]).astype(BF16)
             for a in range(3):
-                at = 512 * (x + a)
-                stack[64 * a : 64 * a + 64, at : at + 512] = fine
-    put_taps(taps, 0, ext_edge[0], FINE_SHIFTS)
-    for x in range(8):
-        put_taps(taps, 512 * x + 512, ext[x], FINE_SHIFTS)
-    put_taps(taps, 4608, ext_edge[1], FINE_SHIFTS)
-    put_grads(grads, nt(taps[...], stack[...]), of_down)
+                plane = x + a - 1
+                if 0 <= plane < 8:
+                    stack[64 * a : 64 * a + 64, 512 * plane : 512 * plane + 512] = fine
+    of_fine = tap_gradient(taps[...], stack[...], edge_taps, stack[64:128, 0:512], stack[64:128, 3584:4096])
+    put_grads(grads, of_fine, of_down)
     first = core[0] == 0
 
     @pl.when(first)
@@ -582,45 +581,48 @@
     from_lower, from_upper = passed_along(to_upper, 1), passed_along(to_lower, -1)
 
     fine = (8, 64, 512)
-    pre, edges, up_back, ext0, cot_plane, cot_patch, w_adj, w_ups, w_dns = call(
+    pre, edges, up_back, taps0, cot_plane, cot_patch, w_adj, w_ups, w_dns = call(
         fine_inner, "fine_inner", 8,
-        [(0, fine, F32), (0, (2, 64, 256), BF16), (0, (64, 1024), F32), (0, fine, BF16), (0, fine, BF16),
+        [(0, fine, F32), (0, (2, 64, 256), BF16), (0, (64, 1024), F32), (0, (576, 4096), BF16), (0, fine, BF16),
          (0, (512, 1024), BF16), (0, (192, 576), BF16), (0, (128, 256), BF16), (0, (128, 256), BF16)],
-        [((576, 4096), BF16)],
+        [],
         [near, table, w_fine, w_down, w_coarse, w_up, feat, cot],
     )
-    hidden0, patch0, coarse_pre, hidden1, pre_edge, ext0_edge, to_upper, to_lower = call(
+    hidden0, patch0, coarse_pre, hidden1, pre_edge, taps0_edge, to_upper, to_lower = call(
         fine_outer, "fine_outer", 4,
         [(0, fine, BF16), (0, (512, 1024), BF16), (0, (64, 1024), F32), (0, (64, 1024), BF16), (0, (2, 64, 512), F32),
-         (0, (2, 64, 512), BF16), (0, (128, 128), BF16), (0, (128, 128), BF16)],
-        [((576, 1024), BF16)],
+         (0, (576, 1024), BF16), (0, (128, 128), BF16), (0, (128, 128), BF16)],
+        [],
         [near, table, from_lower, from_upper, edges, pre, w_fine, w_down, up_back],
     )
     low1, high1 = passed_along(to_upper, 1), passed_along(to_lower, -1)
-    codes, ext1, conv, fine_slope, coarse_slope = call(
+    codes, taps1, conv, fine_slope, coarse_slope = call(
         coarse_inner, "coarse_inner", 4,
-        [(0, (8, 256), I32), (0, (64, 1024), BF16), (0, (64, 1024), F32), (0, fine, F32), (0, (64, 1024), F32)],
-        [((576, 1024), BF16)],
+        [(0, (8, 256), I32), (0, (576, 1024), BF16), (0, (64, 1024), F32), (0, fine, F32), (0, (64, 1024), F32)],
+        [],
         [near, sends, table, from_lower, from_upper, hidden1, pre, pre_edge, w_coarse, coarse_pre],
     )
-    gated, delta_up, ext1_edge, low2, high2 = call(
+    gated, delta_up, taps1_edge, low2, high2 = call(
         coarse_outer, "coarse_outer", 5,
-        [(0, (64, 1024), BF16), (0, (64, 1024), BF16), (0, (2, 64, 256), BF16), (0, (64, 256), BF16), (0, (64, 256), BF16)],
-        [((576, 512), BF16), ((1728, 512), BF16)],
+        [(0, (64, 1024), BF16), (0, (64, 1024), BF16), (0, (576, 512), BF16), (0, (64, 256), BF16), (0, (64, 256), BF16)],
+        [((1728, 512), BF16)],
         [codes, table, hidden1, low1, high1, conv, up_back, w_coarse],
     )
-    decoded, grads_b, back = call(
-        decode, "decode", 6,
-        [(0, (4, 64, 512), BF16), (0, (1152, 128), F32), (0, (64, 1024), F32)],
-        [((576, 1536), BF16), ((192, 1536), BF16), ((256, 1024), BF16)],
-        [table, codes, gated, delta_up, ext1, ext1_edge, hidden0, cot_patch, w_ups, w_adj],
+    grads_b, back = call(
+        turn, "turn", 5,
+        [(0, (1152, 128), F32), (0, (64, 1024), F32)],
+        [((576, 1024), BF16), ((192, 1024), BF16)],
+        [codes, gated, delta_up, taps1, taps1_edge, cot_patch, w_adj],
+    )
+    (decoded,) = call(
+        decode, "decode", 5, [(0, (4, 64, 512), BF16)], [((256, 1024), BF16)], [table, gated, hidden0, w_ups],
     )
     keep, send = call(
-        finish, "finish", 12,
+        finish, "finish", 8,
         [(0, (1152, 128), F32), (0, (1152, 128), BF16)],
-        [((576, 512), BF16), ((256, 2048), BF16), ((576, 5120), BF16), ((192, 5120), BF16), ((1152, 128), F32)],
-        [core, table, codes, delta_up, low2, high2, back, w_adj, coarse_slope, patch0, w_dns, fine_slope, cot_plane, ext0,
-         ext0_edge, grads_b],
+        [((576, 512), BF16), ((256, 2048), BF16), ((192, 4096), BF16), ((1152, 128), F32)],
+        [core, table, codes, delta_up, low2, high2, back, w_adj, coarse_slope, patch0, w_dns, fine_slope, cot_plane, taps0,
+         taps0_edge, grads_b],
     )
     total = total_over_devices(keep, send)
     factor = 1.0 / math.sqrt(lax.axis_size(AXES) * 4 * 512)

time: 93.9 us -> 98.1 us (1.045)
  local copies, waits for them, and re-layouts: 3.58 us -> 7.11 us
  Pallas kernels: 17.7 us -> 18.7 us
    unnamed x18 -> x22, local copies, waits for them, and re-layouts: 3.52 us -> 7.05 us
    ppermute x2, waiting for transfers between devices: 2.42 us -> 1.21 us  [other_core(): return lax.ppermute(x, 'core', [(0, 1), (1, 0)])]
    pallas_call x7 -> x8, Pallas kernels: 16 us -> 17 us  [call(): pl.pallas_call(body, name=name, out_shape=[jax.ShapeDtypeStruct(shape, ki...]
  transfers between devices with their start and end apart: 6 -> 6, of which waited for: 3 -> 2; matrix products, arithmetic and copies ran while one was open for 0% -> 0% of each run, Pallas kernels for 5% -> 7%
where the time goes in v5:
time: 98.1 us; the launch traced here: 97.5 us
  blocking collectives  50.8 us (52%)
  Pallas kernels  18.7 us (19%)
  starting transfers between devices  17.3 us (18%)
  local copies, waits for them, and re-layouts  7.11 us (7%)
  waiting for transfers between devices  2.64 us (3%)
    all_to_all x3, blocking collectives, dealt(): return lax.all_to_all(x.reshape(count, -1, 128), axes, 0, 0, tiled=True)  50.8 us
    pallas_call x8, Pallas kernels, call(): pl.pallas_call(body, name=name, out_shape=[jax.ShapeDtypeStruct(shape, ki...  17 us
    ppermute x4, starting transfers between devices, passed_along(): return lax.ppermute(block, CHIPS, route)  10.5 us
    unnamed x22, local copies, waits for them, and re-layouts  7.05 us
    ppermute x2, starting transfers between devices, other_core(): return lax.ppermute(x, 'core', [(0, 1), (1, 0)])  6.76 us
  transfers between devices with their start and end apart: 6, of which 2 were waited for; matrix products, arithmetic and copies ran while one was open for 0% of the time, Pallas kernels for 7%

profile of v5, /device:TPU:1, one launch (start us, length us, event | category | flops | bytes accessed | tf_op | source)
XLA Modules:
  0.0 97.5 jit_solution(10862383884020880784)
XLA Ops:
  0.6 0.0 copy-start.1
  0.6 1.6 %pack_faces.1 = (bf16[144,128]{1,0:T(8,128)(2,1)}, bf16[144,128]{1,0:T(8,128)(2,1)}) custom-call(s32[1]{0:T(128)} %bitcast.2.core.refs_0_, s32[2,16]{1,0:T(2,128)} %bitcast.26, bf16[4,64,512]{2,1,0:T(8,128)(2,1)} %bitcast.17, bf16[4,64,512]{2,1,0:T(8,128)(2,1)} %bitcast.18), custom_call_target="tpu_custom_call" | custom-call | tf_op jit(solution)/shard_map/pack_faces/pallas_call | solution.py:572
  2.3 3.9 %collective-permute-start = (bf16[144,128]{1,0:T(8,128)(2,1)}, bf16[144,128]{1,0:T(8,128)(2,1)S(1)}, u32[]{:S(2)}, u32[]{:S(2)}) collective-permute-start(bf16[144,128]{1,0:T(8,128)(2,1)} %get-tuple-element.42), channel_id=1, source_target_pairs={{0,2},{2,4},{4,6},{6,8},{8,10},{10,12},{12,14},{14,16},{16,18},{18... | collective-permute-start | bytes 110600 | tf_op jit(solution)/shard_map/ppermute | solution.py:535
  6.2 1.3 %collective-permute-start.1 = (bf16[144,128]{1,0:T(8,128)(2,1)}, bf16[144,128]{1,0:T(8,128)(2,1)S(1)}, u32[]{:S(2)}, u32[]{:S(2)}) collective-permute-start(bf16[144,128]{1,0:T(8,128)(2,1)} %get-tuple-element.43), channel_id=1, source_target_pairs={{2,0},{4,2},{6,4},{8,6},{10,8},{12,10},{14,12},{16,14},{18,16},{20... | collective-permute-start | bytes 110600 | tf_op jit(solution)/shard_map/ppermute | solution.py:535
  7.5 0.0 copy-start
  7.5 0.9 copy-done
  8.4 0.9 copy-done.2
  9.4 0.9 copy-done.3
  10.3 0.9 copy-done.5
  11.3 0.9 copy-done.6
  12.2 0.8 copy-done.7
  13.1 0.8 copy-done.8
  13.9 0.7 copy-done.9
  14.6 3.2 %fine_inner.1 = (f32[8,64,512]{2,1,0:T(8,128)S(1)}, bf16[2,64,256]{2,1,0:T(8,128)(2,1)S(1)}, f32[64,1024]{1,0:T(8,128)S(1)}, bf16[576,4096]{1,0:T(8,128)(2,1)S(1...) custom-call(s32[4,26]{1,0:T(4,128)S(1)} %bitcast.23, ...), custom_call_target="tpu_custom_call" | custom-call | tf_op jit(solution)/shard_map/fine_inner/pallas_call | solution.py:518
  17.8 0.0 copy-start.4
  17.8 2.5 %fine_outer.1 = (bf16[8,64,512]{2,1,0:T(8,128)(2,1)S(1)}, bf16[512,1024]{1,0:T(8,128)(2,1)S(1)}, f32[64,1024]{1,0:T(8,128)S(1)}, bf16[64,1024]{1,0:T(8,128)(2,1)...) custom-call(s32[4,26]{1,0:T(4,128)S(1)} %bitcast.24, ...), custom_call_target="tpu_custom_call" | custom-call | tf_op jit(solution)/shard_map/fine_outer/pallas_call | solution.py:518
  20.3 4.0 %collective-permute-start.2 = (bf16[128,128]{1,0:T(8,128)(2,1)S(1)}, bf16[128,128]{1,0:T(8,128)(2,1)S(1)}, u32[]{:S(2)}, u32[]{:S(2)}) collective-permute-start(bf16[128,128]{1,0:T(8,128)(2,1)S(1)} %get-tuple-element.51), channel_id=1, source_target_pairs={{0,2},{2,4},{4,6},{6,8},{8,10},{10,12},{12,14},{14,16},{16,18},{18... | collective-permute-start | bytes 98312 | tf_op jit(solution)/shard_map/ppermute | solution.py:535
  24.3 1.3 %collective-permute-start.3 = (bf16[128,128]{1,0:T(8,128)(2,1)S(1)}, bf16[128,128]{1,0:T(8,128)(2,1)S(1)}, u32[]{:S(2)}, u32[]{:S(2)}) collective-permute-start(bf16[128,128]{1,0:T(8,128)(2,1)S(1)} %get-tuple-element.52), channel_id=1, source_target_pairs={{2,0},{4,2},{6,4},{8,6},{10,8},{12,10},{14,12},{16,14},{18,16},{20... | collective-permute-start | bytes 98312 | tf_op jit(solution)/shard_map/ppermute | solution.py:535
  25.7 1.9 %coarse_inner.1 = (s32[8,256]{1,0:T(8,128)S(1)}, bf16[576,1024]{1,0:T(8,128)(2,1)S(1)}, f32[64,1024]{1,0:T(8,128)S(1)}, f32[8,64,512]{2,1,0:T(8,128)S(1)}, f32[64,1024]{1,0:T(8,128)S(1)}) custom-call(s32[4,26]{1,0:T(4,128)S(1)} %bitcast.25, s32[2,16]{1,0:T(2,128)S(1)} %bitcast.27, s32[16,2048]{1,0:T(8,128)S(1)} %copy-done.1, ...), custom_call_target="tpu_custom_call" | custom-call | tf_op jit(solution)/shard_map/coarse_inner/pallas_call | solution.py:518
  27.6 1.4 %collective-permute-done.3.refs_4_ = bf16[128,128]{1,0:T(8,128)(2,1)S(1)} collective-permute-done((bf16[128,128]{1,0:T(8,128)(2,1)S(1)}, bf16[128,128]{1,0:T(8,128)(2,1)S(1)}, u32[]{:S(2)}, u32[]{:S(2)}) %collective-permute-start.3) | collective-permute-done | bytes 32800 | tf_op jit(solution)/shard_map/ppermute | solution.py:535
  29.0 1.7 %coarse_outer.1 = (bf16[64,1024]{1,0:T(8,128)(2,1)S(1)}, bf16[64,1024]{1,0:T(8,128)(2,1)S(1)}, bf16[576,512]{1,0:T(8,128)(2,1)S(1)}, bf16[64,256]{1,0:T(8,128)(2,1)S(1)}, bf16[64,256]{1,0:T(8,128)(2,1)S(1)}) custom-call(s32[8,256]{1,0:T(8,128)S(1)} %get-tuple-element.50.refs_0_.refs_2_, s32[16,2048]{1,0:T(8,128)S(1)} %copy-done.1, ...), custom_call_target="tpu_custom_call" | custom-call | tf_op jit(solution)/shard_map/coarse_outer/pallas_call | solution.py:518
  30.7 1.6 %turn.1 = (f32[1152,128]{1,0:T(8,128)S(1)}, f32[64,1024]{1,0:T(8,128)S(1)}) custom-call(s32[8,256]{1,0:T(8,128)S(1)} %get-tuple-element.50.refs_0_.refs_2_, bf16[64,1024]{1,0:T(8,128)(2,1)S(1)} %get-tuple-element.54.refs_1_, bf16[64,1024]{1,0:T(8,128)(2,1)S(1)} %get-tuple-element.57.refs_2_.refs_3_, bf16[576,1024]{1,0:T(8,128)(2,1)S(1)} %get-tuple-element.60.refs_3_, ...), custom_call_target="tpu_custom_call" | custom-call | tf_op jit(solution)/shard_map/turn/pallas_call | solution.py:518
  32.3 3.2 %finish.1 = (f32[1152,128]{1,0:T(8,128)S(1)}, bf16[1152,128]{1,0:T(8,128)(2,1)S(1)}) custom-call(s32[1]{0:T(128)} %bitcast.2.core.refs_0_, s32[16,2048]{1,0:T(8,128)S(1)} %copy-done.1, s32[8,256]{1,0:T(8,128)S(1)} %get-tuple-element.50.refs_0_.refs_2_, bf16[64,1024]{1,0:T(8,128)(2,1)S(1)} %get-tuple-element.57.refs_2_.refs_3_, ...), custom_call_target="tpu_custom_call" | custom-call | tf_op jit(solution)/shard_map/finish/pallas_call | solution.py:518
  35.5 2.7 %collective-permute-start.4 = (bf16[1152,128]{1,0:T(8,128)(2,1)S(1)}, bf16[1152,128]{1,0:T(8,128)(2,1)S(1)}, u32[]{:S(2)}, u32[]{:S(2)}) collective-permute-start(bf16[1152,128]{1,0:T(8,128)(2,1)S(1)} %get-tuple-element.74), channel_id=1, source_target_pairs={{0,1},{1,0},{2,3},{3,2},{4,5},{5,4},{6,7},{7,6},{8,9},{9,8},{10,11... | collective-permute-start | bytes 884744 | tf_op jit(solution)/shard_map/ppermute | solution.py:539
  38.3 1.2 %collective-permute-done.4 = bf16[1152,128]{1,0:T(8,128)(2,1)S(1)} collective-permute-done((bf16[1152,128]{1,0:T(8,128)(2,1)S(1)}, bf16[1152,128]{1,0:T(8,128)(2,1)S(1)}, u32[]{:S(2)}, u32[]{:S(2)}) %collective-permute-start.4) | collective-permute-done | bytes 294944 | tf_op jit(solution)/shard_map/ppermute | solution.py:539
  39.5 0.1 add_convert_fusion
  39.5 23.0 %all_to_all.15 = bf16[16,72,128]{2,1,0:T(8,128)(2,1)S(1)} all-to-all(bf16[16,72,128]{2,1,0:T(8,128)(2,1)S(1)} %bitcast.28), channel_id=1, replica_groups=mesh['z'=8,'y'=4,'x'=4,'core'=2] {'y','x'}, dimensions={0} | all-to-all | bytes 589824 | tf_op jit(solution)/shard_map/all_to_all | solution.py:544
  62.6 17.2 %all_to_all.16 = bf16[8,72,128]{2,1,0:T(8,128)(2,1)S(1)} all-to-all(bf16[8,72,128]{2,1,0:T(8,128)(2,1)S(1)} %broadcast_in_dim.10), channel_id=1, replica_groups=mesh['z'=8,'y'=4,'x'=4,'core'=2] {'z'}, dimensions={0} | all-to-all | bytes 294912 | tf_op jit(solution)/shard_map/all_to_all | solution.py:544
  79.9 10.6 %all_to_all.17 = bf16[16,72,128]{2,1,0:T(8,128)(2,1)S(1)} all-to-all(bf16[16,72,128]{2,1,0:T(8,128)(2,1)S(1)} %broadcast_in_dim.11), channel_id=1, replica_groups=mesh['z'=8,'y'=4,'x'=4,'core'=2] {'y','x'}, dimensions={0} | all-to-all | bytes 589824 | tf_op jit(solution)/shard_map/all_to_all | solution.py:544
  90.5 4.0 %collective-permute-start.5 = (bf16[1152,128]{1,0:T(8,128)(2,1)S(1)}, bf16[1152,128]{1,0:T(8,128)(2,1)S(1)}, u32[]{:S(2)}, u32[]{:S(2)}) collective-permute-start(bf16[1152,128]{1,0:T(8,128)(2,1)S(1)} %bitcast.20), channel_id=1, source_target_pairs={{0,1},{1,0},{2,3},{3,2},{4,5},{5,4},{6,7},{7,6},{8,9},{9,8},{10,11... | collective-permute-start | bytes 884744 | tf_op jit(solution)/shard_map/ppermute | solution.py:539
  94.5 1.4 %decode.1 = bf16[4,64,512]{2,1,0:T(8,128)(2,1)} custom-call(s32[16,2048]{1,0:T(8,128)S(1)} %copy-done.1, bf16[64,1024]{1,0:T(8,128)(2,1)S(1)} %get-tuple-element.54.refs_1_, bf16[8,64,512]{2,1,0:T(8,128)(2,1)S(1)} %get-tuple-element.55.refs_2_, bf16[128,256]{1,0:T(8,128)(2,1)S(1)} %get-tuple-element.56.refs_3_), custom_call_target="tpu_custom_call" | custom-call | tf_op jit(solution)/shard_map/decode/pallas_call | solution.py:518
  96.0 1.5 %unfold.1 = (f32[64,1728]{1,0:T(8,128)}, f32[64,512]{1,0:T(8,128)}, f32[64,1728]{1,0:T(8,128)}, f32[64,512]{1,0:T(8,128)}) custom-call(s32[1]{0:T(128)} %bitcast.2.core.refs_0_, bf16[1152,128]{1,0:T(8,128)(2,1)S(1)} %bitcast.21, bf16[1152,128]{1,0:T(8,128)(2,1)S(1)} %collective-permute-done.5.refs_2_), custom_call_target="tpu_custom_call" | custom-call | tf_op jit(solution)/shard_map/unfold/pallas_call | solution.py:518
  (19 shorter events, 0.2 us)
Async XLA Ops:
  0.6 17.2 %copy-start.1 = (s32[16,2048]{1,0:T(8,128)S(1)}, s32[16,2048]{1,0:T(8,128)}, u32[]{:S(2)}) copy-start(s32[16,2048]{1,0:T(8,128)} %constant.6.clone.refs_1_.refs_2_.refs_0_) | copy-start | bytes 393220
  2.3 15.5 %collective-permute-start = (bf16[144,128]{1,0:T(8,128)(2,1)}, bf16[144,128]{1,0:T(8,128)(2,1)S(1)}, u32[]{:S(2)}, u32[]{:S(2)}) collective-permute-start(bf16[144,128]{1,0:T(8,128)(2,1)} %get-tuple-element.42), channel_id=1, source_target_pairs={{0,2},{2,4},{4,6},{6,8},{8,10},{10,12},{12,14},{14,16},{16,18},{18... | collective-permute-start | bytes 110600 | tf_op jit(solution)/shard_map/ppermute | solution.py:535
  6.2 11.6 %collective-permute-start.1 = (bf16[144,128]{1,0:T(8,128)(2,1)}, bf16[144,128]{1,0:T(8,128)(2,1)S(1)}, u32[]{:S(2)}, u32[]{:S(2)}) collective-permute-start(bf16[144,128]{1,0:T(8,128)(2,1)} %get-tuple-element.43), channel_id=1, source_target_pairs={{2,0},{4,2},{6,4},{8,6},{10,8},{12,10},{14,12},{16,14},{18,16},{20... | collective-permute-start | bytes 110600 | tf_op jit(solution)/shard_map/ppermute | solution.py:535
  7.5 0.9 copy-start
  8.4 0.9 copy-start.2
  9.4 0.9 copy-start.3
  10.3 0.9 copy-start.5
  11.3 0.9 copy-start.6
  12.2 0.8 copy-start.7
  13.1 0.8 copy-start.8
  13.9 0.7 copy-start.9
  17.8 7.9 %copy-start.4 = (bf16[64,1728]{1,0:T(8,128)(2,1)S(1)}, bf16[64,1728]{1,0:T(8,128)(2,1)}, u32[]{:S(2)}) copy-start(bf16[64,1728]{1,0:T(8,128)(2,1)} %refs_7_.3) | copy-start | bytes 663556
  17.8 7.9 %copy-start.10 = (s32[1,1,2,16]{3,2,1,0:T(2,128)S(1)}, s32[1,1,2,16]{3,2,1,0:T(2,128)}, u32[]{:S(2)}) copy-start(s32[1,1,2,16]{3,2,1,0:T(2,128)} %param.11) | copy-start | bytes 388
  20.3 7.2 %collective-permute-start.2 = (bf16[128,128]{1,0:T(8,128)(2,1)S(1)}, bf16[128,128]{1,0:T(8,128)(2,1)S(1)}, u32[]{:S(2)}, u32[]{:S(2)}) collective-permute-start(bf16[128,128]{1,0:T(8,128)(2,1)S(1)} %get-tuple-element.51), channel_id=1, source_target_pairs={{0,2},{2,4},{4,6},{6,8},{8,10},{10,12},{12,14},{14,16},{16,18},{18... | collective-permute-start | bytes 98312 | tf_op jit(solution)/shard_map/ppermute | solution.py:535
  24.3 4.7 %collective-permute-start.3 = (bf16[128,128]{1,0:T(8,128)(2,1)S(1)}, bf16[128,128]{1,0:T(8,128)(2,1)S(1)}, u32[]{:S(2)}, u32[]{:S(2)}) collective-permute-start(bf16[128,128]{1,0:T(8,128)(2,1)S(1)} %get-tuple-element.52), channel_id=1, source_target_pairs={{2,0},{4,2},{6,4},{8,6},{10,8},{12,10},{14,12},{16,14},{18,16},{20... | collective-permute-start | bytes 98312 | tf_op jit(solution)/shard_map/ppermute | solution.py:535
  35.5 4.0 %collective-permute-start.4 = (bf16[1152,128]{1,0:T(8,128)(2,1)S(1)}, bf16[1152,128]{1,0:T(8,128)(2,1)S(1)}, u32[]{:S(2)}, u32[]{:S(2)}) collective-permute-start(bf16[1152,128]{1,0:T(8,128)(2,1)S(1)} %get-tuple-element.74), channel_id=1, source_target_pairs={{0,1},{1,0},{2,3},{3,2},{4,5},{5,4},{6,7},{7,6},{8,9},{9,8},{10,11... | collective-permute-start | bytes 884744 | tf_op jit(solution)/shard_map/ppermute | solution.py:539
  90.5 5.5 %collective-permute-start.5 = (bf16[1152,128]{1,0:T(8,128)(2,1)S(1)}, bf16[1152,128]{1,0:T(8,128)(2,1)S(1)}, u32[]{:S(2)}, u32[]{:S(2)}) collective-permute-start(bf16[1152,128]{1,0:T(8,128)(2,1)S(1)} %bitcast.20), channel_id=1, source_target_pairs={{0,1},{1,0},{2,3},{3,2},{4,5},{5,4},{6,7},{7,6},{8,9},{9,8},{10,11... | collective-permute-start | bytes 884744 | tf_op jit(solution)/shard_map/ppermute | solution.py:539

commit v6 on v4

--- a/solution.py
+++ b/solution.py
@@ -372,10 +372,22 @@
     delta[...] = (up_back[...] * slope(value)).astype(BF16)
 
 
-def decode(table, codes, gated, delta, ext, ext_edge, hidden, cot_patch, w_ups, w_adj,
-           decoded, grads, back, taps, stack, spread):
+def turn(codes, gated, delta, ext, ext_edge, cot_patch, w_adj, grads, back, taps, stack):
     select = onehot(codes[2:3, :], 256)
     back[...] = coarse_inner_conv(delta[...], select, w_adj[...], taps, None)
+    put_taps(taps, 0, ext_edge[0], COARSE_SHIFTS)
+    for x in range(4):
+        put_taps(taps, 256 + 256 * x, ext[:, 256 * x : 256 * x + 256], COARSE_SHIFTS)
+    put_taps(taps, 1280, ext_edge[1], COARSE_SHIFTS)
+    stack[...] = jnp.zeros(stack.shape, BF16)
+    for a in range(3):
+        stack[64 * a : 64 * a + 64, 256 * a : 256 * a + 1024] = delta[...]
+    of_coarse = nt(taps[...], stack[...])
+    of_up = jnp.concatenate([nt(cot_patch[...], gated[...]), jnp.zeros((64, 64), F32)], axis=0)
+    put_grads(grads, of_coarse, of_up)
+
+
+def decode(table, gated, hidden, w_ups, decoded, spread):
     chosen = mm(by_rows(gated[...]), onehot(table[7:8, :1024], 256)).astype(BF16)
     for x in range(4):
         for jl in range(4):
@@ -395,16 +407,6 @@
             ]
             decoded[2 * p, :, 128 * t : 128 * t + 128] = merge(low, even, odd).astype(BF16)
             decoded[2 * p + 1, :, 128 * t : 128 * t + 128] = merge_high(low, even, odd).astype(BF16)
-    put_taps(taps, 0, ext_edge[0], COARSE_SHIFTS)
-    for x in range(4):
-        put_taps(taps, 256 + 256 * x, ext[:, 256 * x : 256 * x + 256], COARSE_SHIFTS)
-    put_taps(taps, 1280, ext_edge[1], COARSE_SHIFTS)
-    stack[...] = jnp.zeros(stack.shape, BF16)
-    for a in range(3):
-        stack[64 * a : 64 * a + 64, 256 * a : 256 * a + 1024] = delta[...]
-    of_coarse = nt(taps[...], stack[...])
-    of_up = jnp.concatenate([nt(cot_patch[...], gated[...]), jnp.zeros((64, 64), F32)], axis=0)
-    put_grads(grads, of_coarse, of_up)
 
 
 def finish(core, table, codes, delta, from_lower, from_upper, back, w_adj, coarse_slope, patch, w_dns, fine_slope,
@@ -609,11 +611,14 @@
         [((576, 512), BF16), ((1728, 512), BF16)],
         [codes, table, hidden1, low1, high1, conv, up_back, w_coarse],
     )
-    decoded, grads_b, back = call(
-        decode, "decode", 6,
-        [(0, (4, 64, 512), BF16), (0, (1152, 128), F32), (0, (64, 1024), F32)],
-        [((576, 1536), BF16), ((192, 1536), BF16), ((256, 1024), BF16)],
-        [table, codes, gated, delta_up, ext1, ext1_edge, hidden0, cot_patch, w_ups, w_adj],
+    grads_b, back = call(
+        turn, "turn", 6,
+        [(0, (1152, 128), F32), (0, (64, 1024), F32)],
+        [((576, 1536), BF16), ((192, 1536), BF16)],
+        [codes, gated, delta_up, ext1, ext1_edge, cot_patch, w_adj],
+    )
+    (decoded,) = call(
+        decode, "decode", 6, [(0, (4, 64, 512), BF16)], [((256, 1024), BF16)], [table, gated, hidden0, w_ups],
     )
     keep, send = call(
         finish, "finish", 12,

time: 93.9 us -> 93.9 us (level)
  waiting for transfers between devices: 3.19 us -> 1.99 us
  Pallas kernels: 17.7 us -> 18.8 us
    ppermute x2, waiting for transfers between devices: 2.42 us -> 1.21 us  [other_core(): return lax.ppermute(x, 'core', [(0, 1), (1, 0)])]
    pallas_call x7 -> x8, Pallas kernels: 16 us -> 17.2 us  [call(): pl.pallas_call(body, name=name, out_shape=[jax.ShapeDtypeStruct(shape, ki...]
  transfers between devices with their start and end apart: 6 -> 6, of which waited for: 3 -> 2; matrix products, arithmetic and copies ran while one was open for 0% -> 0% of each run, Pallas kernels for 5% -> 7%
where the time goes in v6:
time: 93.9 us; the launch traced here: 93.5 us
  blocking collectives  50.8 us (54%)
  Pallas kernels  18.8 us (20%)
  starting transfers between devices  17.2 us (18%)
  local copies, waits for them, and re-layouts  3.58 us (4%)
  waiting for transfers between devices  1.99 us (2%)
    all_to_all x3, blocking collectives, dealt(): return lax.all_to_all(x.reshape(count, -1, 128), axes, 0, 0, tiled=True)  50.8 us
    pallas_call x8, Pallas kernels, call(): pl.pallas_call(body, name=name, out_shape=[jax.ShapeDtypeStruct(shape, ki...  17.2 us
    ppermute x4, starting transfers between devices, passed_along(): return lax.ppermute(block, CHIPS, route)  10.5 us
    ppermute x2, starting transfers between devices, other_core(): return lax.ppermute(x, 'core', [(0, 1), (1, 0)])  6.75 us
    unnamed x18, local copies, waits for them, and re-layouts  3.52 us
  transfers between devices with their start and end apart: 6, of which 2 were waited for; matrix products, arithmetic and copies ran while one was open for 0% of the time, Pallas kernels for 7%

profile of v6, /device:TPU:1, one launch (start us, length us, event | category | flops | bytes accessed | tf_op | source)
XLA Modules:
  0.0 93.5 jit_solution(15121043360482372759)
XLA Ops:
  0.6 0.0 copy-start
  0.7 1.7 %pack_faces.1 = (bf16[144,128]{1,0:T(8,128)(2,1)}, bf16[144,128]{1,0:T(8,128)(2,1)}) custom-call(s32[1]{0:T(128)} %bitcast.2.core.refs_0_, s32[2,16]{1,0:T(2,128)} %bitcast.26, bf16[4,64,512]{2,1,0:T(8,128)(2,1)} %bitcast.17, bf16[4,64,512]{2,1,0:T(8,128)(2,1)} %bitcast.18), custom_call_target="tpu_custom_call" | custom-call | tf_op jit(solution)/shard_map/pack_faces/pallas_call | solution.py:575
  2.3 3.9 %collective-permute-start = (bf16[144,128]{1,0:T(8,128)(2,1)}, bf16[144,128]{1,0:T(8,128)(2,1)S(1)}, u32[]{:S(2)}, u32[]{:S(2)}) collective-permute-start(bf16[144,128]{1,0:T(8,128)(2,1)} %get-tuple-element.42), channel_id=1, source_target_pairs={{0,2},{2,4},{4,6},{6,8},{8,10},{10,12},{12,14},{14,16},{16,18},{18... | collective-permute-start | bytes 110600 | tf_op jit(solution)/shard_map/ppermute | solution.py:538
  6.3 0.0 copy-start.7
  6.3 1.3 %collective-permute-start.1 = (bf16[144,128]{1,0:T(8,128)(2,1)}, bf16[144,128]{1,0:T(8,128)(2,1)S(1)}, u32[]{:S(2)}, u32[]{:S(2)}) collective-permute-start(bf16[144,128]{1,0:T(8,128)(2,1)} %get-tuple-element.43), channel_id=1, source_target_pairs={{2,0},{4,2},{6,4},{8,6},{10,8},{12,10},{14,12},{16,14},{18,16},{20... | collective-permute-start | bytes 110600 | tf_op jit(solution)/shard_map/ppermute | solution.py:538
  7.6 0.0 copy-start.2
  7.6 0.9 copy-done.2
  8.6 0.9 %copy-done.3 = bf16[64,1728]{1,0:T(8,128)(2,1)S(1)} copy-done((bf16[64,1728]{1,0:T(8,128)(2,1)S(1)}, bf16[64,1728]{1,0:T(8,128)(2,1)}, u32[]{:S(2)}) %copy-start.3) | copy-done | bytes 221208
  9.5 0.9 %copy-done.4 = bf16[1,4,64,512]{3,2,1,0:T(8,128)(2,1)S(1)} copy-done((bf16[1,4,64,512]{3,2,1,0:T(8,128)(2,1)S(1)}, bf16[1,4,64,512]{3,2,1,0:T(8,128)(2,1)}, u32[]{:S(2)}) %copy-start.4) | copy-done | bytes 262168
  10.5 3.2 %fine_inner.1 = (f32[8,64,512]{2,1,0:T(8,128)S(1)}, bf16[2,64,256]{2,1,0:T(8,128)(2,1)S(1)}, f32[64,1024]{1,0:T(8,128)S(1)}, bf16[8,64,512]{2,1,0:T(8,128)(2,1)S...) custom-call(s32[4,26]{1,0:T(4,128)S(1)} %bitcast.23, ...), custom_call_target="tpu_custom_call" | custom-call | tf_op jit(solution)/shard_map/fine_inner/pallas_call | solution.py:521
  13.7 0.0 collective-permute-done.refs_2_.refs_3_
  13.7 0.0 collective-permute-done.1.refs_3_.refs_4_
  13.7 2.5 %fine_outer.1 = (bf16[8,64,512]{2,1,0:T(8,128)(2,1)S(1)}, bf16[512,1024]{1,0:T(8,128)(2,1)S(1)}, f32[64,1024]{1,0:T(8,128)S(1)}, bf16[64,1024]{1,0:T(8,128)(2,1)...) custom-call(s32[4,26]{1,0:T(4,128)S(1)} %bitcast.24, ...), custom_call_target="tpu_custom_call" | custom-call | tf_op jit(solution)/shard_map/fine_outer/pallas_call | solution.py:521
  16.2 4.0 %collective-permute-start.2 = (bf16[128,128]{1,0:T(8,128)(2,1)S(1)}, bf16[128,128]{1,0:T(8,128)(2,1)S(1)}, u32[]{:S(2)}, u32[]{:S(2)}) collective-permute-start(bf16[128,128]{1,0:T(8,128)(2,1)S(1)} %get-tuple-element.51), channel_id=1, source_target_pairs={{0,2},{2,4},{4,6},{6,8},{8,10},{10,12},{12,14},{14,16},{16,18},{18... | collective-permute-start | bytes 98312 | tf_op jit(solution)/shard_map/ppermute | solution.py:538
  20.2 1.3 %collective-permute-start.3 = (bf16[128,128]{1,0:T(8,128)(2,1)S(1)}, bf16[128,128]{1,0:T(8,128)(2,1)S(1)}, u32[]{:S(2)}, u32[]{:S(2)}) collective-permute-start(bf16[128,128]{1,0:T(8,128)(2,1)S(1)} %get-tuple-element.52), channel_id=1, source_target_pairs={{2,0},{4,2},{6,4},{8,6},{10,8},{12,10},{14,12},{16,14},{18,16},{20... | collective-permute-start | bytes 98312 | tf_op jit(solution)/shard_map/ppermute | solution.py:538
  21.5 0.0 copy-start.8
  21.5 0.7 copy-done.8
  22.2 1.9 %coarse_inner.1 = (s32[8,256]{1,0:T(8,128)S(1)}, bf16[64,1024]{1,0:T(8,128)(2,1)S(1)}, f32[64,1024]{1,0:T(8,128)S(1)}, f32[8,64,512]{2,1,0:T(8,128)S(1)}, f32[64,1024]{1,0:T(8,128)S(1)}) custom-call(s32[4,26]{1,0:T(4,128)S(1)} %bitcast.25, s32[2,16]{1,0:T(2,128)S(1)} %bitcast.27, s32[16,2048]{1,0:T(8,128)S(1)} %copy-done, ...), custom_call_target="tpu_custom_call" | custom-call | tf_op jit(solution)/shard_map/coarse_inner/pallas_call | solution.py:521
  24.1 0.0 collective-permute-done.2.refs_3_
  24.1 0.8 collective-permute-done.3.refs_4_
  24.9 1.7 %coarse_outer.1 = (bf16[64,1024]{1,0:T(8,128)(2,1)S(1)}, bf16[64,1024]{1,0:T(8,128)(2,1)S(1)}, bf16[2,64,256]{2,1,0:T(8,128)(2,1)S(1)}, bf16[64,256]{1,0:T(8,128)(2,1)S(1)}, bf16[64,256]{1,0:T(8,128)(2,1)S(1)}) custom-call(s32[8,256]{1,0:T(8,128)S(1)} %get-tuple-element.50.refs_0_.refs_2_, s32[16,2048]{1,0:T(8,128)S(1)} %copy-done, ...), custom_call_target="tpu_custom_call" | custom-call | tf_op jit(solution)/shard_map/coarse_outer/pallas_call | solution.py:521
  26.6 1.6 %turn.1 = (f32[1152,128]{1,0:T(8,128)S(1)}, f32[64,1024]{1,0:T(8,128)S(1)}) custom-call(s32[8,256]{1,0:T(8,128)S(1)} %get-tuple-element.50.refs_0_.refs_2_, bf16[64,1024]{1,0:T(8,128)(2,1)S(1)} %get-tuple-element.54.refs_1_, bf16[64,1024]{1,0:T(8,128)(2,1)S(1)} %get-tuple-element.57.refs_2_.refs_3_, bf16[64,1024]{1,0:T(8,128)(2,1)S(1)} %get-tuple-element.60.refs_3_, ...), custom_call_target="tpu_custom_call" | custom-call | tf_op jit(solution)/shard_map/turn/pallas_call | solution.py:521
  28.2 3.3 %finish.1 = (f32[1152,128]{1,0:T(8,128)S(1)}, bf16[1152,128]{1,0:T(8,128)(2,1)S(1)}) custom-call(s32[1]{0:T(128)} %bitcast.2.core.refs_0_, s32[16,2048]{1,0:T(8,128)S(1)} %copy-done, s32[8,256]{1,0:T(8,128)S(1)} %get-tuple-element.50.refs_0_.refs_2_, bf16[64,1024]{1,0:T(8,128)(2,1)S(1)} %get-tuple-element.57.refs_2_.refs_3_, ...), custom_call_target="tpu_custom_call" | custom-call | tf_op jit(solution)/shard_map/finish/pallas_call | solution.py:521
  31.5 2.7 %collective-permute-start.4 = (bf16[1152,128]{1,0:T(8,128)(2,1)S(1)}, bf16[1152,128]{1,0:T(8,128)(2,1)S(1)}, u32[]{:S(2)}, u32[]{:S(2)}) collective-permute-start(bf16[1152,128]{1,0:T(8,128)(2,1)S(1)} %get-tuple-element.74), channel_id=1, source_target_pairs={{0,1},{1,0},{2,3},{3,2},{4,5},{5,4},{6,7},{7,6},{8,9},{9,8},{10,11... | collective-permute-start | bytes 884744 | tf_op jit(solution)/shard_map/ppermute | solution.py:542
  34.2 1.2 %collective-permute-done.4 = bf16[1152,128]{1,0:T(8,128)(2,1)S(1)} collective-permute-done((bf16[1152,128]{1,0:T(8,128)(2,1)S(1)}, bf16[1152,128]{1,0:T(8,128)(2,1)S(1)}, u32[]{:S(2)}, u32[]{:S(2)}) %collective-permute-start.4) | collective-permute-done | bytes 294944 | tf_op jit(solution)/shard_map/ppermute | solution.py:542
  35.4 0.1 add_convert_fusion
  35.5 23.0 %all_to_all.15 = bf16[16,72,128]{2,1,0:T(8,128)(2,1)S(1)} all-to-all(bf16[16,72,128]{2,1,0:T(8,128)(2,1)S(1)} %bitcast.28), channel_id=1, replica_groups=mesh['z'=8,'y'=4,'x'=4,'core'=2] {'y','x'}, dimensions={0} | all-to-all | bytes 589824 | tf_op jit(solution)/shard_map/all_to_all | solution.py:547
  58.6 17.2 %all_to_all.16 = bf16[8,72,128]{2,1,0:T(8,128)(2,1)S(1)} all-to-all(bf16[8,72,128]{2,1,0:T(8,128)(2,1)S(1)} %broadcast_in_dim.10), channel_id=1, replica_groups=mesh['z'=8,'y'=4,'x'=4,'core'=2] {'z'}, dimensions={0} | all-to-all | bytes 294912 | tf_op jit(solution)/shard_map/all_to_all | solution.py:547
  75.9 10.6 %all_to_all.17 = bf16[16,72,128]{2,1,0:T(8,128)(2,1)S(1)} all-to-all(bf16[16,72,128]{2,1,0:T(8,128)(2,1)S(1)} %broadcast_in_dim.11), channel_id=1, replica_groups=mesh['z'=8,'y'=4,'x'=4,'core'=2] {'y','x'}, dimensions={0} | all-to-all | bytes 589824 | tf_op jit(solution)/shard_map/all_to_all | solution.py:547
  86.5 4.0 %collective-permute-start.5 = (bf16[1152,128]{1,0:T(8,128)(2,1)S(1)}, bf16[1152,128]{1,0:T(8,128)(2,1)S(1)}, u32[]{:S(2)}, u32[]{:S(2)}) collective-permute-start(bf16[1152,128]{1,0:T(8,128)(2,1)S(1)} %bitcast.20), channel_id=1, source_target_pairs={{0,1},{1,0},{2,3},{3,2},{4,5},{5,4},{6,7},{7,6},{8,9},{9,8},{10,11... | collective-permute-start | bytes 884744 | tf_op jit(solution)/shard_map/ppermute | solution.py:542
  90.5 1.4 %decode.1 = bf16[4,64,512]{2,1,0:T(8,128)(2,1)} custom-call(s32[16,2048]{1,0:T(8,128)S(1)} %copy-done, bf16[64,1024]{1,0:T(8,128)(2,1)S(1)} %get-tuple-element.54.refs_1_, bf16[8,64,512]{2,1,0:T(8,128)(2,1)S(1)} %get-tuple-element.55.refs_2_, bf16[128,256]{1,0:T(8,128)(2,1)S(1)} %get-tuple-element.56.refs_3_), custom_call_target="tpu_custom_call" | custom-call | tf_op jit(solution)/shard_map/decode/pallas_call | solution.py:521
  92.0 1.5 %unfold.1 = (f32[64,1728]{1,0:T(8,128)}, f32[64,512]{1,0:T(8,128)}, f32[64,1728]{1,0:T(8,128)}, f32[64,512]{1,0:T(8,128)}) custom-call(s32[1]{0:T(128)} %bitcast.2.core.refs_0_, bf16[1152,128]{1,0:T(8,128)(2,1)S(1)} %bitcast.21, bf16[1152,128]{1,0:T(8,128)(2,1)S(1)} %collective-permute-done.5.refs_2_), custom_call_target="tpu_custom_call" | custom-call | tf_op jit(solution)/shard_map/unfold/pallas_call | solution.py:521
  (15 shorter events, 0.2 us)
Async XLA Ops:
  0.6 7.0 %copy-start = (s32[16,2048]{1,0:T(8,128)S(1)}, s32[16,2048]{1,0:T(8,128)}, u32[]{:S(2)}) copy-start(s32[16,2048]{1,0:T(8,128)} %constant.6.clone.refs_1_.refs_2_.refs_0_) | copy-start | bytes 393220
  0.6 7.0 %copy-start.1 = (bf16[1,4,64,512]{3,2,1,0:T(8,128)(2,1)S(1)}, bf16[1,4,64,512]{3,2,1,0:T(8,128)(2,1)}, u32[]{:S(2)}) copy-start(bf16[1,4,64,512]{3,2,1,0:T(8,128)(2,1)} %param.9) | copy-start | bytes 786436
  0.7 7.0 %copy-start.5 = (bf16[64,512]{1,0:T(8,128)(2,1)S(1)}, bf16[64,512]{1,0:T(8,128)(2,1)}, u32[]{:S(2)}) copy-start(bf16[64,512]{1,0:T(8,128)(2,1)} %refs_7_.2) | copy-start | bytes 196612
  0.7 7.0 %copy-start.6 = (bf16[64,512]{1,0:T(8,128)(2,1)S(1)}, bf16[64,512]{1,0:T(8,128)(2,1)}, u32[]{:S(2)}) copy-start(bf16[64,512]{1,0:T(8,128)(2,1)} %refs_5_.1) | copy-start | bytes 196612
  2.3 11.4 %collective-permute-start = (bf16[144,128]{1,0:T(8,128)(2,1)}, bf16[144,128]{1,0:T(8,128)(2,1)S(1)}, u32[]{:S(2)}, u32[]{:S(2)}) collective-permute-start(bf16[144,128]{1,0:T(8,128)(2,1)} %get-tuple-element.42), channel_id=1, source_target_pairs={{0,2},{2,4},{4,6},{6,8},{8,10},{10,12},{12,14},{14,16},{16,18},{18... | collective-permute-start | bytes 110600 | tf_op jit(solution)/shard_map/ppermute | solution.py:538
  6.3 1.4 %copy-start.7 = (s32[1,4,26]{2,1,0:T(4,128)S(1)}, s32[1,4,26]{2,1,0:T(4,128)}, u32[]{:S(2)}) copy-start(s32[1,4,26]{2,1,0:T(4,128)} %param.10) | copy-start | bytes 1252
  6.3 7.4 %collective-permute-start.1 = (bf16[144,128]{1,0:T(8,128)(2,1)}, bf16[144,128]{1,0:T(8,128)(2,1)S(1)}, u32[]{:S(2)}, u32[]{:S(2)}) collective-permute-start(bf16[144,128]{1,0:T(8,128)(2,1)} %get-tuple-element.43), channel_id=1, source_target_pairs={{2,0},{4,2},{6,4},{8,6},{10,8},{12,10},{14,12},{16,14},{18,16},{20... | collective-permute-start | bytes 110600 | tf_op jit(solution)/shard_map/ppermute | solution.py:538
  7.6 0.9 %copy-start.2 = (bf16[64,1728]{1,0:T(8,128)(2,1)S(1)}, bf16[64,1728]{1,0:T(8,128)(2,1)}, u32[]{:S(2)}) copy-start(bf16[64,1728]{1,0:T(8,128)(2,1)} %refs_7_.3) | copy-start | bytes 663556
  8.6 0.9 %copy-start.3 = (bf16[64,1728]{1,0:T(8,128)(2,1)S(1)}, bf16[64,1728]{1,0:T(8,128)(2,1)}, u32[]{:S(2)}) copy-start(bf16[64,1728]{1,0:T(8,128)(2,1)} %refs_6_.1) | copy-start | bytes 663556
  9.5 0.9 %copy-start.4 = (bf16[1,4,64,512]{3,2,1,0:T(8,128)(2,1)S(1)}, bf16[1,4,64,512]{3,2,1,0:T(8,128)(2,1)}, u32[]{:S(2)}) copy-start(bf16[1,4,64,512]{3,2,1,0:T(8,128)(2,1)} %param.16) | copy-start | bytes 786436
  16.2 7.9 %collective-permute-start.2 = (bf16[128,128]{1,0:T(8,128)(2,1)S(1)}, bf16[128,128]{1,0:T(8,128)(2,1)S(1)}, u32[]{:S(2)}, u32[]{:S(2)}) collective-permute-start(bf16[128,128]{1,0:T(8,128)(2,1)S(1)} %get-tuple-element.51), channel_id=1, source_target_pairs={{0,2},{2,4},{4,6},{6,8},{8,10},{10,12},{12,14},{14,16},{16,18},{18... | collective-permute-start | bytes 98312 | tf_op jit(solution)/shard_map/ppermute | solution.py:538
  20.2 4.7 %collective-permute-start.3 = (bf16[128,128]{1,0:T(8,128)(2,1)S(1)}, bf16[128,128]{1,0:T(8,128)(2,1)S(1)}, u32[]{:S(2)}, u32[]{:S(2)}) collective-permute-start(bf16[128,128]{1,0:T(8,128)(2,1)S(1)} %get-tuple-element.52), channel_id=1, source_target_pairs={{2,0},{4,2},{6,4},{8,6},{10,8},{12,10},{14,12},{16,14},{18,16},{20... | collective-permute-start | bytes 98312 | tf_op jit(solution)/shard_map/ppermute | solution.py:538
  21.5 0.7 copy-start.8
  31.5 3.9 %collective-permute-start.4 = (bf16[1152,128]{1,0:T(8,128)(2,1)S(1)}, bf16[1152,128]{1,0:T(8,128)(2,1)S(1)}, u32[]{:S(2)}, u32[]{:S(2)}) collective-permute-start(bf16[1152,128]{1,0:T(8,128)(2,1)S(1)} %get-tuple-element.74), channel_id=1, source_target_pairs={{0,1},{1,0},{2,3},{3,2},{4,5},{5,4},{6,7},{7,6},{8,9},{9,8},{10,11... | collective-permute-start | bytes 884744 | tf_op jit(solution)/shard_map/ppermute | solution.py:542
  86.5 5.4 %collective-permute-start.5 = (bf16[1152,128]{1,0:T(8,128)(2,1)S(1)}, bf16[1152,128]{1,0:T(8,128)(2,1)S(1)}, u32[]{:S(2)}, u32[]{:S(2)}) collective-permute-start(bf16[1152,128]{1,0:T(8,128)(2,1)S(1)} %bitcast.20), channel_id=1, source_target_pairs={{0,1},{1,0},{2,3},{3,2},{4,5},{5,4},{6,7},{7,6},{8,9},{9,8},{10,11... | collective-permute-start | bytes 884744 | tf_op jit(solution)/shard_map/ppermute | solution.py:542
